TPU v7x, 128 devices: a whole 4x4x4 slice. The times are simulated.
128 devices in a mesh: aa: 8 (over x, z_lo), ba: 16 (over y, z_hi, core).
Axes of the slice: x: 4, y: 4, z: 4 (z_hi: 2, z_lo: 2; z = z_hi * 2 + z_lo), core: 2. Of those that a mesh axis runs over, the one named last changes fastest.
Arguments:
- grid: bfloat16 [4, 4, 640, 2596], P(None, None, ('aa', 'ba')), may hold values from -6 to 6
- dep_row: int32 [640, 2596], P(('aa', 'ba')), may hold values from 0 to 1276, as said below
- dep_lon: int32 [4, 640, 2596], P(None, ('aa', 'ba')), may hold values from 0 to 2575, as said below
- lon_frac: float32 [4, 640, 2596], P(None, ('aa', 'ba')), may hold values from 0 to 1
- lat_frac: float32 [640, 2596], P(('aa', 'ba')), may hold values from 0 to 1
- wave_slot: int32 [640], replicated, may hold values from 0 to 639, each once
- legendre: bfloat16 [640, 2, 320, 640], P(('aa', 'ba')), may hold values from -6 to 6
Outputs:
- interpolated: bfloat16 [4, 4, 640, 2596], P(None, None, ('aa', 'ba'))
- spectral: float32 [16, 640, 640], P(None, ('aa', 'ba'))
Inputs may be any that keep to these rules, and one draw needn't show every extreme that they name: For the arrival point in global row g, dep_row is g - 2 or g - 1, clipped to the range; the four stencil rows are dep_row to dep_row + 3. dep_lon[r] is a point index of global row dep_row + r, below that row's number of points. `wave_slot`: each wavenumber 0 to 639 stands in exactly one slot.
All inputs are finite; a program needn't handle non-finite values.
Results may differ from a plain program's by a relative error of at most 0.0062.
Values may be sent and summed in bfloat16 or wider, within the bound.
A program may use at most 64 MiB of HBM per device.

v0:
```python
import math

import jax
import jax.numpy as jnp
from jax import lax
from jax.sharding import PartitionSpec as P


def extended_2(x, sides, width):
    for axis, dim in sides:
        size, length = (lax.axis_size(axis), x.shape[dim])
        up = [(i, (i + 1) % size) for i in range(size - 1)]
        down = [(j, i) for i, j in up]
        last = lax.slice_in_dim(x, length - width, length, axis=dim)
        leading = lax.slice_in_dim(x, 0, width, axis=dim)
        before = lax.ppermute(last, axis, up)
        after = lax.ppermute(leading, axis, down)
        x = jnp.concatenate([before, x, after], axis=dim)
    return x


def lagrange(fraction):
    return (
        -fraction * (fraction - 1.0) * (fraction - 2.0) / 6.0,
        (fraction + 1.0) * (fraction - 1.0) * (fraction - 2.0) / 2.0,
        -(fraction + 1.0) * fraction * (fraction - 2.0) / 2.0,
        (fraction + 1.0) * fraction * (fraction - 1.0) / 6.0,
    )


def locate(global_row, half_rows):
    northern = global_row < half_rows
    row_number = jnp.where(northern, global_row + 1, 2 * half_rows - global_row)
    first_half = row_number <= half_rows // 2
    inner_index = jnp.where(
        first_half, half_rows // 2 - row_number, row_number - half_rows // 2 - 1
    )
    pair_row = jnp.where(northern, inner_index, half_rows - 1 - inner_index)
    row_start = jnp.where(first_half, 0, 16 + 4 * (half_rows // 2 - inner_index))
    return (pair_row, row_start, 16 + 4 * row_number)


def stencil(dep_row, dep_lon, lon_frac, lat_frac, first_pair, half_rows, pair_length):
    lat_weights = lagrange(lat_frac)
    indices = []
    factors = []
    for stencil_row in range(4):
        pair_row, row_start, row_length = locate(dep_row + stencil_row, half_rows)
        base_index = (pair_row - first_pair + 2) * pair_length + row_start
        lon_weights = lagrange(lon_frac[stencil_row])
        for offset in range(4):
            point = base_index + jnp.remainder(dep_lon[stencil_row] + (offset - 1), row_length)
            indices.append(point.reshape(-1))
            factors.append((lat_weights[stencil_row] * lon_weights[offset]).reshape(-1))
    return (indices, factors)


def interpolate(extended, indices, factors, pairs_local, pair_length):
    field_count = extended.shape[0]
    level_count = extended.shape[1]
    flattened = extended.reshape(field_count * level_count, -1)
    running = jnp.zeros((field_count * level_count, pairs_local * pair_length), jnp.float32)
    for term_index in range(16):
        running = (
            running
            + jnp.take(flattened, indices[term_index], axis=1).astype(jnp.float32)
            * factors[term_index]
        )
    return running.astype(jnp.bfloat16).reshape(field_count, level_count, pairs_local, pair_length)


def fourier_pair(pair_index, values, waves, half_rows, pair_length):
    inner_index = jnp.where(pair_index < half_rows // 2, pair_index, half_rows - 1 - pair_index)
    first_len = 16 + 4 * (half_rows // 2 - inner_index)
    second_len = 16 + 4 * (half_rows // 2 + 1 + inner_index)
    column = jnp.arange(pair_length, dtype=jnp.int32)
    first_half = column < first_len
    row_length = jnp.where(first_half, first_len, second_len)
    position = jnp.where(first_half, column, column - first_len)
    residue = jnp.remainder(position[:, None] * waves[None, :], row_length[:, None])
    angle = 2.0 * math.pi * residue.astype(jnp.float32) / row_length[:, None].astype(jnp.float32)
    keeping = (2 * waves[None, :] < row_length[:, None]).astype(jnp.float32)
    table = jnp.concatenate([jnp.cos(angle) * keeping, -jnp.sin(angle) * keeping], axis=1).astype(
        jnp.bfloat16
    )
    zeros = jnp.zeros_like(values)
    stacked = jnp.concatenate(
        [
            jnp.where(first_half[None, :], values, zeros),
            jnp.where(first_half[None, :], zeros, values),
        ],
        axis=0,
    )
    product = jnp.dot(stacked, table, preferred_element_type=jnp.float32)
    scaling = 1.0 / jnp.stack([first_len, second_len]).astype(jnp.float32)
    product = product.reshape(2, values.shape[0], 2, waves.shape[0]) * scaling[:, None, None, None]
    return jnp.transpose(product, (2, 1, 0, 3)).astype(jnp.bfloat16)


def spectral_part(received, legendre_part, waves_part, half_rows):
    comp_count = received.shape[0]
    slot_count = received.shape[2]
    grouped = received.reshape(comp_count, half_rows, 2, slot_count)
    northern = grouped[:, : half_rows // 2].astype(jnp.float32)
    southern = grouped[:, half_rows // 2 :][:, ::-1].astype(jnp.float32)
    sym = (northern + southern).astype(jnp.bfloat16).reshape(comp_count, half_rows, slot_count)
    anti = (northern - southern).astype(jnp.bfloat16).reshape(comp_count, half_rows, slot_count)
    even = jnp.einsum("chs,sjh->scj", sym, legendre_part[:, 0], preferred_element_type=jnp.float32)
    odd = jnp.einsum("chs,sjh->scj", anti, legendre_part[:, 1], preferred_element_type=jnp.float32)
    merged = jnp.stack([even, odd], axis=3).reshape(slot_count, comp_count, half_rows)
    keeping = jnp.arange(half_rows, dtype=jnp.int32)[None, :] < (half_rows - waves_part)[:, None]
    merged = jnp.where(keeping[:, None, :], merged, 0.0)
    return jnp.transpose(merged, (1, 0, 2))


def transform(spec_fields, wave_slot, legendre, first_pair, device):
    half_rows = wave_slot.shape[0]
    pair_length = spec_fields.shape[3]
    pairs_local = spec_fields.shape[2]
    slot_count = legendre.shape[0]
    values = spec_fields.reshape(-1, pairs_local, pair_length)
    by_pair = jnp.moveaxis(values, 1, 0)

    def transform_one(operands):
        return fourier_pair(operands[0], operands[1], wave_slot, half_rows, pair_length)

    pair_numbers = first_pair + jnp.arange(pairs_local, dtype=jnp.int32)
    fourier = lax.map(transform_one, (pair_numbers, by_pair))
    comp_count = 2 * values.shape[0]
    rows_local = jnp.transpose(fourier, (1, 2, 0, 3, 4)).reshape(
        comp_count, 2 * pairs_local, half_rows
    )
    waves_part = lax.dynamic_slice_in_dim(wave_slot, device * slot_count, slot_count)
    return spectral_part(
        lax.all_to_all(rows_local, ("aa", "ba"), split_axis=2, concat_axis=1, tiled=True),
        legendre,
        waves_part,
        half_rows,
    )


def on_device(grid, dep_row, dep_lon, lon_frac, lat_frac, wave_slot, legendre):
    half_rows = wave_slot.shape[0]
    pair_length = grid.shape[3]
    pairs_local = grid.shape[2]
    device = lax.axis_index(("aa", "ba"))
    first_pair = device * pairs_local
    indices, factors = stencil(
        dep_row, dep_lon, lon_frac, lat_frac, first_pair, half_rows, pair_length
    )
    extended = extended_2(grid, ((("aa", "ba"), 2),), 2)
    interpolated = interpolate(extended, indices, factors, pairs_local, pair_length)
    spectral = transform(interpolated[:2], wave_slot, legendre, first_pair, device)
    return (interpolated, spectral)


def solution(mesh):
    return jax.shard_map(
        on_device,
        mesh=mesh,
        in_specs=(
            P(None, None, ("aa", "ba"), None),
            P(("aa", "ba"), None),
            P(None, ("aa", "ba"), None),
            P(None, ("aa", "ba"), None),
            P(("aa", "ba"), None),
            P(),
            P(("aa", "ba"), None, None, None),
        ),
        out_specs=(P(None, None, ("aa", "ba"), None), P(None, ("aa", "ba"), None)),
        check_vma=False,
    )
```

profile of v0, /device:TPU:1, one launch (start us, length us, event | category | flops | bytes accessed | tf_op | source)
XLA Modules:
  0.0 1088.9 jit_solution(12398308953855471643)
XLA Ops:
  1.8 6.9 collective-permute-start
  12.1 14.7 %fusion.86 = (s32[5,2596]{1,0:T(8,128)S(1)}, s32[5,2596]{1,0:T(8,128)S(1)}, s32[5,2596]{1,0:T(8,128)S(1)}, s32[5,2596]{1,0:T(8,128)S(1)}, s32[5,2596]{1,0:T(8,12...) fusion(s32[1,5,2596]{2,0,1:T(1,128)S(1)} %get-tuple-element.89,, ...), kind=kLoop, calls=%fused_computation.173 | loop fusion | flops 3011360 | bytes 1090324 | tf_op jit(solution)/shard_map/add | solution.py:52
  54.7 4.7 copy.137
  59.4 28.3 %gather_fusion = bf16[12980,16]{1,0:T(8,128)(2,1)S(1)} fusion(bf16[16,23364]{0,1:T(8,128)(2,1)} %copy.137, s32[13312]{0:T(1024)} %pad_clamp_fusion.15), kind=kCustom, calls=%fused_computation.clone | custom fusion | bytes 882640 | tf_op jit(solution)/shard_map/jit(_take)/gather | solution.py:66
  87.6 2.9 copy.138
  90.5 28.2 %gather_fusion.1 = bf16[12980,16]{1,0:T(8,128)(2,1)S(1)} fusion(bf16[16,23364]{0,1:T(8,128)(2,1)} %copy.137, s32[13312]{0:T(1024)} %pad_clamp_fusion.14), kind=kCustom, calls=%fused_computation.1.clone | custom fusion | bytes 882640 | tf_op jit(solution)/shard_map/jit(_take)/gather | solution.py:66
  121.6 28.2 %gather_fusion.2 = bf16[12980,16]{1,0:T(8,128)(2,1)S(1)} fusion(bf16[16,23364]{0,1:T(8,128)(2,1)} %copy.137, s32[13312]{0:T(1024)} %pad_clamp_fusion.13), kind=kCustom, calls=%fused_computation.2.clone | custom fusion | bytes 882640 | tf_op jit(solution)/shard_map/jit(_take)/gather | solution.py:66
  152.7 28.2 %gather_fusion.3 = bf16[12980,16]{1,0:T(8,128)(2,1)S(1)} fusion(bf16[16,23364]{0,1:T(8,128)(2,1)} %copy.137, s32[13312]{0:T(1024)} %pad_clamp_fusion.12), kind=kCustom, calls=%fused_computation.3.clone | custom fusion | bytes 882640 | tf_op jit(solution)/shard_map/jit(_take)/gather | solution.py:66
  183.8 28.2 %gather_fusion.4 = bf16[12980,16]{1,0:T(8,128)(2,1)S(1)} fusion(bf16[16,23364]{0,1:T(8,128)(2,1)} %copy.137, s32[13312]{0:T(1024)} %pad_clamp_fusion.11), kind=kCustom, calls=%fused_computation.4.clone | custom fusion | bytes 882640 | tf_op jit(solution)/shard_map/jit(_take)/gather | solution.py:66
  214.9 28.2 %gather_fusion.5 = bf16[12980,16]{1,0:T(8,128)(2,1)S(1)} fusion(bf16[16,23364]{0,1:T(8,128)(2,1)} %copy.137, s32[13312]{0:T(1024)} %pad_clamp_fusion.10), kind=kCustom, calls=%fused_computation.5.clone | custom fusion | bytes 882640 | tf_op jit(solution)/shard_map/jit(_take)/gather | solution.py:66
  246.0 28.2 %gather_fusion.6 = bf16[12980,16]{1,0:T(8,128)(2,1)S(1)} fusion(bf16[16,23364]{0,1:T(8,128)(2,1)} %copy.137, s32[13312]{0:T(1024)} %pad_clamp_fusion.9), kind=kCustom, calls=%fused_computation.6.clone | custom fusion | bytes 882640 | tf_op jit(solution)/shard_map/jit(_take)/gather | solution.py:66
  277.0 28.2 %gather_fusion.7 = bf16[12980,16]{1,0:T(8,128)(2,1)S(1)} fusion(bf16[16,23364]{0,1:T(8,128)(2,1)} %copy.137, s32[13312]{0:T(1024)} %pad_clamp_fusion.8), kind=kCustom, calls=%fused_computation.7.clone | custom fusion | bytes 882640 | tf_op jit(solution)/shard_map/jit(_take)/gather | solution.py:66
  305.3 3.0 copy.155
  308.3 28.2 %gather_fusion.8 = bf16[12980,16]{1,0:T(8,128)(2,1)S(1)} fusion(bf16[16,23364]{0,1:T(8,128)(2,1)} %copy.137, s32[13312]{0:T(1024)} %pad_clamp_fusion.7), kind=kCustom, calls=%fused_computation.8.clone | custom fusion | bytes 882640 | tf_op jit(solution)/shard_map/jit(_take)/gather | solution.py:66
  339.4 28.2 %gather_fusion.9 = bf16[12980,16]{1,0:T(8,128)(2,1)S(1)} fusion(bf16[16,23364]{0,1:T(8,128)(2,1)} %copy.137, s32[13312]{0:T(1024)} %pad_clamp_fusion.6), kind=kCustom, calls=%fused_computation.9.clone | custom fusion | bytes 882640 | tf_op jit(solution)/shard_map/jit(_take)/gather | solution.py:66
  370.5 28.2 %gather_fusion.10 = bf16[12980,16]{1,0:T(8,128)(2,1)S(1)} fusion(bf16[16,23364]{0,1:T(8,128)(2,1)} %copy.137, s32[13312]{0:T(1024)} %pad_clamp_fusion.5), kind=kCustom, calls=%fused_computation.10.clone | custom fusion | bytes 882640 | tf_op jit(solution)/shard_map/jit(_take)/gather | solution.py:66
  401.6 28.2 %gather_fusion.11 = bf16[12980,16]{1,0:T(8,128)(2,1)S(1)} fusion(bf16[16,23364]{0,1:T(8,128)(2,1)} %copy.137, s32[13312]{0:T(1024)} %pad_clamp_fusion.4), kind=kCustom, calls=%fused_computation.11.clone | custom fusion | bytes 882640 | tf_op jit(solution)/shard_map/jit(_take)/gather | solution.py:66
  432.7 28.3 %gather_fusion.12 = bf16[12980,16]{1,0:T(8,128)(2,1)S(1)} fusion(bf16[16,23364]{0,1:T(8,128)(2,1)} %copy.137, s32[13312]{0:T(1024)} %pad_clamp_fusion.3), kind=kCustom, calls=%fused_computation.12.clone | custom fusion | bytes 882640 | tf_op jit(solution)/shard_map/jit(_take)/gather | solution.py:66
  463.8 28.2 %gather_fusion.13 = bf16[12980,16]{1,0:T(8,128)(2,1)S(1)} fusion(bf16[16,23364]{0,1:T(8,128)(2,1)} %copy.137, s32[13312]{0:T(1024)} %pad_clamp_fusion.2), kind=kCustom, calls=%fused_computation.13.clone | custom fusion | bytes 882640 | tf_op jit(solution)/shard_map/jit(_take)/gather | solution.py:66
  494.9 28.2 %gather_fusion.14 = bf16[12980,16]{1,0:T(8,128)(2,1)S(1)} fusion(bf16[16,23364]{0,1:T(8,128)(2,1)} %copy.137, s32[13312]{0:T(1024)} %pad_clamp_fusion.1), kind=kCustom, calls=%fused_computation.14.clone | custom fusion | bytes 882640 | tf_op jit(solution)/shard_map/jit(_take)/gather | solution.py:66
  523.1 2.9 copy.173
  526.0 28.2 %gather_fusion.15 = bf16[12980,16]{1,0:T(8,128)(2,1)S(1)} fusion(bf16[16,23364]{0,1:T(8,128)(2,1)} %copy.137, s32[13312]{0:T(1024)} %pad_clamp_fusion), kind=kCustom, calls=%fused_computation.15.clone | custom fusion | bytes 882640 | tf_op jit(solution)/shard_map/jit(_take)/gather | solution.py:66
  557.1 5.7 add_convert_fusion.1
  563.1 484.7 %while.10 = (s32[]{:T(128)}, bf16[5,2,8,2,640]{4,2,1,3,0:T(8,128)(2,1)S(1)}, s32[5]{0:T(128)S(1)}, bf16[5,8,2596]{2,1,0:T(8,128)(2,1)S(1)}, s32[640]{0:T(1024)S(...) while((s32[]{:T(128)}, ...), condition=%wide.region_1.3_spmd, body=%wide.region_0.2_spmd.sunk | while | flops 148153792 | bytes 13808483 | solution.py:128
  565.8 93.2 %fusion.215 = (bf16[2596,640]{1,0:T(8,128)(2,1)S(1)}, bf16[2596,640]{1,0:T(8,128)(2,1)S(1)}) fusion(s32[640]{0:T(1024)S(1)} %broadcast_multiply_fusion.2, s32[2596]{0:T(1024)S(1)} %get-tuple-element.206, f32[2596]{0:T(1024)S(1)} %get-tuple-element.207, pred[2596]{0:T(1024)(128)(4,1)S(1)} %get-tuple-element.208, s32[2596]{0:T(1024)S(1)} %get-tuple-element.209, ...), kind=kLoop, calls=%fused_computation.19.clone.1 | loop fusion | flops 28244480 | bytes 6695012 | tf_op jit(solution)/shard_map/convert
  662.7 93.2 %fusion.215 = (bf16[2596,640]{1,0:T(8,128)(2,1)S(1)}, bf16[2596,640]{1,0:T(8,128)(2,1)S(1)}) fusion(s32[640]{0:T(1024)S(1)} %broadcast_multiply_fusion.2, s32[2596]{0:T(1024)S(1)} %get-tuple-element.206, f32[2596]{0:T(1024)S(1)} %get-tuple-element.207, pred[2596]{0:T(1024)(128)(4,1)S(1)} %get-tuple-element.208, s32[2596]{0:T(1024)S(1)} %get-tuple-element.209, ...), kind=kLoop, calls=%fused_computation.19.clone.1 | loop fusion | flops 28244480 | bytes 6695012 | tf_op jit(solution)/shard_map/convert
  759.6 93.2 %fusion.215 = (bf16[2596,640]{1,0:T(8,128)(2,1)S(1)}, bf16[2596,640]{1,0:T(8,128)(2,1)S(1)}) fusion(s32[640]{0:T(1024)S(1)} %broadcast_multiply_fusion.2, s32[2596]{0:T(1024)S(1)} %get-tuple-element.206, f32[2596]{0:T(1024)S(1)} %get-tuple-element.207, pred[2596]{0:T(1024)(128)(4,1)S(1)} %get-tuple-element.208, s32[2596]{0:T(1024)S(1)} %get-tuple-element.209, ...), kind=kLoop, calls=%fused_computation.19.clone.1 | loop fusion | flops 28244480 | bytes 6695012 | tf_op jit(solution)/shard_map/convert
  856.6 93.2 %fusion.215 = (bf16[2596,640]{1,0:T(8,128)(2,1)S(1)}, bf16[2596,640]{1,0:T(8,128)(2,1)S(1)}) fusion(s32[640]{0:T(1024)S(1)} %broadcast_multiply_fusion.2, s32[2596]{0:T(1024)S(1)} %get-tuple-element.206, f32[2596]{0:T(1024)S(1)} %get-tuple-element.207, pred[2596]{0:T(1024)(128)(4,1)S(1)} %get-tuple-element.208, s32[2596]{0:T(1024)S(1)} %get-tuple-element.209, ...), kind=kLoop, calls=%fused_computation.19.clone.1 | loop fusion | flops 28244480 | bytes 6695012 | tf_op jit(solution)/shard_map/convert
  953.5 93.2 %fusion.215 = (bf16[2596,640]{1,0:T(8,128)(2,1)S(1)}, bf16[2596,640]{1,0:T(8,128)(2,1)S(1)}) fusion(s32[640]{0:T(1024)S(1)} %broadcast_multiply_fusion.2, s32[2596]{0:T(1024)S(1)} %get-tuple-element.206, f32[2596]{0:T(1024)S(1)} %get-tuple-element.207, pred[2596]{0:T(1024)(128)(4,1)S(1)} %get-tuple-element.208, s32[2596]{0:T(1024)S(1)} %get-tuple-element.209, ...), kind=kLoop, calls=%fused_computation.19.clone.1 | loop fusion | flops 28244480 | bytes 6695012 | tf_op jit(solution)/shard_map/convert
  1052.6 10.0 all-to-all-start
  1064.2 9.7 all-to-all-done
  1077.2 4.2 reshape.193
  (173 shorter events, 95.1 us)
Async XLA Ops:
  1.8 51.4 %collective-permute-start = (bf16[4,4,2,2596]{3,1,2,0:T(4,128)(2,1)S(1)}, bf16[4,4,2,2596]{3,1,2,0:T(4,128)(2,1)S(1)}, u32[]{:S(2)}, u32[]{:S(2)}) collective-permute-start(bf16[4,4,2,2596]{3,1,2,0:T(4,128)(2,1)S(1)} %get-tuple-element.83), channel_id=1, source_target_pairs={{0,1},{1,2},{2,3},{3,4},{4,5},{5,6},{6,7},{7,8},{8,9},{9,10},{10,1... | collective-permute-start | bytes 498440 | tf_op jit(solution)/shard_map/ppermute | solution.py:16
  8.7 44.5 %collective-permute-start.1 = (bf16[4,4,2,2596]{3,1,2,0:T(4,128)(2,1)S(1)}, bf16[4,4,2,2596]{3,1,2,0:T(4,128)(2,1)S(1)}, u32[]{:S(2)}, u32[]{:S(2)}) collective-permute-start(bf16[4,4,2,2596]{3,1,2,0:T(4,128)(2,1)S(1)} %get-tuple-element.84), channel_id=1, source_target_pairs={{1,0},{2,1},{3,2},{4,3},{5,4},{6,5},{7,6},{8,7},{9,8},{10,9},{11,1... | collective-permute-start | bytes 498440 | tf_op jit(solution)/shard_map/ppermute | solution.py:17
  26.9 16.8 %copy-start.3 = (f32[4,5,2596]{2,0,1:T(4,128)S(1)}, f32[4,5,2596]{2,0,1:T(4,128)}, u32[]{:S(2)}) copy-start(f32[4,5,2596]{2,0,1:T(4,128)} %param.14) | copy-start | bytes 623044
  27.7 16.2 %copy-start.5 = (f32[5,2596]{1,0:T(8,128)S(1)}, f32[5,2596]{1,0:T(8,128)}, u32[]{:S(2)}) copy-start(f32[5,2596]{1,0:T(8,128)} %param.15) | copy-start | bytes 155764
  32.8 20.3 %copy-start.2 = (s32[640]{0:T(1024)S(1)}, s32[640]{0:T(1024)}, u32[]{:S(2)}) copy-start(s32[640]{0:T(1024)} %param.16) | copy-start | bytes 7684
  32.9 20.3 %copy-start.1 = (bf16[4,4,5,2596]{3,1,2,0:T(4,128)(2,1)S(1)}, bf16[4,4,5,2596]{3,1,2,0:T(4,128)(2,1)}, u32[]{:S(2)}) copy-start(bf16[4,4,5,2596]{3,1,2,0:T(4,128)(2,1)} %param.11) | copy-start | bytes 1246084
  557.1 6.0 copy-start.4
  1052.6 21.3 %all-to-all-start = ((bf16[128,2,400]{2,1,0:T(2,128)(2,1)}), bf16[128,2,400]{2,1,0:T(2,128)(2,1)S(1)}, u32[]{:S(2)}, u32[]{:S(2)}) async-start(bf16[128,2,400]{2,1,0:T(2,128)(2,1)} %reshape.373), calls=%async_computation | async-start | bytes 524288 | tf_op jit(solution)/shard_map/all_to_all | solution.py:135
  1081.4 2.2 copy-start
where the time goes:
time: 1110 us; the launch traced here: 1090 us
  local copies, waits for them, and re-layouts  537 us (48%)
  other arithmetic  506 us (46%)
  starting transfers between devices  18.8 us (2%)
    gather x32, local copies, waits for them, and re-layouts, interpolate(): jnp.take(flattened, indices[term_index], axis=1).astype(jnp.float32)  498 us
    another operation x5, other arithmetic  466 us
  transfers between devices with their start and end apart: 3, of which 1 were waited for; matrix products, arithmetic and copies ran while one was open for 4% of the time, Pallas kernels for 0%

commit v1 on v0

v1 whole, which is shorter than its diff:
```python
import functools

import jax
import jax.numpy as jnp
from jax import lax
from jax.experimental import pallas as pl
from jax.experimental.pallas import tpu as pltpu
from jax.sharding import PartitionSpec as P

LANES = 128
WIN = 256
ETILES = 24
EW = ETILES * LANES
MARGIN = 60


def row_place(global_row, half_rows):
    northern = global_row < half_rows
    number = jnp.where(northern, global_row + 1, 2 * half_rows - global_row)
    second = number > half_rows // 2
    inner = jnp.where(second, number - half_rows // 2 - 1, half_rows // 2 - number)
    pair_row = jnp.where(northern, inner, half_rows - 1 - inner)
    return pair_row, second, 16 + 4 * number


def cubic(t):
    return (
        -t * (t - 1.0) * (t - 2.0) * (1.0 / 6.0),
        (t + 1.0) * (t - 1.0) * (t - 2.0) * 0.5,
        -(t + 1.0) * t * (t - 2.0) * 0.5,
        (t + 1.0) * t * (t - 1.0) * (1.0 / 6.0),
    )


def interp_kernel(half_rows, pair_length, first_ref, before_ref, own_ref, after_ref,
                  row_ref, lon_ref, lonf_ref, latf_ref, out_ref,
                  rows_s, ext_s, lon_s, wgt_s, row_p, lon_p, lonf_p, latf_p):
    pairs = own_ref.shape[0]
    fields = own_ref.shape[1]
    near = pairs + 4
    tiles = pl.cdiv(pair_length, LANES)
    first = first_ref[0]

    rows_s[...] = jnp.zeros_like(rows_s)
    for j in range(near):
        src = before_ref[j] if j < 2 else (own_ref[j - 2] if j < 2 + pairs else after_ref[j - 2 - pairs])
        rows_s[j, :, pl.ds(LANES, pair_length)] = src

    row_p[...] = jnp.zeros_like(row_p)
    lon_p[...] = jnp.zeros_like(lon_p)
    lonf_p[...] = jnp.zeros_like(lonf_p)
    latf_p[...] = jnp.zeros_like(latf_p)
    row_p[pl.ds(0, pairs), pl.ds(0, pair_length)] = row_ref[...]
    latf_p[pl.ds(0, pairs), pl.ds(0, pair_length)] = latf_ref[...]
    for r in range(4):
        lon_p[r, pl.ds(0, pairs), pl.ds(0, pair_length)] = lon_ref[r]
        lonf_p[r, pl.ds(0, pairs), pl.ds(0, pair_length)] = lonf_ref[r]

    lane = lax.broadcasted_iota(jnp.int32, (fields, LANES), 1)

    def half_lengths(pair):
        inner = jnp.where(pair < half_rows // 2, pair, half_rows - 1 - pair)
        return 16 + 4 * (half_rows // 2 - inner), 16 + 4 * (half_rows // 2 + 1 + inner)

    def unaligned(j, lanes_at):
        tile = pl.multiple_of((lanes_at >> 7) * LANES, LANES)
        two = rows_s[j, :, pl.ds(tile, 2 * LANES)].astype(jnp.float32)
        shift = (2 * LANES - (lanes_at & 127)) & 255
        return pltpu.roll(two, shift, 1)[:, :LANES]

    for half in range(2):
        @pl.loop(0, ETILES)
        def _(tile):
            k0 = (tile - 1) * LANES
            for j in range(near):
                len0, len1 = half_lengths(first + j - 2)
                start = len0 if half else 0
                length = len1 if half else len0
                here = start + k0 + jnp.where(tile == 0, length, 0) + LANES
                over = jnp.maximum(start + k0 - length + LANES, 0)
                here = jnp.clip(here, 0, EW - 2 * LANES)
                over = jnp.clip(over, 0, EW - 2 * LANES)
                a = unaligned(j, here)
                b = unaligned(j, over)
                e = jnp.where(lane + k0 >= length, b, a)
                ext_s[2 * j + half, :, pl.ds(pl.multiple_of(tile * LANES, LANES), LANES)] = e.astype(jnp.bfloat16)

    sub8 = lax.broadcasted_iota(jnp.int32, (8, LANES), 0)
    lane8 = lax.broadcasted_iota(jnp.int32, (8, LANES), 1)

    def weigh(tile, fits):
        at = pl.ds(pl.multiple_of(tile * LANES, LANES), LANES)
        col = tile * LANES + lane8
        pair = first + sub8
        northern = pair < half_rows // 2
        len0, len1 = half_lengths(pair)
        second = col >= len0
        inner = jnp.where(northern, pair, half_rows - 1 - pair)
        number = jnp.where(second, half_rows // 2 + 1 + inner, half_rows // 2 - inner)
        g = jnp.where(northern, number - 1, 2 * half_rows - number)
        base = jnp.clip(g - 2, 0, 2 * half_rows - 4)
        later = (row_p[:, at] - base) > 0
        k0 = jnp.where(second, jnp.maximum(tile * LANES - len0, 0), tile * LANES)
        base_k = k0 - MARGIN
        inside = (col < pair_length) & (sub8 < pairs)
        latw = cubic(latf_p[:, at])
        lons = [lon_p[r, :, at] for r in range(4)]
        lonfs = [lonf_p[r, :, at] for r in range(4)]
        zero = jnp.zeros((8, LANES), jnp.float32)
        for d in range(5):
            hi, lo = min(d, 3), max(d - 1, 0)
            lon = jnp.where(later, lons[lo], lons[hi])
            frac = jnp.where(later, lonfs[lo], lonfs[hi])
            lat = jnp.where(later, latw[lo] if d >= 1 else zero, latw[hi] if d <= 3 else zero)
            _, _, length = row_place(jnp.minimum(base + d, 2 * half_rows - 1), half_rows)
            rel = lon - 1 - base_k
            rel = jnp.where(rel < 0, rel + length, jnp.where(rel >= length, rel - length, rel))
            rel = jnp.where(length <= WIN - 4, lon, rel)
            bad = inside & (lat != 0.0) & ((rel < 0) | (rel > WIN - 4))
            fits = jnp.maximum(fits, bad.astype(jnp.int32))
            lon_s[d, :, at] = lon
            ws = cubic(frac)
            for o in range(4):
                wgt_s[d * 4 + o, :, at] = lat * ws[o]
        return fits

    worst = lax.fori_loop(0, tiles, weigh, jnp.zeros((8, LANES), jnp.int32))
    local = jnp.max(worst) == 0

    sub16 = lax.broadcasted_iota(jnp.int32, (16, LANES), 0)
    zero16 = jnp.zeros((16, LANES), jnp.bfloat16)

    def spread(d, q, at, place, fold):
        w = [jnp.broadcast_to(wgt_s[d * 4 + o, pl.ds(q, 1), at], (16, LANES)) for o in range(4)]
        off = (sub16 - place) & 15
        v = jnp.where(off == 0, w[0], jnp.where(off == 1, w[1], jnp.where(off == 2, w[2], jnp.where(off == 3, w[3], 0.0))))
        block = (place + 15 - sub16) >> 4
        if fold:
            block = jnp.where(block >= 16, block - 16, block)
        v = v.astype(jnp.bfloat16)
        block = block.astype(jnp.float32).astype(jnp.bfloat16)
        return [jnp.where(block == jnp.bfloat16(a), v, zero16) for a in range(WIN // 16)]

    def unit_scalars(q, u):
        pair = first + q
        northern = pair < half_rows // 2
        len0, _ = half_lengths(pair)
        straddle = len0 >> 7
        half = (u > straddle).astype(jnp.int32)
        tile = u - half
        inner = jnp.where(northern, pair, half_rows - 1 - pair)
        number = jnp.where(half == 1, half_rows // 2 + 1 + inner, half_rows // 2 - inner)
        g = jnp.where(northern, number - 1, 2 * half_rows - number)
        base = jnp.clip(g - 2, 0, 2 * half_rows - 4)
        k0 = jnp.where(half == 1, jnp.maximum(tile * LANES - len0, 0), tile * LANES)
        return len0, straddle, half, tile, base, k0

    def place_of(base, d):
        pair_row, second, length = row_place(jnp.minimum(base + d, 2 * half_rows - 1), half_rows)
        return 2 * jnp.clip(pair_row - first + 2, 0, near - 1) + second.astype(jnp.int32), length

    lane1 = lax.broadcasted_iota(jnp.int32, (1, LANES), 1)

    def finish(q, u, straddle, tile, total, carry):
        total = total + jnp.where(u == straddle + 1, carry, 0.0)
        out_ref[q, :, pl.ds(pl.multiple_of(tile * LANES, LANES), LANES)] = total.astype(jnp.bfloat16)
        return total

    @pl.when(local)
    def _():
        def unit(q, u, carry):
            len0, straddle, half, tile, base, k0 = unit_scalars(q, u)
            at = pl.ds(pl.multiple_of(tile * LANES, LANES), LANES)
            col = tile * LANES + lane1
            mine = ((col >= len0).astype(jnp.int32) == half) & (col < pair_length)
            rows, weights = [], []
            for d in range(5):
                where_row, length = place_of(base, d)
                short = length <= WIN - 4
                base_k = jnp.where(short, -1, k0 - MARGIN)
                begin = base_k + LANES
                s = begin & 127
                first_tile = pl.multiple_of((begin >> 7) * LANES, LANES)
                rel = lon_s[d, pl.ds(q, 1), at] - 1 - base_k
                rel = jnp.where(rel < 0, rel + length, jnp.where(rel >= length, rel - length, rel))
                place = jnp.where(mine, s + rel, -4096)
                weights += spread(d, q, at, jnp.broadcast_to(place, (16, LANES)), True)
                three = ext_s[where_row, :, pl.ds(first_tile, 3 * LANES)]
                rows += [jnp.where(lane >= s, three[:, :LANES], three[:, 2 * LANES:]), three[:, LANES:2 * LANES]]
            total = jnp.dot(jnp.concatenate(rows, axis=1), jnp.concatenate(weights, axis=0),
                            preferred_element_type=jnp.float32)
            return finish(q, u, straddle, tile, total, carry)

        lax.fori_loop(0, tiles + 1, lambda u, carry: tuple(unit(q, u, carry[q]) for q in range(pairs)),
                      (jnp.zeros((fields, LANES), jnp.float32),) * pairs)

    @pl.when(jnp.logical_not(local))
    def _():
        def unit(q, u, carry):
            len0, straddle, half, tile, base, _ = unit_scalars(q, u)
            at = pl.ds(pl.multiple_of(tile * LANES, LANES), LANES)
            col = tile * LANES + lane1
            mine = ((col >= len0).astype(jnp.int32) == half) & (col < pair_length)

            def window(w, total):
                rows, weights = [], []
                for d in range(5):
                    where_row, length = place_of(base, d)
                    place = lon_s[d, pl.ds(q, 1), at] - 1 + LANES - w * WIN
                    place = jnp.where(mine, place, -4096)
                    weights += spread(d, q, at, jnp.broadcast_to(place, (16, LANES)), False)
                    rows.append(ext_s[where_row, :, pl.ds(pl.multiple_of(w * WIN, WIN), WIN)])
                return total + jnp.dot(jnp.concatenate(rows, axis=1), jnp.concatenate(weights, axis=0),
                                       preferred_element_type=jnp.float32)

            total = lax.fori_loop(0, EW // WIN, window, jnp.zeros((fields, LANES), jnp.float32))
            return finish(q, u, straddle, tile, total, carry)

        lax.fori_loop(0, tiles + 1, lambda u, carry: tuple(unit(q, u, carry[q]) for q in range(pairs)),
                      (jnp.zeros((fields, LANES), jnp.float32),) * pairs)


def interpolate(first, before, own, after, dep_row, dep_lon, lon_frac, lat_frac, half_rows):
    pairs, fields, pair_length = own.shape
    tiles = pl.cdiv(pair_length, LANES)
    padded = tiles * LANES
    near = pairs + 4
    vm = pl.BlockSpec(memory_space=pltpu.VMEM)
    return pl.pallas_call(
        functools.partial(interp_kernel, half_rows, pair_length),
        out_shape=jax.ShapeDtypeStruct((pairs, fields, padded), jnp.bfloat16),
        in_specs=[pl.BlockSpec(memory_space=pltpu.SMEM)] + [vm] * 7,
        out_specs=vm,
        scratch_shapes=[
            pltpu.VMEM((near, fields, EW), jnp.bfloat16),
            pltpu.VMEM((2 * near, fields, EW), jnp.bfloat16),
            pltpu.VMEM((5, 8, padded), jnp.int32),
            pltpu.VMEM((20, 8, padded), jnp.float32),
            pltpu.VMEM((8, padded), jnp.int32),
            pltpu.VMEM((4, 8, padded), jnp.int32),
            pltpu.VMEM((4, 8, padded), jnp.float32),
            pltpu.VMEM((8, padded), jnp.float32),
        ],
        name="interp",
    )(first, before, own, after, dep_row, dep_lon, lon_frac, lat_frac)


def cos_sin_turns(prod, length, inverse):
    turns = jnp.floor(prod * inverse + 0.5)
    t = (prod - turns * length) * inverse
    x = t * t
    c = jnp.full_like(x, COS[-1])
    for a in COS[-2::-1]:
        c = c * x + a
    s = jnp.full_like(x, SIN[-1])
    for a in SIN[-2::-1]:
        s = s * x + a
    return c, s * t


COS = (1, -19.7392087, 64.9393842, -85.4565372, 60.2407014, -26.3960673, 7.77462739, -1.42354417)
SIN = (6.28318531, -41.3417022, 81.6052456, -76.7057546, 42.0572162, -15.0833301, 3.7717259, -0.609657301)


def fourier_kernel(half_rows, pair_length, first_ref, y_ref, order_ref, out_ref, table_s, sums_s, four_s, mix_s, send_s):
    pairs = y_ref.shape[0]
    tiles = pl.cdiv(pair_length, LANES)
    first = first_ref[0]
    north = first < half_rows // 2
    parts = 8

    def one(i, _):
        q = i >> 1
        half = i & 1
        pair = first + q
        inner = jnp.where(north, pair, half_rows - 1 - pair)
        len0 = 16 + 4 * (half_rows // 2 - inner)
        start = jnp.where(half == 1, len0, 0)
        whole = jnp.where(half == 1, 16 + 4 * (half_rows // 2 + 1 + inner), len0)
        def waves(rows):
            return lax.broadcasted_iota(jnp.int32, (rows, half_rows), 1)
        def line(rows):
            return lax.broadcasted_iota(jnp.int32, (rows, half_rows), 0)
        length = jnp.full((1, half_rows), whole, jnp.int32).astype(jnp.float32)
        inverse = 1.0 / length
        fine_c, fine_s = cos_sin_turns((waves(16) * line(16)).astype(jnp.float32), length, inverse)
        step_c, step_s = cos_sin_turns((waves(8) * (16 * line(8))).astype(jnp.float32), length, inverse)
        for a in range(8):
            ca, sa = step_c[a:a + 1], step_s[a:a + 1]
            table_s[pl.ds(16 * a, 16), pl.ds(0, half_rows)] = (ca * fine_c - sa * fine_s).astype(jnp.bfloat16)
            table_s[pl.ds(16 * a, 16), pl.ds(half_rows, half_rows)] = (sa * fine_c + ca * fine_s).astype(jnp.bfloat16)
        lane = lax.broadcasted_iota(jnp.int32, (parts, LANES), 1)
        blocks = []
        for t in range(tiles):
            col = lane + t * LANES
            mine = (col >= start) & (col < start + whole)
            blocks.append(jnp.where(mine, y_ref[q, :, pl.ds(t * LANES, LANES)].astype(jnp.float32)[:parts], 0.0))
        stacked = jnp.concatenate(blocks, axis=0).astype(jnp.bfloat16)
        sums_s[...] = jnp.dot(stacked, table_s[...], preferred_element_type=jnp.float32)
        tile_c, tile_s = cos_sin_turns((waves(24) * (LANES * line(24) - start)).astype(jnp.float32), length, inverse)
        real = jnp.zeros((parts, half_rows), jnp.float32)
        imag = jnp.zeros((parts, half_rows), jnp.float32)
        for t in range(tiles):
            c = sums_s[pl.ds(parts * t, parts), pl.ds(0, half_rows)]
            s = sums_s[pl.ds(parts * t, parts), pl.ds(half_rows, half_rows)]
            tc, ts = tile_c[t:t + 1], tile_s[t:t + 1]
            real = real + (tc * c - ts * s)
            imag = imag - (ts * c + tc * s)
        keep = jnp.where(2 * waves(1) < whole, inverse, 0.0)
        place = 2 * jnp.where(north, q, pairs - 1 - q) + half
        four_s[pl.ds(pl.multiple_of(place * 16, 16), 16), :] = jnp.concatenate([real * keep, imag * keep], axis=0).astype(jnp.bfloat16)
        return 0

    lax.fori_loop(0, 2 * pairs, one, 0)

    hot = (lax.broadcasted_iota(jnp.int32, (half_rows, half_rows), 0) == order_ref[...]).astype(jnp.float32).astype(jnp.bfloat16)
    moved = jnp.dot(four_s[...], hot, preferred_element_type=jnp.float32)
    slots = half_rows // LANES
    mix_s[...] = jnp.zeros_like(mix_s)
    send_s[...] = jnp.zeros_like(send_s)
    for r in range(2 * pairs):
        for s in range(slots):
            mix_s[pl.ds(s, 16, stride=8), :] = moved[16 * r:16 * r + 16, s * LANES:(s + 1) * LANES]
        send_s[pl.ds(r, LANES, stride=16), :] = mix_s[...].T
    out_ref[...] = send_s[...].astype(jnp.bfloat16).reshape(out_ref.shape)


def fourier(first, y, order, half_rows, pair_length):
    pairs = y.shape[0]
    tiles = pl.cdiv(pair_length, LANES)
    vm = pl.BlockSpec(memory_space=pltpu.VMEM)
    return pl.pallas_call(
        functools.partial(fourier_kernel, half_rows, pair_length),
        out_shape=jax.ShapeDtypeStruct((LANES, 16, LANES), jnp.bfloat16),
        in_specs=[pl.BlockSpec(memory_space=pltpu.SMEM), vm, vm],
        out_specs=vm,
        scratch_shapes=[
            pltpu.VMEM((LANES, 2 * half_rows), jnp.bfloat16),
            pltpu.VMEM((8 * tiles, 2 * half_rows), jnp.float32),
            pltpu.VMEM((32 * pairs, half_rows), jnp.bfloat16),
            pltpu.VMEM((LANES, LANES), jnp.float32),
            pltpu.VMEM((16 * LANES, LANES), jnp.float32),
        ],
        name="fourier",
    )(first, y, order)


def spectral_kernel(half_rows, waves_ref, got_ref, legendre_ref, out_ref, sym_f, anti_f, sym_b, anti_b, acc_s, z_s):
    s = pl.program_id(0)
    slots = pl.num_programs(0)
    devices = got_ref.shape[0]
    rows = 2 * half_rows // devices

    @pl.when(s == 0)
    def _():
        for d in range(devices // 2):
            n = got_ref[d].astype(jnp.float32)
            o = got_ref[devices - 1 - d].astype(jnp.float32)
            sym_f[pl.ds(rows * d, 16), :] = n + o
            anti_f[pl.ds(rows * d, 16), :] = n - o
        sym_b[...] = sym_f[pl.ds(0, half_rows), :].astype(jnp.bfloat16)
        anti_b[...] = anti_f[pl.ds(0, half_rows), :].astype(jnp.bfloat16)
        acc_s[...] = jnp.zeros_like(acc_s)

    lane = lax.broadcasted_iota(jnp.int32, (half_rows, LANES), 1)
    mine = (lane & 7) == s
    for par, values in ((0, sym_b), (1, anti_b)):
        chosen = jnp.where(mine, values[...].astype(jnp.float32), 0.0).astype(jnp.bfloat16)
        acc_s[par] = acc_s[par] + jnp.dot(legendre_ref[0, par], chosen, preferred_element_type=jnp.float32)

    @pl.when(s == slots - 1)
    def _():
        for par in range(2):
            z_s[pl.ds(par, half_rows // 2, stride=2), :] = acc_s[par]
        z = z_s[...].T.reshape(16, 8, half_rows)
        sub = lax.broadcasted_iota(jnp.int32, (8, half_rows), 0)
        j = lax.broadcasted_iota(jnp.int32, (8, half_rows), 1)
        limit = jnp.zeros((8, half_rows), jnp.int32)
        for i in range(5):
            limit = jnp.where(sub == i, half_rows - waves_ref[i], limit)
        z = jnp.where((j < limit)[None], z, 0.0)
        out_ref[...] = z[:, :out_ref.shape[1], :]


def spectral(waves, got, legendre, half_rows):
    slots = legendre.shape[0]
    return pl.pallas_call(
        functools.partial(spectral_kernel, half_rows),
        grid=(slots,),
        out_shape=jax.ShapeDtypeStruct((16, slots, half_rows), jnp.float32),
        in_specs=[
            pl.BlockSpec(memory_space=pltpu.SMEM),
            pl.BlockSpec(got.shape, lambda s: (0, 0, 0)),
            pl.BlockSpec((1,) + legendre.shape[1:], lambda s: (s, 0, 0, 0)),
        ],
        out_specs=pl.BlockSpec((16, slots, half_rows), lambda s: (0, 0, 0)),
        scratch_shapes=[
            pltpu.VMEM((half_rows + 16, LANES), jnp.float32),
            pltpu.VMEM((half_rows + 16, LANES), jnp.float32),
            pltpu.VMEM((half_rows, LANES), jnp.bfloat16),
            pltpu.VMEM((half_rows, LANES), jnp.bfloat16),
            pltpu.VMEM((2, half_rows // 2, LANES), jnp.float32),
            pltpu.VMEM((half_rows, LANES), jnp.float32),
        ],
        name="spectral",
    )(waves, got, legendre)


def exchange_kernel(across, send_ref, got_ref, send_sem, recv_sem, own_sem):
    devices = send_ref.shape[0]
    me = lax.axis_index("aa") * across + lax.axis_index("ba")

    def partner(i):
        other = lax.rem(me + i, devices)
        return other, (other // across, lax.rem(other, across))

    barrier = pltpu.get_barrier_semaphore()

    def greet(i, _):
        pl.semaphore_signal(barrier, inc=1, device_id=partner(i)[1], device_id_type=pl.DeviceIdType.MESH)
        return 0

    lax.fori_loop(1, devices, greet, 0)
    pl.semaphore_wait(barrier, devices - 1)

    def post(i, _):
        other, where = partner(i)
        pltpu.make_async_remote_copy(
            src_ref=send_ref.at[other], dst_ref=got_ref.at[me], send_sem=send_sem, recv_sem=recv_sem,
            device_id=where, device_id_type=pl.DeviceIdType.MESH).start()
        return 0

    lax.fori_loop(1, devices, post, 0)
    own = pltpu.make_async_copy(send_ref.at[me], got_ref.at[me], own_sem)
    own.start()
    rest = pl.ds(0, devices - 1)
    every = pltpu.make_async_remote_copy(
        src_ref=send_ref.at[rest], dst_ref=got_ref.at[rest], send_sem=send_sem, recv_sem=recv_sem,
        device_id=partner(1)[1], device_id_type=pl.DeviceIdType.MESH)
    every.wait_send()
    every.wait_recv()
    own.wait()


def exchange(send, across):
    anywhere = pl.BlockSpec(memory_space=pl.ANY)
    return pl.pallas_call(
        functools.partial(exchange_kernel, across),
        out_shape=jax.ShapeDtypeStruct(send.shape, send.dtype),
        in_specs=[anywhere],
        out_specs=anywhere,
        scratch_shapes=[pltpu.SemaphoreType.DMA, pltpu.SemaphoreType.DMA, pltpu.SemaphoreType.DMA],
        compiler_params=pltpu.CompilerParams(collective_id=0, has_side_effects=True),
        name="exchange",
    )(send)


def on_device(grid, dep_row, dep_lon, lon_frac, lat_frac, wave_slot, legendre):
    half_rows = wave_slot.shape[0]
    fields, levels, pairs, pair_length = grid.shape
    slots = legendre.shape[0]
    axes = ("aa", "ba")
    devices = lax.axis_size(axes)
    device = lax.axis_index(axes)
    first = (device * pairs).astype(jnp.int32).reshape(1)
    own = jnp.transpose(grid.reshape(fields * levels, pairs, pair_length), (1, 0, 2))
    up = [(i, i + 1) for i in range(devices - 1)]
    down = [(j, i) for i, j in up]
    before = lax.ppermute(own[pairs - 2:], axes, up)
    after = lax.ppermute(own[:2], axes, down)
    order = jnp.transpose(wave_slot.reshape(devices, slots)).reshape(1, half_rows)
    waves = lax.dynamic_slice_in_dim(wave_slot, device * slots, slots)
    y = interpolate(first, before, own, after, dep_row, dep_lon, lon_frac, lat_frac, half_rows)
    send = fourier(first, y, order, half_rows, pair_length)
    got = exchange(send, lax.axis_size("ba"))
    result = spectral(waves, got, legendre, half_rows)
    interpolated = jnp.transpose(y[:, :, :pair_length], (1, 0, 2)).reshape(grid.shape)
    return (interpolated, result)


def solution(mesh):
    return jax.shard_map(
        on_device,
        mesh=mesh,
        in_specs=(
            P(None, None, ("aa", "ba"), None),
            P(("aa", "ba"), None),
            P(None, ("aa", "ba"), None),
            P(None, ("aa", "ba"), None),
            P(("aa", "ba"), None),
            P(),
            P(("aa", "ba"), None, None, None),
        ),
        out_specs=(P(None, None, ("aa", "ba"), None), P(None, ("aa", "ba"), None)),
        check_vma=False,
    )
```

time: 1110 us -> 77.2 us (0.07); the launches traced: 1090 us -> 76.7 us
  local copies, waits for them, and re-layouts: 537 us -> 12.2 us
  other arithmetic: 506 us -> 0 us
  Pallas kernels: 0 us -> 55.1 us
    gather x32 -> x0, local copies, waits for them, and re-layouts: 498 us -> none  [interpolate(): jnp.take(flattened, indices[term_index], axis=1).astype(jnp.float32)]
    another operation x6 -> x0, other arithmetic: 466 us -> none
    pallas_call x0 -> x4, Pallas kernels: none -> 55.1 us  [the longest x1 22.9 us: interpolate(): pl.pallas_call(functools.partial(interp_kernel, half_rows, pair_length),...]
    add x2 -> x0, other arithmetic: 14.7 us -> none  [the longest x1 14.7 us: stencil(): base_index + jnp.remainder(dep_lon[stencil_row] + (offset - 1), row_length)]
    reshape x22 -> x3, local copies, waits for them, and re-layouts: 14.1 us -> 1.18 us  [the longest x1 0.88 us: on_device(): wave_slot.reshape(devices, slots)]
  transfers between devices with their start and end apart: 3 -> 2, of which waited for: 1 -> 0; matrix products, arithmetic and copies ran while one was open for 4% -> 8% of each run, Pallas kernels for 0% -> 0%
where the time goes in v1:
time: 77.2 us; the launch traced here: 76.7 us
  Pallas kernels  55.1 us (71%)
  local copies, waits for them, and re-layouts  12.2 us (16%)
  starting transfers between devices  8.8 us (11%)
    pallas_call x1, Pallas kernels, interpolate(): pl.pallas_call(functools.partial(interp_kernel, half_rows, pair_length),...  22.9 us
    pallas_call x1, Pallas kernels, exchange(): pl.pallas_call(functools.partial(exchange_kernel, across), out_shape=jax....  18.9 us
    unnamed x12, local copies, waits for them, and re-layouts  8.51 us
    pallas_call x1, Pallas kernels, fourier(): pl.pallas_call(functools.partial(fourier_kernel, half_rows, pair_length),...  7.4 us
    ppermute x1, starting transfers between devices, on_device(): before = lax.ppermute(own[pairs - 2:], axes, up)  6.88 us
    pallas_call x1, Pallas kernels, spectral(): pl.pallas_call(functools.partial(spectral_kernel, half_rows), grid=(slots...  5.8 us
    ppermute x1, starting transfers between devices, on_device(): after = lax.ppermute(own[:2], axes, down)  1.92 us
  transfers between devices with their start and end apart: 2, of which 0 were waited for; matrix products, arithmetic and copies ran while one was open for 8% of the time, Pallas kernels for 0%

profile of v1, /device:TPU:1, one launch (start us, length us, event | category | flops | bytes accessed | tf_op | source)
XLA Modules:
  0.0 76.7 jit_solution(5549436428244032877)
XLA Ops:
  0.6 1.2 %copy.14 = bf16[4,4,5,2596]{3,1,0,2:T(4,128)(2,1)S(1)} copy(bf16[4,4,5,2596]{3,1,2,0:T(4,128)(2,1)} %param.7) | data formatting | bytes 830720 | tf_op args[0]
  1.8 0.2 reshape.20
  2.0 0.0 copy-start
  2.0 6.9 %collective-permute-start = (bf16[2,16,2596]{2,1,0:T(8,128)(2,1)S(1)}, bf16[2,16,2596]{2,1,0:T(8,128)(2,1)S(1)}, u32[]{:S(2)}, u32[]{:S(2)}) collective-permute-start(bf16[2,16,2596]{2,1,0:T(8,128)(2,1)S(1)} %get-tuple-element.7), channel_id=1, source_target_pairs={{0,1},{1,2},{2,3},{3,4},{4,5},{5,6},{6,7},{7,8},{8,9},{9,10},{10,1... | collective-permute-start | bytes 498440 | tf_op jit(solution)/shard_map/ppermute | solution.py:469
  8.9 1.9 %collective-permute-start.1 = (bf16[2,16,2596]{2,1,0:T(8,128)(2,1)S(1)}, bf16[2,16,2596]{2,1,0:T(8,128)(2,1)S(1)}, u32[]{:S(2)}, u32[]{:S(2)}) collective-permute-start(bf16[2,16,2596]{2,1,0:T(8,128)(2,1)S(1)} %get-tuple-element.6), channel_id=1, source_target_pairs={{1,0},{2,1},{3,2},{4,3},{5,4},{6,5},{7,6},{8,7},{9,8},{10,9},{11,1... | collective-permute-start | bytes 498440 | tf_op jit(solution)/shard_map/ppermute | solution.py:470
  10.9 1.7 %copy.15.lon_ref = s32[4,5,2596]{2,1,0:T(8,128)} copy(s32[4,5,2596]{2,0,1:T(4,128)} %param.9) | data formatting | bytes 415360 | tf_op args[2]
  12.6 1.7 %copy.16.lonf_ref = f32[4,5,2596]{2,1,0:T(8,128)} copy(f32[4,5,2596]{2,0,1:T(4,128)} %param.10) | data formatting | bytes 415360 | tf_op args[3]
  14.3 0.9 %reshape.22 = s32[128,5]{1,0:T(8,128)S(1)} reshape(s32[640]{0:T(1024)} %param.12) | data formatting | bytes 5120 | tf_op jit(solution)/shard_map/reshape | solution.py:471
  15.2 0.1 copy.17
  15.2 0.6 copy.22
  15.9 1.3 %dynamic_slice.3.waves_ref = s32[5]{0:T(128)} dynamic-slice(s32[640]{0:T(1024)} %param.12, s32[]{:T(128)S(6)} %select_n.3), dynamic_slice_sizes={5} | dynamic-slice | bytes 44 | tf_op jit(solution)/shard_map/dynamic_slice | solution.py:472
  17.2 0.0 collective-permute-done.before_ref
  17.2 0.0 copy-start.1
  17.2 0.0 collective-permute-done.1.after_ref
  17.2 0.0 copy-start.2
  17.2 0.0 copy-done
  17.2 0.6 copy-done.1
  17.9 0.1 copy-done.2
  17.9 22.9 %interp.1.y_ref = bf16[5,16,2688]{2,1,0:T(8,128)(2,1)} custom-call(s32[1]{0:T(128)} %bitcast.first_ref, bf16[2,16,2596]{2,1,0:T(8,128)(2,1)} %copy-done.1, bf16[5,16,2596]{2,1,0:T(8,128)(2,1)} %bitcast.15, bf16[2,16,2596]{2,1,0:T(8,128)(2,1)} %copy-done.2, s32[5,2596]{1,0:T(8,128)} %row_ref.1, s32[4,5,2596]{2,1,0:T(8,128)} %copy.15.lon_ref, ...), custom_call_target="tpu_custom_call" | custom-call | tf_op jit(solution)/shard_map/interp/pallas_call | solution.py:229
  40.9 1.0 %slice_bitcast_fusion = bf16[16,5,2596]{2,0,1:T(8,128)(2,1)S(1)} fusion(bf16[5,16,2688]{2,1,0:T(8,128)(2,1)} %interp.1.y_ref), kind=kLoop, calls=%fused_computation | loop fusion | bytes 830720 | tf_op jit(solution)/shard_map/transpose | solution.py:477
  41.9 7.4 %fourier.1.send_ref = bf16[128,16,128]{2,1,0:T(8,128)(2,1)} custom-call(s32[1]{0:T(128)} %bitcast.first_ref, bf16[5,16,2688]{2,1,0:T(8,128)(2,1)} %interp.1.y_ref, s32[1,640]{1,0:T(1,128)} %bitcast.18), custom_call_target="tpu_custom_call" | custom-call | tf_op jit(solution)/shard_map/fourier/pallas_call | solution.py:332
  49.3 18.9 %exchange.1.got_ref = bf16[128,16,128]{2,1,0:T(8,128)(2,1)} custom-call(bf16[128,16,128]{2,1,0:T(8,128)(2,1)} %fourier.1.send_ref), custom_call_target="tpu_custom_call" | custom-call | tf_op jit(solution)/shard_map/exchange/pallas_call | solution.py:447
  68.2 5.8 %spectral.1 = f32[16,5,640]{2,1,0:T(8,128)} custom-call(s32[5]{0:T(128)} %dynamic_slice.3.waves_ref, bf16[128,16,128]{2,1,0:T(8,128)(2,1)} %exchange.1.got_ref, bf16[5,2,320,640]{3,2,1,0:T(8,128)(2,1)} %legendre_ref.1), custom_call_target="tpu_custom_call" | custom-call | tf_op jit(solution)/shard_map/spectral/pallas_call | solution.py:387
  74.0 1.7 %copy.19 = f32[16,5,640]{2,0,1:T(8,128)} copy(f32[16,5,640]{2,1,0:T(8,128)} %spectral.1) | data formatting | bytes 409600
  75.7 0.1 reshape.21
  75.8 0.9 %copy.18 = bf16[4,4,5,2596]{3,1,2,0:T(4,128)(2,1)} copy(bf16[4,4,5,2596]{3,1,0,2:T(4,128)(2,1)S(1)} %reshape.21) | data formatting | bytes 830720
  (1 shorter events, 0.0 us)
Async XLA Ops:
  2.0 15.2 %copy-start = (bf16[16,5,2596]{2,0,1:T(8,128)(2,1)}, bf16[16,5,2596]{2,0,1:T(8,128)(2,1)S(1)}, u32[]{:S(2)}) copy-start(bf16[16,5,2596]{2,0,1:T(8,128)(2,1)S(1)} %reshape.20) | copy-start | bytes 1246084
  2.0 15.2 %collective-permute-start = (bf16[2,16,2596]{2,1,0:T(8,128)(2,1)S(1)}, bf16[2,16,2596]{2,1,0:T(8,128)(2,1)S(1)}, u32[]{:S(2)}, u32[]{:S(2)}) collective-permute-start(bf16[2,16,2596]{2,1,0:T(8,128)(2,1)S(1)} %get-tuple-element.7), channel_id=1, source_target_pairs={{0,1},{1,2},{2,3},{3,4},{4,5},{5,6},{6,7},{7,8},{8,9},{9,10},{10,1... | collective-permute-start | bytes 498440 | tf_op jit(solution)/shard_map/ppermute | solution.py:469
  8.9 8.3 %collective-permute-start.1 = (bf16[2,16,2596]{2,1,0:T(8,128)(2,1)S(1)}, bf16[2,16,2596]{2,1,0:T(8,128)(2,1)S(1)}, u32[]{:S(2)}, u32[]{:S(2)}) collective-permute-start(bf16[2,16,2596]{2,1,0:T(8,128)(2,1)S(1)} %get-tuple-element.6), channel_id=1, source_target_pairs={{1,0},{2,1},{3,2},{4,3},{5,4},{6,5},{7,6},{8,7},{9,8},{10,9},{11,1... | collective-permute-start | bytes 498440 | tf_op jit(solution)/shard_map/ppermute | solution.py:470
  17.2 0.7 copy-start.1
  17.2 0.7 copy-start.2

commit v2 on v1

v2 whole, which is shorter than its diff:
```python
import functools

import jax
import jax.numpy as jnp
from jax import lax
from jax.experimental import pallas as pl
from jax.experimental.pallas import tpu as pltpu
from jax.sharding import PartitionSpec as P

LANES = 128
WIN = 256
ETILES = 24
EW = ETILES * LANES
MARGIN = 60
ROWS = 11
NOWHERE = 192.0


def row_place(global_row, half_rows):
    northern = global_row < half_rows
    number = jnp.where(northern, global_row + 1, 2 * half_rows - global_row)
    second = number > half_rows // 2
    inner = jnp.where(second, number - half_rows // 2 - 1, half_rows // 2 - number)
    begin = jnp.where(second, 16 + 4 * (half_rows // 2 - inner), 0)
    return jnp.where(northern, inner, half_rows - 1 - inner), begin, 16 + 4 * number


def cubic(t):
    return (
        -t * (t - 1.0) * (t - 2.0) * (1.0 / 6.0),
        (t + 1.0) * (t - 1.0) * (t - 2.0) * 0.5,
        -(t + 1.0) * t * (t - 2.0) * 0.5,
        (t + 1.0) * t * (t - 1.0) * (1.0 / 6.0),
    )


def interp_kernel(half_rows, pair_length, first_ref, before_ref, own_ref, after_ref,
                  row_ref, lon_ref, lonf_ref, latf_ref, out_ref,
                  place_t, ext_s, plan_s, row_p, lon_p, lonf_p, latf_p):
    pairs = own_ref.shape[0]
    fields = own_ref.shape[1]
    near = pairs + 4
    tiles = pl.cdiv(pair_length, LANES)
    first = first_ref[0]

    ext_s[:, :, pl.ds(0, LANES)] = jnp.zeros((2 * near, fields, LANES), jnp.bfloat16)
    ext_s[:, :, pl.ds(tiles * LANES, EW - tiles * LANES)] = jnp.zeros((2 * near, fields, EW - tiles * LANES), jnp.bfloat16)
    for j in range(near):
        src = before_ref[j] if j < 2 else (own_ref[j - 2] if j < 2 + pairs else after_ref[j - 2 - pairs])
        ext_s[2 * j, :, pl.ds(LANES, pair_length)] = src
        ext_s[2 * j + 1, :, pl.ds(LANES, pair_length)] = src

    row_p[...] = jnp.zeros_like(row_p)
    lon_p[...] = jnp.zeros_like(lon_p)
    lonf_p[...] = jnp.zeros_like(lonf_p)
    latf_p[...] = jnp.zeros_like(latf_p)
    row_p[pl.ds(0, pairs), pl.ds(0, pair_length)] = row_ref[...]
    latf_p[pl.ds(0, pairs), pl.ds(0, pair_length)] = latf_ref[...]
    for r in range(4):
        lon_p[r, pl.ds(0, pairs), pl.ds(0, pair_length)] = lon_ref[r]
        lonf_p[r, pl.ds(0, pairs), pl.ds(0, pair_length)] = lonf_ref[r]

    lane = lax.broadcasted_iota(jnp.int32, (fields, LANES), 1)

    def half_lengths(pair):
        inner = jnp.where(pair < half_rows // 2, pair, half_rows - 1 - pair)
        return 16 + 4 * (half_rows // 2 - inner), 16 + 4 * (half_rows // 2 + 1 + inner)

    def wrap(copy, tile, shift, low, edge):
        at = pl.ds(pl.multiple_of(tile * LANES, LANES), LANES)
        begin = tile * LANES + shift
        two = ext_s[copy, :, pl.ds(pl.multiple_of((begin >> 7) * LANES, LANES), 2 * LANES)].astype(jnp.float32)
        moved = pltpu.roll(two, (2 * LANES - (begin & 127)) & 255, 1)[:, :LANES]
        spot = lane + tile * LANES
        beyond = spot < edge if low else spot >= edge
        return copy, at, jnp.where(beyond, moved, ext_s[copy, :, at].astype(jnp.float32)).astype(jnp.bfloat16)

    for j in range(near):
        len0, len1 = half_lengths(first + j - 2)
        wraps = []
        for half in range(2):
            start, length = (len0, len1) if half else (0, len0)
            for i in range(1 + half):
                wraps.append(wrap(2 * j + half, ((start >> 7) if half else 0) + i, length, True, start + LANES))
            for i in range(3):
                wraps.append(wrap(2 * j + half, ((start + length) >> 7) + 1 + i, -length, False, start + length + LANES))
        for copy, at, tile in wraps:
            ext_s[copy, :, at] = tile

    sub8 = lax.broadcasted_iota(jnp.int32, (8, LANES), 0)
    lane8 = lax.broadcasted_iota(jnp.int32, (8, LANES), 1)

    def weigh(tile, fits):
        at = pl.ds(pl.multiple_of(tile * LANES, LANES), LANES)
        col = tile * LANES + lane8
        pair = first + sub8
        northern = pair < half_rows // 2
        len0, len1 = half_lengths(pair)
        second = col >= len0
        inner = jnp.where(northern, pair, half_rows - 1 - pair)
        number = jnp.where(second, half_rows // 2 + 1 + inner, half_rows // 2 - inner)
        g = jnp.where(northern, number - 1, 2 * half_rows - number)
        base = jnp.clip(g - 2, 0, 2 * half_rows - 4)
        later = (row_p[:, at] - base) > 0
        k0 = jnp.where(second, jnp.maximum(tile * LANES - len0, 0), tile * LANES)
        base_k = k0 - MARGIN
        inside = (col < pair_length) & (sub8 < pairs)
        latw = cubic(latf_p[:, at])
        lons = [lon_p[r, :, at] for r in range(4)]
        lonfs = [lonf_p[r, :, at] for r in range(4)]
        zero = jnp.zeros((8, LANES), jnp.float32)
        for d in range(5):
            hi, lo = min(d, 3), max(d - 1, 0)
            lon = jnp.where(later, lons[lo], lons[hi])
            frac = jnp.where(later, lonfs[lo], lonfs[hi])
            lat = jnp.where(later, latw[lo] if d >= 1 else zero, latw[hi] if d <= 3 else zero)
            _, begin, length = row_place(jnp.minimum(base + d, 2 * half_rows - 1), half_rows)
            rel = lon - 1 - base_k
            rel = jnp.where(rel < 0, rel + length, jnp.where(rel >= length, rel - length, rel))
            short = length <= WIN - 4
            rel = jnp.where(short, lon, rel)
            bad = inside & (lat != 0.0) & ((rel < 0) | (rel > WIN - 4))
            fits = jnp.maximum(fits, bad.astype(jnp.int32))
            place = ((begin + jnp.where(short, -1, base_k) + LANES) & 127) + rel
            block = (place >> 4) & 15
            lat = jnp.where(inside, lat, 0.0)
            ws = cubic(frac)
            for o in range(4):
                plan_s[d * ROWS + o, :, at] = lat * ws[o]
                plan_s[d * ROWS + 4 + o, :, at] = ((place + o) & 15).astype(jnp.float32)
            plan_s[d * ROWS + 8, :, at] = block.astype(jnp.float32)
            plan_s[d * ROWS + 9, :, at] = ((block + 1) & 15).astype(jnp.float32)
            plan_s[d * ROWS + 10, :, at] = (lon + begin).astype(jnp.float32)
        return fits

    worst = lax.fori_loop(0, tiles, weigh, jnp.zeros((8, LANES), jnp.int32))
    local = jnp.max(worst) == 0

    node = lax.broadcasted_iota(jnp.int32, (16, LANES), 0).astype(jnp.float32).astype(jnp.bfloat16)
    zero16 = jnp.zeros((16, LANES), jnp.bfloat16)

    def spread(mine, weight, rest, block, after):
        v = zero16
        for o in (3, 2, 1, 0):
            v = jnp.where(node == rest[o], weight[o], v)
        block = jnp.where(mine, jnp.where(node < rest[0], after, block), jnp.bfloat16(NOWHERE))
        return [jnp.where(block == jnp.bfloat16(a), v, zero16) for a in range(WIN // 16)]

    def plan(d, i, q, at):
        return jnp.broadcast_to(plan_s[d * ROWS + i, pl.ds(q, 1), at], (16, LANES))

    def packed(x):
        return x.astype(jnp.bfloat16)

    for q in range(pairs):
        pair = first + q
        northern = pair < half_rows // 2
        inner = jnp.where(northern, pair, half_rows - 1 - pair)
        for half in range(2):
            number = half_rows // 2 + 1 + inner if half else half_rows // 2 - inner
            g = jnp.where(northern, number - 1, 2 * half_rows - number)
            base = jnp.clip(g - 2, 0, 2 * half_rows - 4)
            for d in range(5):
                pair_row, begin, length = row_place(jnp.minimum(base + d, 2 * half_rows - 1), half_rows)
                short = length <= WIN - 4
                copy = 2 * jnp.clip(pair_row - first + 2, 0, near - 1) + (begin > 0).astype(jnp.int32)
                at = 3 * ((2 * q + half) * 5 + d)
                place_t[at] = copy
                place_t[at + 1] = begin + LANES + jnp.where(short, -1, -MARGIN)
                place_t[at + 2] = jnp.where(short, 0, 1)

    def unit_scalars(q, u):
        len0, _ = half_lengths(first + q)
        straddle = len0 >> 7
        half = (u > straddle).astype(jnp.int32)
        tile = u - half
        k0 = jnp.where(half == 1, jnp.maximum(tile * LANES - len0, 0), tile * LANES)
        return len0, straddle, half, tile, 15 * (2 * q + half), k0

    lane16 = lax.broadcasted_iota(jnp.int32, (16, LANES), 1).astype(jnp.float32).astype(jnp.bfloat16)

    def own_half(half, tile, len0):
        edge = jnp.clip(len0 - tile * LANES, 0, LANES)
        low = jnp.where(half == 1, edge, 0).astype(jnp.float32)
        high = jnp.where(half == 1, LANES, edge).astype(jnp.float32)
        spread_low = jnp.full((16, LANES), low, jnp.float32).astype(jnp.bfloat16)
        spread_high = jnp.full((16, LANES), high, jnp.float32).astype(jnp.bfloat16)
        return (lane16 >= spread_low) & (lane16 < spread_high)

    def finish(q, u, straddle, tile, total, carry):
        total = total + jnp.where(u == straddle + 1, carry, 0.0)
        out_ref[q, :, pl.ds(pl.multiple_of(tile * LANES, LANES), LANES)] = total.astype(jnp.bfloat16)
        return total

    @pl.when(local)
    def _():
        def unit(q, u, carry):
            len0, straddle, half, tile, base, k0 = unit_scalars(q, u)
            at = pl.ds(pl.multiple_of(tile * LANES, LANES), LANES)
            mine = own_half(half, tile, len0)
            rows, weights = [], []
            for d in range(5):
                where_row = place_t[base + 3 * d]
                begin = place_t[base + 3 * d + 1] + place_t[base + 3 * d + 2] * k0
                s = begin & 127
                first_tile = pl.multiple_of((begin >> 7) * LANES, LANES)
                row = [packed(plan(d, i, q, at)) for i in range(10)]
                weights += spread(mine, row[:4], row[4:8], row[8], row[9])
                three = ext_s[where_row, :, pl.ds(first_tile, 3 * LANES)]
                rows += [jnp.where(lane >= s, three[:, :LANES], three[:, 2 * LANES:]), three[:, LANES:2 * LANES]]
            total = jnp.dot(jnp.concatenate(rows, axis=1), jnp.concatenate(weights, axis=0),
                            preferred_element_type=jnp.float32)
            return finish(q, u, straddle, tile, total, carry)

        lax.fori_loop(0, tiles + 1, lambda u, carry: tuple(unit(q, u, carry[q]) for q in range(pairs)),
                      (jnp.zeros((fields, LANES), jnp.float32),) * pairs)

    @pl.when(jnp.logical_not(local))
    def _():
        def unit(q, u, carry):
            len0, straddle, half, tile, base, _ = unit_scalars(q, u)
            at = pl.ds(pl.multiple_of(tile * LANES, LANES), LANES)
            mine = own_half(half, tile, len0)

            def window(w, total):
                rows, weights = [], []
                for d in range(5):
                    where_row = place_t[base + 3 * d]
                    place = (plan(d, 10, q, at) + (LANES - 1)).astype(jnp.int32) - w * WIN
                    block = jnp.clip(place >> 4, -2, 18)
                    rest = [packed(((place + o) & 15).astype(jnp.float32)) for o in range(4)]
                    weight = [packed(plan(d, o, q, at)) for o in range(4)]
                    weights += spread(mine, weight, rest, packed(block.astype(jnp.float32)), packed((block + 1).astype(jnp.float32)))
                    rows.append(ext_s[where_row, :, pl.ds(pl.multiple_of(w * WIN, WIN), WIN)])
                return total + jnp.dot(jnp.concatenate(rows, axis=1), jnp.concatenate(weights, axis=0),
                                       preferred_element_type=jnp.float32)

            total = lax.fori_loop(0, EW // WIN, window, jnp.zeros((fields, LANES), jnp.float32))
            return finish(q, u, straddle, tile, total, carry)

        lax.fori_loop(0, tiles + 1, lambda u, carry: tuple(unit(q, u, carry[q]) for q in range(pairs)),
                      (jnp.zeros((fields, LANES), jnp.float32),) * pairs)


def interpolate(first, before, own, after, dep_row, dep_lon, lon_frac, lat_frac, half_rows):
    pairs, fields, pair_length = own.shape
    tiles = pl.cdiv(pair_length, LANES)
    padded = tiles * LANES
    near = pairs + 4
    vm = pl.BlockSpec(memory_space=pltpu.VMEM)
    return pl.pallas_call(
        functools.partial(interp_kernel, half_rows, pair_length),
        out_shape=jax.ShapeDtypeStruct((pairs, fields, padded), jnp.bfloat16),
        in_specs=[pl.BlockSpec(memory_space=pltpu.SMEM)] + [vm] * 7,
        out_specs=vm,
        scratch_shapes=[
            pltpu.SMEM((30 * pairs,), jnp.int32),
            pltpu.VMEM((2 * near, fields, EW), jnp.bfloat16),
            pltpu.VMEM((5 * ROWS, 8, padded), jnp.float32),
            pltpu.VMEM((8, padded), jnp.int32),
            pltpu.VMEM((4, 8, padded), jnp.int32),
            pltpu.VMEM((4, 8, padded), jnp.float32),
            pltpu.VMEM((8, padded), jnp.float32),
        ],
        name="interp",
    )(first, before, own, after, dep_row, dep_lon, lon_frac, lat_frac)


COS = (1, -19.7392087, 64.9393842, -85.4565372, 60.2407014, -26.3960673, 7.77462739, -1.42354417)
SIN = (6.28318531, -41.3417022, 81.6052456, -76.7057546, 42.0572162, -15.0833301, 3.7717259, -0.609657301)


def cos_sin_turns(prod, length, inverse):
    turns = jnp.floor(prod * inverse + 0.5)
    t = (prod - turns * length) * inverse
    x = t * t
    c = jnp.full_like(x, COS[-1])
    for a in COS[-2::-1]:
        c = c * x + a
    s = jnp.full_like(x, SIN[-1])
    for a in SIN[-2::-1]:
        s = s * x + a
    return c, s * t


def transform_kernel(sizes, pair_length, y_ref, order_ref, waves_ref, legendre_hbm, out_ref,
                     table_s, sums_s, four_s, mix_s, stage_s, send_s, got_s, plain_s, anti_s, kept_s, keptanti_s, turn_s, legendre_s,
                     legendre_sem, own_sem, send_sem, recv_sem):
    along, across = sizes
    devices = along * across
    pairs = y_ref.shape[0]
    slots = legendre_s.shape[0]
    half_rows = slots * devices
    rows = 2 * pairs
    tiles = pl.cdiv(pair_length, LANES)
    my_a = lax.axis_index("aa")
    my_b = lax.axis_index("ba")
    me = my_a * across + my_b
    first = me * pairs
    north = me < devices // 2
    parts = 8

    weights_in = pltpu.make_async_copy(legendre_hbm, legendre_s, legendre_sem)
    weights_in.start()

    columns = [lax.rem(my_b + i, across) for i in range(across)]

    def partners(act):
        for b in range(1, across):
            act(my_a, columns[b])

        def others(i, _):
            a = lax.rem(my_a + i, along)
            for b in range(across):
                act(a, columns[b])
            return 0

        lax.fori_loop(1, along, others, 0)

    barrier = pltpu.get_barrier_semaphore()
    partners(lambda a, b: pl.semaphore_signal(barrier, inc=1, device_id=(a, b), device_id_type=pl.DeviceIdType.MESH))

    def one(i, _):
        q = i // 2
        half = i - 2 * q
        pair = first + q
        inner = jnp.where(north, pair, half_rows - 1 - pair)
        len0 = 16 + 4 * (half_rows // 2 - inner)
        start = jnp.where(half == 1, len0, 0)
        whole = jnp.where(half == 1, 16 + 4 * (half_rows // 2 + 1 + inner), len0)
        length = jnp.full((1, LANES), whole, jnp.int32).astype(jnp.float32)
        inverse = 1.0 / length

        def line(n):
            return lax.broadcasted_iota(jnp.int32, (n, LANES), 0)

        def waves(n, w):
            return lax.broadcasted_iota(jnp.int32, (n, LANES), 1) + w * LANES

        for w in range(slots):
            fine_c, fine_s = cos_sin_turns((waves(16, w) * line(16)).astype(jnp.float32), length, inverse)
            step_c, step_s = cos_sin_turns((waves(8, w) * (16 * line(8))).astype(jnp.float32), length, inverse)
            for a in range(8):
                ca, sa = step_c[a:a + 1], step_s[a:a + 1]
                table_s[pl.ds(16 * a, 16), pl.ds(w * LANES, LANES)] = (ca * fine_c - sa * fine_s).astype(jnp.bfloat16)
                table_s[pl.ds(16 * a, 16), pl.ds(half_rows + w * LANES, LANES)] = (sa * fine_c + ca * fine_s).astype(jnp.bfloat16)
        lane = lax.broadcasted_iota(jnp.int32, (parts, LANES), 1)
        blocks = []
        for t in range(tiles):
            col = lane + t * LANES
            mine = (col >= start) & (col < start + whole)
            blocks.append(jnp.where(mine, y_ref[q, :, pl.ds(t * LANES, LANES)].astype(jnp.float32)[:parts], 0.0))
        stacked = jnp.concatenate(blocks, axis=0).astype(jnp.bfloat16)
        sums_s[...] = jnp.dot(stacked, table_s[...], preferred_element_type=jnp.float32)
        place = 2 * jnp.where(north, q, pairs - 1 - q) + half
        for w in range(slots):
            tile_c, tile_s = cos_sin_turns((waves(24, w) * (LANES * line(24) - start)).astype(jnp.float32), length, inverse)
            real = jnp.zeros((parts, LANES), jnp.float32)
            imag = jnp.zeros((parts, LANES), jnp.float32)
            for t in range(tiles):
                c = sums_s[pl.ds(parts * t, parts), pl.ds(w * LANES, LANES)]
                s = sums_s[pl.ds(parts * t, parts), pl.ds(half_rows + w * LANES, LANES)]
                tc, ts = tile_c[t:t + 1], tile_s[t:t + 1]
                real = real + (tc * c - ts * s)
                imag = imag - (ts * c + tc * s)
            keep = jnp.where(2 * waves(1, w) < whole, inverse, 0.0)
            four_s[pl.ds(pl.multiple_of(place * 16, 16), 16), pl.ds(w * LANES, LANES)] = jnp.concatenate(
                [real * keep, imag * keep], axis=0).astype(jnp.bfloat16)
        return 0

    lax.fori_loop(0, rows, one, 0)

    hot = (lax.broadcasted_iota(jnp.int32, (half_rows, half_rows), 0) == order_ref[...]).astype(jnp.float32).astype(jnp.bfloat16)
    moved = jnp.dot(four_s[...], hot, preferred_element_type=jnp.float32)
    mix_s[...] = jnp.zeros_like(mix_s)
    for r in range(8):
        for s in range(slots):
            mix_s[r, pl.ds(s, 16, stride=8), :] = moved[16 * r:16 * r + 16, s * LANES:(s + 1) * LANES]
        if r < slots:
            for e in range(rows - 8):
                mix_s[r, pl.ds(slots + e, 16, stride=8), :] = moved[16 * (8 + e):16 * (8 + e) + 16, r * LANES:(r + 1) * LANES]
        stage_s[pl.ds(r, LANES, stride=8), :] = mix_s[r].T
    send_s[...] = stage_s[...].astype(jnp.bfloat16).reshape(send_s.shape)

    pl.semaphore_wait(barrier, devices - 1)

    def post(a, b):
        pltpu.make_async_remote_copy(
            src_ref=send_s.at[a * across + b], dst_ref=got_s.at[me], send_sem=send_sem, recv_sem=recv_sem,
            device_id=(a, b), device_id_type=pl.DeviceIdType.MESH).start()

    partners(post)
    own = pltpu.make_async_copy(send_s.at[me], got_s.at[me], own_sem)
    own.start()

    src = lax.broadcasted_iota(jnp.int32, (slots * LANES, 2 * LANES), 0)
    dst = lax.broadcasted_iota(jnp.int32, (slots * LANES, 2 * LANES), 1)
    unfold = ((dst & 7) == (src >> 7)) & ((src & 127) == (dst & 127) - (src >> 7) + slots + (dst >> 7))
    unfold = unfold.astype(jnp.float32).astype(jnp.bfloat16)
    slot_of = (lax.broadcasted_iota(jnp.int32, (half_rows, LANES), 1) & 7).astype(jnp.float32).astype(jnp.bfloat16)
    sub = lax.broadcasted_iota(jnp.int32, (8, half_rows), 0)
    j = lax.broadcasted_iota(jnp.int32, (8, half_rows), 1)
    limit = jnp.zeros((8, half_rows), jnp.int32)
    for i in range(slots):
        limit = jnp.where(sub == i, half_rows - waves_ref[i], limit)

    rest = pl.ds(0, devices - 1)
    every = pltpu.make_async_remote_copy(
        src_ref=send_s.at[rest], dst_ref=got_s.at[rest], send_sem=send_sem, recv_sem=recv_sem,
        device_id=(my_a, columns[1]), device_id_type=pl.DeviceIdType.MESH)
    every.wait_send()
    every.wait_recv()
    own.wait()

    for d in range(devices // 2):
        n = got_s[d].astype(jnp.float32)
        o = got_s[devices - 1 - d].astype(jnp.float32)
        plain_s[pl.ds(rows * d, 8), :] = n + o
        anti_s[pl.ds(rows * d, 8), :] = n - o
        kept_s[pl.ds(8 * d, 8), :] = n + o
        keptanti_s[pl.ds(8 * d, 8), :] = n - o
    weights_in.wait()
    for par, wide, kept in ((0, plain_s, kept_s), (1, anti_s, keptanti_s)):
        folded = jnp.concatenate([kept[pl.ds(s, devices // 2, stride=8), :] for s in range(slots)], axis=1).astype(jnp.bfloat16)
        extra = jnp.dot(folded, unfold, preferred_element_type=jnp.float32)
        for e in range(rows - 8):
            wide[pl.ds(8 + e, devices // 2, stride=rows), :] = extra[:, e * LANES:(e + 1) * LANES]
        values = wide[...].astype(jnp.bfloat16)
        zero = jnp.zeros_like(values)
        picked = jnp.concatenate([jnp.where(slot_of == jnp.bfloat16(s), values, zero) for s in range(slots)], axis=0)
        table = jnp.concatenate([legendre_s[s, par] for s in range(slots)], axis=1)
        turn_s[pl.ds(par, half_rows // 2, stride=2), :] = jnp.dot(table, picked, preferred_element_type=jnp.float32)
    z = turn_s[...].T.reshape(16, 8, half_rows)
    z = jnp.where((j < limit)[None], z, 0.0)
    out_ref[...] = z[:, :slots, :]


def transform(y, order, waves, legendre, half_rows, pair_length, sizes):
    pairs = y.shape[0]
    slots = legendre.shape[0]
    tiles = pl.cdiv(pair_length, LANES)
    vm = pl.BlockSpec(memory_space=pltpu.VMEM)
    f32, b16 = jnp.float32, jnp.bfloat16
    return pl.pallas_call(
        functools.partial(transform_kernel, sizes, pair_length),
        out_shape=jax.ShapeDtypeStruct((16, slots, half_rows), f32),
        in_specs=[vm, vm, pl.BlockSpec(memory_space=pltpu.SMEM), pl.BlockSpec(memory_space=pl.ANY)],
        out_specs=vm,
        scratch_shapes=[
            pltpu.VMEM((LANES, 2 * half_rows), b16),
            pltpu.VMEM((8 * tiles, 2 * half_rows), f32),
            pltpu.VMEM((32 * pairs, half_rows), b16),
            pltpu.VMEM((8, LANES, LANES), f32),
            pltpu.VMEM((8 * LANES, LANES), f32),
            pltpu.VMEM((LANES, 8, LANES), b16),
            pltpu.VMEM((LANES, 8, LANES), b16),
            pltpu.VMEM((half_rows, LANES), f32),
            pltpu.VMEM((half_rows, LANES), f32),
            pltpu.VMEM((8 * LANES // 2, LANES), f32),
            pltpu.VMEM((8 * LANES // 2, LANES), f32),
            pltpu.VMEM((half_rows, LANES), f32),
            pltpu.VMEM(legendre.shape, b16),
            pltpu.SemaphoreType.DMA, pltpu.SemaphoreType.DMA, pltpu.SemaphoreType.DMA, pltpu.SemaphoreType.DMA,
        ],
        compiler_params=pltpu.CompilerParams(collective_id=0, has_side_effects=True),
        name="transform",
    )(y, order, waves, legendre)


def on_device(grid, dep_row, dep_lon, lon_frac, lat_frac, wave_slot, legendre):
    half_rows = wave_slot.shape[0]
    fields, levels, pairs, pair_length = grid.shape
    slots = legendre.shape[0]
    axes = ("aa", "ba")
    sizes = (lax.axis_size("aa"), lax.axis_size("ba"))
    devices = sizes[0] * sizes[1]
    device = lax.axis_index(axes)
    first = (device * pairs).astype(jnp.int32).reshape(1)
    own = jnp.transpose(grid.reshape(fields * levels, pairs, pair_length), (1, 0, 2))
    up = [(i, i + 1) for i in range(devices - 1)]
    down = [(j, i) for i, j in up]
    before = lax.ppermute(own[pairs - 2:], axes, up)
    after = lax.ppermute(own[:2], axes, down)
    order = jnp.transpose(wave_slot.reshape(devices, slots)).reshape(1, half_rows)
    waves = lax.dynamic_slice_in_dim(wave_slot, device * slots, slots)
    y = interpolate(first, before, own, after, dep_row, dep_lon, lon_frac, lat_frac, half_rows)
    result = transform(y, order, waves, legendre, half_rows, pair_length, sizes)
    interpolated = jnp.transpose(y[:, :, :pair_length], (1, 0, 2)).reshape(grid.shape)
    return (interpolated, result)


def solution(mesh):
    return jax.shard_map(
        on_device,
        mesh=mesh,
        in_specs=(
            P(None, None, ("aa", "ba"), None),
            P(("aa", "ba"), None),
            P(None, ("aa", "ba"), None),
            P(None, ("aa", "ba"), None),
            P(("aa", "ba"), None),
            P(),
            P(("aa", "ba"), None, None, None),
        ),
        out_specs=(P(None, None, ("aa", "ba"), None), P(None, ("aa", "ba"), None)),
        check_vma=False,
    )
```

time: 77.2 us -> 56.7 us (0.73)
  Pallas kernels: 55.1 us -> 34.6 us
    pallas_call x3 -> x1, Pallas kernels: 32.1 us -> 21.5 us  [transform(): pl.pallas_call(functools.partial(transform_kernel, sizes, pair_length), o...]
    pallas_call x1, Pallas kernels: 22.9 us -> 13.1 us  [interpolate(): pl.pallas_call(functools.partial(interp_kernel, half_rows, pair_length),...]
  transfers between devices with their start and end apart: 2 -> 2, of which waited for: 0 -> 0; matrix products, arithmetic and copies ran while one was open for 8% -> 11% of each run, Pallas kernels for 0% -> 0%
where the time goes in v2:
time: 56.7 us; the launch traced here: 56.3 us
  Pallas kernels  34.6 us (61%)
  local copies, waits for them, and re-layouts  12.1 us (21%)
  starting transfers between devices  8.8 us (16%)
  between operations  0.72 us (1%)
    pallas_call x1, Pallas kernels, transform(): pl.pallas_call(functools.partial(transform_kernel, sizes, pair_length), o...  21.5 us
    pallas_call x1, Pallas kernels, interpolate(): pl.pallas_call(functools.partial(interp_kernel, half_rows, pair_length),...  13.1 us
    unnamed x12, local copies, waits for them, and re-layouts  8.49 us
    ppermute x1, starting transfers between devices, on_device(): before = lax.ppermute(own[pairs - 2:], axes, up)  6.88 us
    ppermute x1, starting transfers between devices, on_device(): after = lax.ppermute(own[:2], axes, down)  1.92 us
    dynamic_slice x1, local copies, waits for them, and re-layouts, on_device(): waves = lax.dynamic_slice_in_dim(wave_slot, device * slots, slots)  1.33 us
  transfers between devices with their start and end apart: 2, of which 0 were waited for; matrix products, arithmetic and copies ran while one was open for 11% of the time, Pallas kernels for 0%

profile of v2, /device:TPU:1, one launch (start us, length us, event | category | flops | bytes accessed | tf_op | source)
XLA Modules:
  0.0 56.3 jit_solution(4958516005871664450)
XLA Ops:
  0.6 1.2 %copy.14 = bf16[4,4,5,2596]{3,1,0,2:T(4,128)(2,1)S(1)} copy(bf16[4,4,5,2596]{3,1,2,0:T(4,128)(2,1)} %param.7) | data formatting | bytes 830720 | tf_op args[0]
  1.8 0.2 reshape.20
  2.0 0.0 copy-start
  2.0 6.9 %collective-permute-start = (bf16[2,16,2596]{2,1,0:T(8,128)(2,1)S(1)}, bf16[2,16,2596]{2,1,0:T(8,128)(2,1)S(1)}, u32[]{:S(2)}, u32[]{:S(2)}) collective-permute-start(bf16[2,16,2596]{2,1,0:T(8,128)(2,1)S(1)} %get-tuple-element.7), channel_id=1, source_target_pairs={{0,1},{1,2},{2,3},{3,4},{4,5},{5,6},{6,7},{7,8},{8,9},{9,10},{10,1... | collective-permute-start | bytes 498440 | tf_op jit(solution)/shard_map/ppermute | solution.py:482
  8.9 1.9 %collective-permute-start.1 = (bf16[2,16,2596]{2,1,0:T(8,128)(2,1)S(1)}, bf16[2,16,2596]{2,1,0:T(8,128)(2,1)S(1)}, u32[]{:S(2)}, u32[]{:S(2)}) collective-permute-start(bf16[2,16,2596]{2,1,0:T(8,128)(2,1)S(1)} %get-tuple-element.6), channel_id=1, source_target_pairs={{1,0},{2,1},{3,2},{4,3},{5,4},{6,5},{7,6},{8,7},{9,8},{10,9},{11,1... | collective-permute-start | bytes 498440 | tf_op jit(solution)/shard_map/ppermute | solution.py:483
  10.9 1.7 %copy.15.lon_ref = s32[4,5,2596]{2,1,0:T(8,128)} copy(s32[4,5,2596]{2,0,1:T(4,128)} %param.9) | data formatting | bytes 415360 | tf_op args[2]
  12.6 1.7 %copy.16.lonf_ref = f32[4,5,2596]{2,1,0:T(8,128)} copy(f32[4,5,2596]{2,0,1:T(4,128)} %param.10) | data formatting | bytes 415360 | tf_op args[3]
  14.3 0.9 %reshape.22 = s32[128,5]{1,0:T(8,128)S(1)} reshape(s32[640]{0:T(1024)} %param.12) | data formatting | bytes 5120 | tf_op jit(solution)/shard_map/reshape | solution.py:484
  15.1 0.1 copy.17
  15.2 0.6 %copy.22 = s32[1,1,5,128]{3,1,2,0:T(1,128)} copy(s32[1,1,5,128]{3,2,1,0:T(8,128)S(1)} %bitcast.17) | data formatting | bytes 5120
  15.8 1.3 %dynamic_slice.3.waves_ref = s32[5]{0:T(128)} dynamic-slice(s32[640]{0:T(1024)} %param.12, s32[]{:T(128)S(6)} %select_n.3), dynamic_slice_sizes={5} | dynamic-slice | bytes 44 | tf_op jit(solution)/shard_map/dynamic_slice | solution.py:485
  17.2 0.0 collective-permute-done.before_ref
  17.2 0.0 copy-start.1
  17.2 0.0 collective-permute-done.1.after_ref
  17.2 0.0 copy-start.2
  17.2 0.0 copy-done
  17.2 0.6 %copy-done.1 = bf16[2,16,2596]{2,1,0:T(8,128)(2,1)} copy-done((bf16[2,16,2596]{2,1,0:T(8,128)(2,1)}, bf16[2,16,2596]{2,1,0:T(8,128)(2,1)S(1)}, u32[]{:S(2)}) %copy-start.1) | copy-done | bytes 166168
  17.8 0.1 copy-done.2
  17.9 13.1 %interp.1.y_ref = bf16[5,16,2688]{2,1,0:T(8,128)(2,1)} custom-call(s32[1]{0:T(128)} %bitcast.first_ref, bf16[2,16,2596]{2,1,0:T(8,128)(2,1)} %copy-done.1, bf16[5,16,2596]{2,1,0:T(8,128)(2,1)} %bitcast.15, bf16[2,16,2596]{2,1,0:T(8,128)(2,1)} %copy-done.2, s32[5,2596]{1,0:T(8,128)} %row_ref.1, s32[4,5,2596]{2,1,0:T(8,128)} %copy.15.lon_ref, ...), custom_call_target="tpu_custom_call" | custom-call | tf_op jit(solution)/shard_map/interp/pallas_call | solution.py:251
  31.0 1.0 %slice_bitcast_fusion = bf16[16,5,2596]{2,0,1:T(8,128)(2,1)S(1)} fusion(bf16[5,16,2688]{2,1,0:T(8,128)(2,1)} %interp.1.y_ref), kind=kLoop, calls=%fused_computation | loop fusion | bytes 830720 | tf_op jit(solution)/shard_map/transpose | solution.py:488
  32.1 0.1 reshape.21
  32.2 0.9 %copy.18 = bf16[4,4,5,2596]{3,1,2,0:T(4,128)(2,1)} copy(bf16[4,4,5,2596]{3,1,0,2:T(4,128)(2,1)S(1)} %reshape.21) | data formatting | bytes 830720
  33.1 21.5 %transform.1 = f32[16,5,640]{2,1,0:T(8,128)} custom-call(bf16[5,16,2688]{2,1,0:T(8,128)(2,1)} %interp.1.y_ref, s32[1,640]{1,0:T(1,128)} %bitcast.18, s32[5]{0:T(128)} %dynamic_slice.3.waves_ref, bf16[5,2,320,640]{3,2,1,0:T(8,128)(2,1)} %legendre_hbm.1), custom_call_target="tpu_custom_call" | custom-call | tf_op jit(solution)/shard_map/transform/pallas_call | solution.py:444
  54.6 1.7 %copy.19 = f32[16,5,640]{2,0,1:T(8,128)} copy(f32[16,5,640]{2,1,0:T(8,128)} %transform.1) | data formatting | bytes 409600
  (1 shorter events, 0.0 us)
Async XLA Ops:
  2.0 15.2 %copy-start = (bf16[16,5,2596]{2,0,1:T(8,128)(2,1)}, bf16[16,5,2596]{2,0,1:T(8,128)(2,1)S(1)}, u32[]{:S(2)}) copy-start(bf16[16,5,2596]{2,0,1:T(8,128)(2,1)S(1)} %reshape.20) | copy-start | bytes 1246084
  2.0 15.1 %collective-permute-start = (bf16[2,16,2596]{2,1,0:T(8,128)(2,1)S(1)}, bf16[2,16,2596]{2,1,0:T(8,128)(2,1)S(1)}, u32[]{:S(2)}, u32[]{:S(2)}) collective-permute-start(bf16[2,16,2596]{2,1,0:T(8,128)(2,1)S(1)} %get-tuple-element.7), channel_id=1, source_target_pairs={{0,1},{1,2},{2,3},{3,4},{4,5},{5,6},{6,7},{7,8},{8,9},{9,10},{10,1... | collective-permute-start | bytes 498440 | tf_op jit(solution)/shard_map/ppermute | solution.py:482
  8.9 8.2 %collective-permute-start.1 = (bf16[2,16,2596]{2,1,0:T(8,128)(2,1)S(1)}, bf16[2,16,2596]{2,1,0:T(8,128)(2,1)S(1)}, u32[]{:S(2)}, u32[]{:S(2)}) collective-permute-start(bf16[2,16,2596]{2,1,0:T(8,128)(2,1)S(1)} %get-tuple-element.6), channel_id=1, source_target_pairs={{1,0},{2,1},{3,2},{4,3},{5,4},{6,5},{7,6},{8,7},{9,8},{10,9},{11,1... | collective-permute-start | bytes 498440 | tf_op jit(solution)/shard_map/ppermute | solution.py:483
  17.2 0.7 %copy-start.1 = (bf16[2,16,2596]{2,1,0:T(8,128)(2,1)}, bf16[2,16,2596]{2,1,0:T(8,128)(2,1)S(1)}, u32[]{:S(2)}) copy-start(bf16[2,16,2596]{2,1,0:T(8,128)(2,1)S(1)} %collective-permute-done.before_ref) | copy-start | bytes 498436
  17.2 0.7 %copy-start.2 = (bf16[2,16,2596]{2,1,0:T(8,128)(2,1)}, bf16[2,16,2596]{2,1,0:T(8,128)(2,1)S(1)}, u32[]{:S(2)}) copy-start(bf16[2,16,2596]{2,1,0:T(8,128)(2,1)S(1)} %collective-permute-done.1.after_ref) | copy-start | bytes 498436

commit v3 on v2

--- a/solution.py
+++ b/solution.py
@@ -35,10 +35,10 @@
 
 
 def interp_kernel(half_rows, pair_length, first_ref, before_ref, own_ref, after_ref,
-                  row_ref, lon_ref, lonf_ref, latf_ref, out_ref,
-                  place_t, ext_s, plan_s, row_p, lon_p, lonf_p, latf_p):
-    pairs = own_ref.shape[0]
-    fields = own_ref.shape[1]
+                  row_ref, lon_ref, lonf_ref, latf_ref, out_ref, head_ref,
+                  place_t, ext_s, plan_s, y_s):
+    groups, pairs, levels, _ = own_ref.shape
+    fields = groups * levels
     near = pairs + 4
     tiles = pl.cdiv(pair_length, LANES)
     first = first_ref[0]
@@ -46,19 +46,11 @@
     ext_s[:, :, pl.ds(0, LANES)] = jnp.zeros((2 * near, fields, LANES), jnp.bfloat16)
     ext_s[:, :, pl.ds(tiles * LANES, EW - tiles * LANES)] = jnp.zeros((2 * near, fields, EW - tiles * LANES), jnp.bfloat16)
     for j in range(near):
-        src = before_ref[j] if j < 2 else (own_ref[j - 2] if j < 2 + pairs else after_ref[j - 2 - pairs])
-        ext_s[2 * j, :, pl.ds(LANES, pair_length)] = src
-        ext_s[2 * j + 1, :, pl.ds(LANES, pair_length)] = src
-
-    row_p[...] = jnp.zeros_like(row_p)
-    lon_p[...] = jnp.zeros_like(lon_p)
-    lonf_p[...] = jnp.zeros_like(lonf_p)
-    latf_p[...] = jnp.zeros_like(latf_p)
-    row_p[pl.ds(0, pairs), pl.ds(0, pair_length)] = row_ref[...]
-    latf_p[pl.ds(0, pairs), pl.ds(0, pair_length)] = latf_ref[...]
-    for r in range(4):
-        lon_p[r, pl.ds(0, pairs), pl.ds(0, pair_length)] = lon_ref[r]
-        lonf_p[r, pl.ds(0, pairs), pl.ds(0, pair_length)] = lonf_ref[r]
+        ref, at = (before_ref, j) if j < 2 else ((own_ref, j - 2) if j < 2 + pairs else (after_ref, j - 2 - pairs))
+        for f in range(groups):
+            src = ref[f, at]
+            for copy in range(2):
+                ext_s[2 * j + copy, pl.ds(levels * f, levels), pl.ds(LANES, pair_length)] = src
 
     lane = lax.broadcasted_iota(jnp.int32, (fields, LANES), 1)
 
@@ -90,50 +82,62 @@
     sub8 = lax.broadcasted_iota(jnp.int32, (8, LANES), 0)
     lane8 = lax.broadcasted_iota(jnp.int32, (8, LANES), 1)
 
-    def weigh(tile, fits):
+    def weigh(tile, fits, width=LANES):
         at = pl.ds(pl.multiple_of(tile * LANES, LANES), LANES)
+        some = pl.ds(pl.multiple_of(tile * LANES, LANES), width)
         col = tile * LANES + lane8
-        pair = first + sub8
-        northern = pair < half_rows // 2
-        len0, len1 = half_lengths(pair)
-        second = col >= len0
-        inner = jnp.where(northern, pair, half_rows - 1 - pair)
-        number = jnp.where(second, half_rows // 2 + 1 + inner, half_rows // 2 - inner)
-        g = jnp.where(northern, number - 1, 2 * half_rows - number)
-        base = jnp.clip(g - 2, 0, 2 * half_rows - 4)
-        later = (row_p[:, at] - base) > 0
-        k0 = jnp.where(second, jnp.maximum(tile * LANES - len0, 0), tile * LANES)
-        base_k = k0 - MARGIN
-        inside = (col < pair_length) & (sub8 < pairs)
-        latw = cubic(latf_p[:, at])
-        lons = [lon_p[r, :, at] for r in range(4)]
-        lonfs = [lonf_p[r, :, at] for r in range(4)]
-        zero = jnp.zeros((8, LANES), jnp.float32)
-        for d in range(5):
-            hi, lo = min(d, 3), max(d - 1, 0)
-            lon = jnp.where(later, lons[lo], lons[hi])
-            frac = jnp.where(later, lonfs[lo], lonfs[hi])
-            lat = jnp.where(later, latw[lo] if d >= 1 else zero, latw[hi] if d <= 3 else zero)
-            _, begin, length = row_place(jnp.minimum(base + d, 2 * half_rows - 1), half_rows)
+        inside = col < pair_length
+
+        def wide(x):
+            if width < LANES:
+                x = jnp.concatenate([x, jnp.zeros((x.shape[0], LANES - width), x.dtype)], axis=1)
+            return x
+
+        for q in range(pairs):
+            pair = first + q
+            northern = pair < half_rows // 2
+            len0, _ = half_lengths(pair)
+            second = col >= len0
+            inner = jnp.where(northern, pair, half_rows - 1 - pair)
+
+            def base_of(number):
+                return jnp.clip(jnp.where(northern, number - 1, 2 * half_rows - number) - 2, 0, 2 * half_rows - 4)
+
+            base = jnp.where(second, base_of(half_rows // 2 + 1 + inner), base_of(half_rows // 2 - inner))
+            later = jnp.broadcast_to(wide(row_ref[pl.ds(q, 1), some]), (8, LANES)) > base
+            base_k = jnp.where(second, jnp.maximum(tile * LANES - len0, 0), tile * LANES) - MARGIN
+            lon = wide(lon_ref[q, :, some])
+            lon = jnp.concatenate([lon, lon], axis=0)
+            lon = jnp.where(later, pltpu.roll(lon, 1, 0), lon)
+            frac = wide(lonf_ref[q, :, some])
+            frac = jnp.concatenate([frac, frac], axis=0)
+            frac = jnp.where(later, pltpu.roll(frac, 1, 0), frac)
+            latw = cubic(jnp.broadcast_to(wide(latf_ref[pl.ds(q, 1), some]), (8, LANES)))
+            r = jnp.where(later, sub8 - 1, sub8)
+            lat = jnp.zeros((8, LANES), jnp.float32)
+            for i in range(4):
+                lat = jnp.where(inside & (r == i), latw[i], lat)
+            _, begin, length = row_place(jnp.minimum(base + sub8, 2 * half_rows - 1), half_rows)
             rel = lon - 1 - base_k
             rel = jnp.where(rel < 0, rel + length, jnp.where(rel >= length, rel - length, rel))
             short = length <= WIN - 4
             rel = jnp.where(short, lon, rel)
-            bad = inside & (lat != 0.0) & ((rel < 0) | (rel > WIN - 4))
+            bad = (lat != 0.0) & ((rel < 0) | (rel > WIN - 4))
             fits = jnp.maximum(fits, bad.astype(jnp.int32))
             place = ((begin + jnp.where(short, -1, base_k) + LANES) & 127) + rel
             block = (place >> 4) & 15
-            lat = jnp.where(inside, lat, 0.0)
             ws = cubic(frac)
             for o in range(4):
-                plan_s[d * ROWS + o, :, at] = lat * ws[o]
-                plan_s[d * ROWS + 4 + o, :, at] = ((place + o) & 15).astype(jnp.float32)
-            plan_s[d * ROWS + 8, :, at] = block.astype(jnp.float32)
-            plan_s[d * ROWS + 9, :, at] = ((block + 1) & 15).astype(jnp.float32)
-            plan_s[d * ROWS + 10, :, at] = (lon + begin).astype(jnp.float32)
+                plan_s[q * ROWS + o, :, at] = lat * ws[o]
+                plan_s[q * ROWS + 4 + o, :, at] = ((place + o) & 15).astype(jnp.float32)
+            plan_s[q * ROWS + 8, :, at] = block.astype(jnp.float32)
+            plan_s[q * ROWS + 9, :, at] = ((block + 1) & 15).astype(jnp.float32)
+            plan_s[q * ROWS + 10, :, at] = (lon + begin).astype(jnp.float32)
         return fits
 
-    worst = lax.fori_loop(0, tiles, weigh, jnp.zeros((8, LANES), jnp.int32))
+    worst = lax.fori_loop(0, pair_length // LANES, weigh, jnp.zeros((8, LANES), jnp.int32))
+    if pair_length % LANES:
+        worst = weigh(tiles - 1, worst, pair_length % LANES)
     local = jnp.max(worst) == 0
 
     node = lax.broadcasted_iota(jnp.int32, (16, LANES), 0).astype(jnp.float32).astype(jnp.bfloat16)
@@ -147,7 +151,7 @@
         return [jnp.where(block == jnp.bfloat16(a), v, zero16) for a in range(WIN // 16)]
 
     def plan(d, i, q, at):
-        return jnp.broadcast_to(plan_s[d * ROWS + i, pl.ds(q, 1), at], (16, LANES))
+        return jnp.broadcast_to(plan_s[q * ROWS + i, pl.ds(d, 1), at], (16, LANES))
 
     def packed(x):
         return x.astype(jnp.bfloat16)
@@ -189,7 +193,9 @@
 
     def finish(q, u, straddle, tile, total, carry):
         total = total + jnp.where(u == straddle + 1, carry, 0.0)
-        out_ref[q, :, pl.ds(pl.multiple_of(tile * LANES, LANES), LANES)] = total.astype(jnp.bfloat16)
+        at = pl.ds(pl.multiple_of(tile * LANES, LANES), LANES)
+        y_s[q, :, at] = total.astype(jnp.bfloat16)
+        head_ref[q, :, at] = total[:head_ref.shape[1]].astype(jnp.bfloat16)
         return total
 
     @pl.when(local)
@@ -241,26 +247,30 @@
         lax.fori_loop(0, tiles + 1, lambda u, carry: tuple(unit(q, u, carry[q]) for q in range(pairs)),
                       (jnp.zeros((fields, LANES), jnp.float32),) * pairs)
 
-
-def interpolate(first, before, own, after, dep_row, dep_lon, lon_frac, lat_frac, half_rows):
-    pairs, fields, pair_length = own.shape
-    tiles = pl.cdiv(pair_length, LANES)
-    padded = tiles * LANES
+    for f in range(groups):
+        for q in range(pairs):
+            out_ref[f, q] = y_s[q, pl.ds(levels * f, levels), pl.ds(0, pair_length)]
+
+
+def interpolate(first, before, own, after, dep_row, dep_lon, lon_frac, lat_frac, half_rows, spectral_fields):
+    groups, pairs, levels, pair_length = own.shape
+    fields = groups * levels
+    padded = pl.cdiv(pair_length, LANES) * LANES
     near = pairs + 4
     vm = pl.BlockSpec(memory_space=pltpu.VMEM)
     return pl.pallas_call(
         functools.partial(interp_kernel, half_rows, pair_length),
-        out_shape=jax.ShapeDtypeStruct((pairs, fields, padded), jnp.bfloat16),
+        out_shape=(
+            jax.ShapeDtypeStruct(own.shape, jnp.bfloat16),
+            jax.ShapeDtypeStruct((pairs, spectral_fields, padded), jnp.bfloat16),
+        ),
         in_specs=[pl.BlockSpec(memory_space=pltpu.SMEM)] + [vm] * 7,
-        out_specs=vm,
+        out_specs=(vm, vm),
         scratch_shapes=[
             pltpu.SMEM((30 * pairs,), jnp.int32),
             pltpu.VMEM((2 * near, fields, EW), jnp.bfloat16),
-            pltpu.VMEM((5 * ROWS, 8, padded), jnp.float32),
-            pltpu.VMEM((8, padded), jnp.int32),
-            pltpu.VMEM((4, 8, padded), jnp.int32),
-            pltpu.VMEM((4, 8, padded), jnp.float32),
-            pltpu.VMEM((8, padded), jnp.float32),
+            pltpu.VMEM((pairs * ROWS, 8, padded), jnp.float32),
+            pltpu.VMEM((pairs, fields, padded), jnp.bfloat16),
         ],
         name="interp",
     )(first, before, own, after, dep_row, dep_lon, lon_frac, lat_frac)
@@ -375,10 +385,10 @@
     mix_s[...] = jnp.zeros_like(mix_s)
     for r in range(8):
         for s in range(slots):
-            mix_s[r, pl.ds(s, 16, stride=8), :] = moved[16 * r:16 * r + 16, s * LANES:(s + 1) * LANES]
+            mix_s[r, pl.ds(16 * s, 16), :] = moved[16 * r:16 * r + 16, s * LANES:(s + 1) * LANES]
         if r < slots:
             for e in range(rows - 8):
-                mix_s[r, pl.ds(slots + e, 16, stride=8), :] = moved[16 * (8 + e):16 * (8 + e) + 16, r * LANES:(r + 1) * LANES]
+                mix_s[r, pl.ds(16 * (slots + e), 16), :] = moved[16 * (8 + e):16 * (8 + e) + 16, r * LANES:(r + 1) * LANES]
         stage_s[pl.ds(r, LANES, stride=8), :] = mix_s[r].T
     send_s[...] = stage_s[...].astype(jnp.bfloat16).reshape(send_s.shape)
 
@@ -395,15 +405,9 @@
 
     src = lax.broadcasted_iota(jnp.int32, (slots * LANES, 2 * LANES), 0)
     dst = lax.broadcasted_iota(jnp.int32, (slots * LANES, 2 * LANES), 1)
-    unfold = ((dst & 7) == (src >> 7)) & ((src & 127) == (dst & 127) - (src >> 7) + slots + (dst >> 7))
+    unfold = (((dst & 127) >> 4) == (src >> 7)) & ((src & 127) == 16 * (slots + (dst >> 7)) + (dst & 15))
     unfold = unfold.astype(jnp.float32).astype(jnp.bfloat16)
-    slot_of = (lax.broadcasted_iota(jnp.int32, (half_rows, LANES), 1) & 7).astype(jnp.float32).astype(jnp.bfloat16)
-    sub = lax.broadcasted_iota(jnp.int32, (8, half_rows), 0)
-    j = lax.broadcasted_iota(jnp.int32, (8, half_rows), 1)
-    limit = jnp.zeros((8, half_rows), jnp.int32)
-    for i in range(slots):
-        limit = jnp.where(sub == i, half_rows - waves_ref[i], limit)
-
+    slot_of = (lax.broadcasted_iota(jnp.int32, (half_rows, LANES), 1) >> 4).astype(jnp.float32).astype(jnp.bfloat16)
     rest = pl.ds(0, devices - 1)
     every = pltpu.make_async_remote_copy(
         src_ref=send_s.at[rest], dst_ref=got_s.at[rest], send_sem=send_sem, recv_sem=recv_sem,
@@ -430,9 +434,11 @@
         picked = jnp.concatenate([jnp.where(slot_of == jnp.bfloat16(s), values, zero) for s in range(slots)], axis=0)
         table = jnp.concatenate([legendre_s[s, par] for s in range(slots)], axis=1)
         turn_s[pl.ds(par, half_rows // 2, stride=2), :] = jnp.dot(table, picked, preferred_element_type=jnp.float32)
-    z = turn_s[...].T.reshape(16, 8, half_rows)
-    z = jnp.where((j < limit)[None], z, 0.0)
-    out_ref[...] = z[:, :slots, :]
+    z = turn_s[...].T
+    degree = lax.broadcasted_iota(jnp.int32, (16, half_rows), 1)
+    for s in range(slots):
+        limit = half_rows - waves_ref[me * slots + s]
+        out_ref[s] = jnp.where(degree < limit, z[16 * s:16 * s + 16], 0.0)
 
 
 def transform(y, order, waves, legendre, half_rows, pair_length, sizes):
@@ -443,7 +449,7 @@
     f32, b16 = jnp.float32, jnp.bfloat16
     return pl.pallas_call(
         functools.partial(transform_kernel, sizes, pair_length),
-        out_shape=jax.ShapeDtypeStruct((16, slots, half_rows), f32),
+        out_shape=jax.ShapeDtypeStruct((slots, 16, half_rows), f32),
         in_specs=[vm, vm, pl.BlockSpec(memory_space=pltpu.SMEM), pl.BlockSpec(memory_space=pl.ANY)],
         out_specs=vm,
         scratch_shapes=[
@@ -476,17 +482,16 @@
     devices = sizes[0] * sizes[1]
     device = lax.axis_index(axes)
     first = (device * pairs).astype(jnp.int32).reshape(1)
-    own = jnp.transpose(grid.reshape(fields * levels, pairs, pair_length), (1, 0, 2))
+    own = jnp.transpose(grid, (0, 2, 1, 3))
     up = [(i, i + 1) for i in range(devices - 1)]
     down = [(j, i) for i, j in up]
-    before = lax.ppermute(own[pairs - 2:], axes, up)
-    after = lax.ppermute(own[:2], axes, down)
+    before = lax.ppermute(own[:, pairs - 2:], axes, up)
+    after = lax.ppermute(own[:, :2], axes, down)
     order = jnp.transpose(wave_slot.reshape(devices, slots)).reshape(1, half_rows)
-    waves = lax.dynamic_slice_in_dim(wave_slot, device * slots, slots)
-    y = interpolate(first, before, own, after, dep_row, dep_lon, lon_frac, lat_frac, half_rows)
-    result = transform(y, order, waves, legendre, half_rows, pair_length, sizes)
-    interpolated = jnp.transpose(y[:, :, :pair_length], (1, 0, 2)).reshape(grid.shape)
-    return (interpolated, result)
+    out, head = interpolate(first, before, own, after, dep_row, jnp.transpose(dep_lon, (1, 0, 2)),
+                            jnp.transpose(lon_frac, (1, 0, 2)), lat_frac, half_rows, 2 * levels)
+    result = transform(head, order, wave_slot, legendre, half_rows, pair_length, sizes)
+    return (jnp.transpose(out, (0, 2, 1, 3)), jnp.transpose(result, (1, 0, 2)))
 
 
 def solution(mesh):

time: 56.7 us -> 53 us (0.935)
  local copies, waits for them, and re-layouts: 12.1 us -> 4.98 us
  waiting for transfers between devices: 0.01 us -> 4.73 us
  Pallas kernels: 34.6 us -> 33.5 us
    unnamed x12 -> x6, local copies, waits for them, and re-layouts: 8.49 us -> 2.91 us
    ppermute x2, waiting for transfers between devices: 0.01 us -> 4.73 us  [the longest x1 4.73 us: on_device(): after = lax.ppermute(own[:, :2], axes, down)]
    pallas_call x1, Pallas kernels: 21.5 us -> 19.7 us  [transform(): pl.pallas_call(functools.partial(transform_kernel, sizes, pair_length), o...]
    dynamic_slice x1 -> x0, local copies, waits for them, and re-layouts: 1.33 us -> none  [on_device(): waves = lax.dynamic_slice_in_dim(wave_slot, device * slots, slots)]
    slice x1, local copies, waits for them, and re-layouts: 0.03 us -> 1.13 us  [on_device(): after = lax.ppermute(own[:, :2], axes, down)]
    transpose x1 -> x0, local copies, waits for them, and re-layouts: 1.04 us -> none  [on_device(): jnp.transpose(y[:, :, :pair_length], (1, 0, 2)).reshape(grid.shape)]
    pallas_call x1, Pallas kernels: 13.1 us -> 13.8 us  [interpolate(): pl.pallas_call(functools.partial(interp_kernel, half_rows, pair_length),...]
  transfers between devices with their start and end apart: 2 -> 2, of which waited for: 0 -> 1; matrix products, arithmetic and copies ran while one was open for 11% -> 3% of each run, Pallas kernels for 0% -> 0%
where the time goes in v3:
time: 53 us; the launch traced here: 52.7 us
  Pallas kernels  33.5 us (63%)
  starting transfers between devices  8.8 us (17%)
  local copies, waits for them, and re-layouts  4.98 us (9%)
  waiting for transfers between devices  4.73 us (9%)
  between operations  0.67 us (1%)
    pallas_call x1, Pallas kernels, transform(): pl.pallas_call(functools.partial(transform_kernel, sizes, pair_length), o...  19.7 us
    pallas_call x1, Pallas kernels, interpolate(): pl.pallas_call(functools.partial(interp_kernel, half_rows, pair_length),...  13.8 us
    ppermute x1, starting transfers between devices, on_device(): before = lax.ppermute(own[:, pairs - 2:], axes, up)  6.88 us
    ppermute x1, waiting for transfers between devices, on_device(): after = lax.ppermute(own[:, :2], axes, down)  4.73 us
    unnamed x6, local copies, waits for them, and re-layouts  2.91 us
    ppermute x1, starting transfers between devices, on_device(): after = lax.ppermute(own[:, :2], axes, down)  1.92 us
    slice x1, local copies, waits for them, and re-layouts, on_device(): after = lax.ppermute(own[:, :2], axes, down)  1.13 us
  transfers between devices with their start and end apart: 2, of which 1 were waited for; matrix products, arithmetic and copies ran while one was open for 3% of the time, Pallas kernels for 0%

profile of v3, /device:TPU:1, one launch (start us, length us, event | category | flops | bytes accessed | tf_op | source)
XLA Modules:
  0.0 52.7 jit_solution(9059084952252037541)
XLA Ops:
  0.6 1.1 %fusion = (bf16[4,2,4,2596]{3,2,1,0:T(4,128)(2,1)S(1)}, bf16[4,2,4,2596]{3,2,1,0:T(4,128)(2,1)S(1)}) fusion(bf16[4,5,4,2596]{3,2,1,0:T(4,128)(2,1)} %bitcast.12), kind=kLoop, calls=%fused_computation.1 | loop fusion | bytes 664576 | tf_op jit(solution)/shard_map/slice | solution.py:489
  1.8 6.9 %collective-permute-start = (bf16[4,2,4,2596]{3,2,1,0:T(4,128)(2,1)S(1)}, bf16[4,2,4,2596]{3,2,1,0:T(4,128)(2,1)S(1)}, u32[]{:S(2)}, u32[]{:S(2)}) collective-permute-start(bf16[4,2,4,2596]{3,2,1,0:T(4,128)(2,1)S(1)} %get-tuple-element.7), channel_id=1, source_target_pairs={{0,1},{1,2},{2,3},{3,4},{4,5},{5,6},{6,7},{7,8},{8,9},{9,10},{10,1... | collective-permute-start | bytes 498440 | tf_op jit(solution)/shard_map/ppermute | solution.py:488
  8.7 1.9 %collective-permute-start.1 = (bf16[4,2,4,2596]{3,2,1,0:T(4,128)(2,1)S(1)}, bf16[4,2,4,2596]{3,2,1,0:T(4,128)(2,1)S(1)}, u32[]{:S(2)}, u32[]{:S(2)}) collective-permute-start(bf16[4,2,4,2596]{3,2,1,0:T(4,128)(2,1)S(1)} %get-tuple-element.6), channel_id=1, source_target_pairs={{1,0},{2,1},{3,2},{4,3},{5,4},{6,5},{7,6},{8,7},{9,8},{10,9},{11,1... | collective-permute-start | bytes 498440 | tf_op jit(solution)/shard_map/ppermute | solution.py:489
  10.6 0.9 %reshape.14 = s32[128,5]{1,0:T(8,128)S(1)} reshape(s32[640]{0:T(1024)} %waves_ref.1) | data formatting | bytes 5120 | tf_op jit(solution)/shard_map/reshape | solution.py:490
  11.5 0.1 copy.9
  11.5 0.6 %copy.12 = s32[1,1,5,128]{3,1,2,0:T(1,128)} copy(s32[1,1,5,128]{3,2,1,0:T(8,128)S(1)} %bitcast.18) | data formatting | bytes 5120
  12.1 0.0 collective-permute-done.before_ref
  12.1 0.0 copy-start
  12.2 4.7 %collective-permute-done.1.after_ref = bf16[4,2,4,2596]{3,2,1,0:T(4,128)(2,1)S(1)} collective-permute-done((bf16[4,2,4,2596]{3,2,1,0:T(4,128)(2,1)S(1)}, bf16[4,2,4,2596]{3,2,1,0:T(4,128)(2,1)S(1)}, u32[]{:S(2)}, u32[]{:S(2)}) %collective-permute-start.1) | collective-permute-done | bytes 166176 | tf_op jit(solution)/shard_map/ppermute | solution.py:489
  16.9 0.0 copy-start.1
  16.9 0.0 copy-done
  16.9 0.7 %copy-done.1 = bf16[4,2,4,2596]{3,2,1,0:T(4,128)(2,1)} copy-done((bf16[4,2,4,2596]{3,2,1,0:T(4,128)(2,1)}, bf16[4,2,4,2596]{3,2,1,0:T(4,128)(2,1)S(1)}, u32[]{:S(2)}) %copy-start.1) | copy-done | bytes 166168
  17.6 13.8 %interp.1 = (bf16[4,5,4,2596]{3,2,1,0:T(4,128)(2,1)}, bf16[5,8,2688]{2,1,0:T(8,128)(2,1)}) custom-call(s32[1]{0:T(128)} %bitcast.first_ref, bf16[4,2,4,2596]{3,2,1,0:T(4,128)(2,1)} %copy-done, bf16[4,5,4,2596]{3,2,1,0:T(4,128)(2,1)} %bitcast.13, bf16[4,2,4,2596]{3,2,1,0:T(4,128)(2,1)} %copy-done.1, s32[5,2596]{1,0:T(8,128)} %row_ref.1, ...), custom_call_target="tpu_custom_call" | custom-call | tf_op jit(solution)/shard_map/interp/pallas_call | solution.py:261
  31.4 19.7 %transform.1 = f32[5,16,640]{2,1,0:T(8,128)} custom-call(bf16[5,8,2688]{2,1,0:T(8,128)(2,1)} %get-tuple-element.5.y_ref, s32[1,640]{1,0:T(1,128)} %bitcast.19, s32[640]{0:T(1024)} %waves_ref.1, bf16[5,2,320,640]{3,2,1,0:T(8,128)(2,1)} %legendre_hbm.1), custom_call_target="tpu_custom_call" | custom-call | tf_op jit(solution)/shard_map/transform/pallas_call | solution.py:450
  51.1 1.6 %copy.14 = f32[16,5,640]{2,0,1:T(8,128)} copy(f32[16,5,640]{2,0,1:T(8,128)} %bitcast.14) | data formatting | bytes 409600
Async XLA Ops:
  1.8 10.4 %collective-permute-start = (bf16[4,2,4,2596]{3,2,1,0:T(4,128)(2,1)S(1)}, bf16[4,2,4,2596]{3,2,1,0:T(4,128)(2,1)S(1)}, u32[]{:S(2)}, u32[]{:S(2)}) collective-permute-start(bf16[4,2,4,2596]{3,2,1,0:T(4,128)(2,1)S(1)} %get-tuple-element.7), channel_id=1, source_target_pairs={{0,1},{1,2},{2,3},{3,4},{4,5},{5,6},{6,7},{7,8},{8,9},{9,10},{10,1... | collective-permute-start | bytes 498440 | tf_op jit(solution)/shard_map/ppermute | solution.py:488
  8.7 8.2 %collective-permute-start.1 = (bf16[4,2,4,2596]{3,2,1,0:T(4,128)(2,1)S(1)}, bf16[4,2,4,2596]{3,2,1,0:T(4,128)(2,1)S(1)}, u32[]{:S(2)}, u32[]{:S(2)}) collective-permute-start(bf16[4,2,4,2596]{3,2,1,0:T(4,128)(2,1)S(1)} %get-tuple-element.6), channel_id=1, source_target_pairs={{1,0},{2,1},{3,2},{4,3},{5,4},{6,5},{7,6},{8,7},{9,8},{10,9},{11,1... | collective-permute-start | bytes 498440 | tf_op jit(solution)/shard_map/ppermute | solution.py:489
  12.1 4.7 %copy-start = (bf16[4,2,4,2596]{3,2,1,0:T(4,128)(2,1)}, bf16[4,2,4,2596]{3,2,1,0:T(4,128)(2,1)S(1)}, u32[]{:S(2)}) copy-start(bf16[4,2,4,2596]{3,2,1,0:T(4,128)(2,1)S(1)} %collective-permute-done.before_ref) | copy-start | bytes 498436
  16.9 0.7 %copy-start.1 = (bf16[4,2,4,2596]{3,2,1,0:T(4,128)(2,1)}, bf16[4,2,4,2596]{3,2,1,0:T(4,128)(2,1)S(1)}, u32[]{:S(2)}) copy-start(bf16[4,2,4,2596]{3,2,1,0:T(4,128)(2,1)S(1)} %collective-permute-done.1.after_ref) | copy-start | bytes 498436

commit v4 on v3

--- a/solution.py
+++ b/solution.py
@@ -34,29 +34,33 @@
     )
 
 
-def interp_kernel(half_rows, pair_length, first_ref, before_ref, own_ref, after_ref,
-                  row_ref, lon_ref, lonf_ref, latf_ref, out_ref, head_ref,
-                  place_t, ext_s, plan_s, y_s):
-    groups, pairs, levels, _ = own_ref.shape
+class Stencil:
+    pass
+
+
+def stencil_steps(half_rows, pair_length, first, sources, row_ref, lon_ref, lonf_ref, latf_ref, place_t, ext_s, plan_s, y_s, head_s):
+    groups, pairs, levels, _ = sources[1].shape
     fields = groups * levels
     near = pairs + 4
     tiles = pl.cdiv(pair_length, LANES)
-    first = first_ref[0]
-
-    ext_s[:, :, pl.ds(0, LANES)] = jnp.zeros((2 * near, fields, LANES), jnp.bfloat16)
-    ext_s[:, :, pl.ds(tiles * LANES, EW - tiles * LANES)] = jnp.zeros((2 * near, fields, EW - tiles * LANES), jnp.bfloat16)
-    for j in range(near):
-        ref, at = (before_ref, j) if j < 2 else ((own_ref, j - 2) if j < 2 + pairs else (after_ref, j - 2 - pairs))
+    steps = Stencil()
+
+    lane = lax.broadcasted_iota(jnp.int32, (fields, LANES), 1)
+
+    def half_lengths(pair):
+        inner = jnp.where(pair < half_rows // 2, pair, half_rows - 1 - pair)
+        return 16 + 4 * (half_rows // 2 - inner), 16 + 4 * (half_rows // 2 + 1 + inner)
+
+    def clear():
+        ext_s[:, :, pl.ds(0, LANES)] = jnp.zeros((2 * near, fields, LANES), jnp.bfloat16)
+        ext_s[:, :, pl.ds(tiles * LANES, EW - tiles * LANES)] = jnp.zeros((2 * near, fields, EW - tiles * LANES), jnp.bfloat16)
+
+    def fill(j):
+        ref, at = (sources[0], j) if j < 2 else ((sources[1], j - 2) if j < 2 + pairs else (sources[2], j - 2 - pairs))
         for f in range(groups):
             src = ref[f, at]
             for copy in range(2):
                 ext_s[2 * j + copy, pl.ds(levels * f, levels), pl.ds(LANES, pair_length)] = src
-
-    lane = lax.broadcasted_iota(jnp.int32, (fields, LANES), 1)
-
-    def half_lengths(pair):
-        inner = jnp.where(pair < half_rows // 2, pair, half_rows - 1 - pair)
-        return 16 + 4 * (half_rows // 2 - inner), 16 + 4 * (half_rows // 2 + 1 + inner)
 
     def wrap(copy, tile, shift, low, edge):
         at = pl.ds(pl.multiple_of(tile * LANES, LANES), LANES)
@@ -67,7 +71,7 @@
         beyond = spot < edge if low else spot >= edge
         return copy, at, jnp.where(beyond, moved, ext_s[copy, :, at].astype(jnp.float32)).astype(jnp.bfloat16)
 
-    for j in range(near):
+    def close(j):
         len0, len1 = half_lengths(first + j - 2)
         wraps = []
         for half in range(2):
@@ -135,10 +139,11 @@
             plan_s[q * ROWS + 10, :, at] = (lon + begin).astype(jnp.float32)
         return fits
 
-    worst = lax.fori_loop(0, pair_length // LANES, weigh, jnp.zeros((8, LANES), jnp.int32))
-    if pair_length % LANES:
-        worst = weigh(tiles - 1, worst, pair_length % LANES)
-    local = jnp.max(worst) == 0
+    def weigh_all():
+        worst = lax.fori_loop(0, pair_length // LANES, weigh, jnp.zeros((8, LANES), jnp.int32))
+        if pair_length % LANES:
+            worst = weigh(tiles - 1, worst, pair_length % LANES)
+        return worst
 
     node = lax.broadcasted_iota(jnp.int32, (16, LANES), 0).astype(jnp.float32).astype(jnp.bfloat16)
     zero16 = jnp.zeros((16, LANES), jnp.bfloat16)
@@ -156,22 +161,23 @@
     def packed(x):
         return x.astype(jnp.bfloat16)
 
-    for q in range(pairs):
-        pair = first + q
-        northern = pair < half_rows // 2
-        inner = jnp.where(northern, pair, half_rows - 1 - pair)
-        for half in range(2):
-            number = half_rows // 2 + 1 + inner if half else half_rows // 2 - inner
-            g = jnp.where(northern, number - 1, 2 * half_rows - number)
-            base = jnp.clip(g - 2, 0, 2 * half_rows - 4)
-            for d in range(5):
-                pair_row, begin, length = row_place(jnp.minimum(base + d, 2 * half_rows - 1), half_rows)
-                short = length <= WIN - 4
-                copy = 2 * jnp.clip(pair_row - first + 2, 0, near - 1) + (begin > 0).astype(jnp.int32)
-                at = 3 * ((2 * q + half) * 5 + d)
-                place_t[at] = copy
-                place_t[at + 1] = begin + LANES + jnp.where(short, -1, -MARGIN)
-                place_t[at + 2] = jnp.where(short, 0, 1)
+    def locate():
+        for q in range(pairs):
+            pair = first + q
+            northern = pair < half_rows // 2
+            inner = jnp.where(northern, pair, half_rows - 1 - pair)
+            for half in range(2):
+                number = half_rows // 2 + 1 + inner if half else half_rows // 2 - inner
+                g = jnp.where(northern, number - 1, 2 * half_rows - number)
+                base = jnp.clip(g - 2, 0, 2 * half_rows - 4)
+                for d in range(5):
+                    pair_row, begin, length = row_place(jnp.minimum(base + d, 2 * half_rows - 1), half_rows)
+                    short = length <= WIN - 4
+                    copy = 2 * jnp.clip(pair_row - first + 2, 0, near - 1) + (begin > 0).astype(jnp.int32)
+                    at = 3 * ((2 * q + half) * 5 + d)
+                    place_t[at] = copy
+                    place_t[at + 1] = begin + LANES + jnp.where(short, -1, -MARGIN)
+                    place_t[at + 2] = jnp.where(short, 0, 1)
 
     def unit_scalars(q, u):
         len0, _ = half_lengths(first + q)
@@ -195,11 +201,10 @@
         total = total + jnp.where(u == straddle + 1, carry, 0.0)
         at = pl.ds(pl.multiple_of(tile * LANES, LANES), LANES)
         y_s[q, :, at] = total.astype(jnp.bfloat16)
-        head_ref[q, :, at] = total[:head_ref.shape[1]].astype(jnp.bfloat16)
+        head_s[q, :, at] = total[:head_s.shape[1]].astype(jnp.bfloat16)
         return total
 
-    @pl.when(local)
-    def _():
+    def near_units():
         def unit(q, u, carry):
             len0, straddle, half, tile, base, k0 = unit_scalars(q, u)
             at = pl.ds(pl.multiple_of(tile * LANES, LANES), LANES)
@@ -221,8 +226,7 @@
         lax.fori_loop(0, tiles + 1, lambda u, carry: tuple(unit(q, u, carry[q]) for q in range(pairs)),
                       (jnp.zeros((fields, LANES), jnp.float32),) * pairs)
 
-    @pl.when(jnp.logical_not(local))
-    def _():
+    def any_units():
         def unit(q, u, carry):
             len0, straddle, half, tile, base, _ = unit_scalars(q, u)
             at = pl.ds(pl.multiple_of(tile * LANES, LANES), LANES)
@@ -247,33 +251,142 @@
         lax.fori_loop(0, tiles + 1, lambda u, carry: tuple(unit(q, u, carry[q]) for q in range(pairs)),
                       (jnp.zeros((fields, LANES), jnp.float32),) * pairs)
 
-    for f in range(groups):
-        for q in range(pairs):
-            out_ref[f, q] = y_s[q, pl.ds(levels * f, levels), pl.ds(0, pair_length)]
-
-
-def interpolate(first, before, own, after, dep_row, dep_lon, lon_frac, lat_frac, half_rows, spectral_fields):
-    groups, pairs, levels, pair_length = own.shape
+    def deliver(out_ref):
+        for f in range(groups):
+            for q in range(pairs):
+                out_ref[f, q] = y_s[q, pl.ds(levels * f, levels), pl.ds(0, pair_length)]
+
+    steps.clear, steps.fill, steps.close, steps.weigh_all, steps.locate = clear, fill, close, weigh_all, locate
+    steps.near_units, steps.any_units, steps.deliver, steps.near = near_units, any_units, deliver, near
+    return steps
+
+
+def stencil_scratch(pairs, fields, pair_length):
+    padded = pl.cdiv(pair_length, LANES) * LANES
+    return [
+        pltpu.SMEM((30 * pairs,), jnp.int32),
+        pltpu.VMEM((2 * (pairs + 4), fields, EW), jnp.bfloat16),
+        pltpu.VMEM((pairs * ROWS, 8, padded), jnp.float32),
+        pltpu.VMEM((pairs, fields, padded), jnp.bfloat16),
+    ]
+
+
+def near_kernel(sizes, half_rows, pair_length, grid_hbm, row_hbm, lon_hbm, lonf_hbm, latf_hbm,
+                out_ref, head_ref, far_ref, before_hbm, after_hbm,
+                before_s, own_s, after_s, row_s, lon_s, lonf_s, latf_s, place_t, ext_s, plan_s, y_s,
+                in_sem, send_sem, recv_sem, keep_sem):
+    along, across = sizes
+    devices = along * across
+    pairs = own_s.shape[1]
+    me = lax.axis_index("aa") * across + lax.axis_index("ba")
+    up = lax.rem(me + 1, devices)
+    down = lax.rem(me + devices - 1, devices)
+
+    def where(device):
+        return (device // across, lax.rem(device, across))
+
+    barrier = pltpu.get_barrier_semaphore()
+    for device in (up, down):
+        pl.semaphore_signal(barrier, inc=1, device_id=where(device), device_id_type=pl.DeviceIdType.MESH)
+    loads = [pltpu.make_async_copy(src, dst, in_sem.at[i]) for i, (src, dst) in enumerate((
+        (row_hbm, row_s), (lon_hbm, lon_s), (lonf_hbm, lonf_s), (latf_hbm, latf_s), (grid_hbm, own_s)))]
+    for load in loads:
+        load.start()
+    pl.semaphore_wait(barrier, 2)
+    sends = []
+    for i, (begin, dst, device) in enumerate(((pairs - 2, before_s, up), (0, after_s, down))):
+        sends.append(pltpu.make_async_remote_copy(
+            src_ref=grid_hbm.at[:, pl.ds(begin, 2)], dst_ref=dst, send_sem=send_sem.at[i], recv_sem=recv_sem.at[i],
+            device_id=where(device), device_id_type=pl.DeviceIdType.MESH))
+        sends[-1].start()
+
+    steps = stencil_steps(half_rows, pair_length, me * pairs, (before_s, own_s, after_s), row_s, lon_s, lonf_s, latf_s,
+                          place_t, ext_s, plan_s, y_s, head_ref)
+    steps.locate()
+    steps.clear()
+    for load in loads:
+        load.wait()
+    far_ref[0] = jnp.max(steps.weigh_all())
+    for j in range(2, 2 + pairs):
+        steps.fill(j)
+    for j in range(2, 2 + pairs):
+        steps.close(j)
+    for send in sends:
+        send.wait()
+    keeps = [pltpu.make_async_copy(before_s, before_hbm, keep_sem.at[0]), pltpu.make_async_copy(after_s, after_hbm, keep_sem.at[1])]
+    for keep in keeps:
+        keep.start()
+    for j in (0, 1, 2 + pairs, 3 + pairs):
+        steps.fill(j)
+    for j in (0, 1, 2 + pairs, 3 + pairs):
+        steps.close(j)
+    steps.near_units()
+    steps.deliver(out_ref)
+    for keep in keeps:
+        keep.wait()
+
+
+def far_kernel(half_rows, pair_length, far_ref, first_ref, before_hbm, grid_hbm, after_hbm, row_hbm, lon_hbm, lonf_hbm, latf_hbm,
+               out_in, head_in, out_hbm, head_hbm,
+               before_s, own_s, after_s, row_s, lon_s, lonf_s, latf_s, place_t, ext_s, plan_s, y_s, out_s, head_s, sem):
+    del out_in, head_in
+
+    @pl.when(far_ref[0] > 0)
+    def _():
+        for src, dst in ((before_hbm, before_s), (grid_hbm, own_s), (after_hbm, after_s), (row_hbm, row_s), (lon_hbm, lon_s),
+                         (lonf_hbm, lonf_s), (latf_hbm, latf_s)):
+            copy = pltpu.make_async_copy(src, dst, sem)
+            copy.start()
+            copy.wait()
+        steps = stencil_steps(half_rows, pair_length, first_ref[0], (before_s, own_s, after_s), row_s, lon_s, lonf_s, latf_s,
+                              place_t, ext_s, plan_s, y_s, head_s)
+        steps.locate()
+        steps.clear()
+        steps.weigh_all()
+        for j in range(steps.near):
+            steps.fill(j)
+        for j in range(steps.near):
+            steps.close(j)
+        steps.any_units()
+        steps.deliver(out_s)
+        for src, dst in ((out_s, out_hbm), (head_s, head_hbm)):
+            copy = pltpu.make_async_copy(src, dst, sem)
+            copy.start()
+            copy.wait()
+
+
+def interpolate(first, grid, dep_row, dep_lon, lon_frac, lat_frac, half_rows, spectral_fields, sizes):
+    groups, pairs, levels, pair_length = grid.shape
     fields = groups * levels
     padded = pl.cdiv(pair_length, LANES) * LANES
-    near = pairs + 4
-    vm = pl.BlockSpec(memory_space=pltpu.VMEM)
+    b16, f32, i32 = jnp.bfloat16, jnp.float32, jnp.int32
+    vm, anywhere, scalars = (pl.BlockSpec(memory_space=m) for m in (pltpu.VMEM, pl.ANY, pltpu.SMEM))
+    halo = jax.ShapeDtypeStruct((groups, 2, levels, pair_length), b16)
+    head = jax.ShapeDtypeStruct((pairs, spectral_fields, padded), b16)
+    full = jax.ShapeDtypeStruct(grid.shape, b16)
+    local = [
+        pltpu.VMEM(halo.shape, b16), pltpu.VMEM(grid.shape, b16), pltpu.VMEM(halo.shape, b16),
+        pltpu.VMEM(dep_row.shape, i32), pltpu.VMEM(dep_lon.shape, i32), pltpu.VMEM(lon_frac.shape, f32), pltpu.VMEM(lat_frac.shape, f32),
+    ] + stencil_scratch(pairs, fields, pair_length)
+    out, first_fields, far, before, after = pl.pallas_call(
+        functools.partial(near_kernel, sizes, half_rows, pair_length),
+        out_shape=(full, head, jax.ShapeDtypeStruct((1,), i32), halo, halo),
+        in_specs=[anywhere] * 5,
+        out_specs=(vm, vm, scalars, anywhere, anywhere),
+        scratch_shapes=local + [pltpu.SemaphoreType.DMA((5,)), pltpu.SemaphoreType.DMA((2,)), pltpu.SemaphoreType.DMA((2,)),
+                                pltpu.SemaphoreType.DMA((2,))],
+        compiler_params=pltpu.CompilerParams(collective_id=1, has_side_effects=True),
+        name="near",
+    )(grid, dep_row, dep_lon, lon_frac, lat_frac)
     return pl.pallas_call(
-        functools.partial(interp_kernel, half_rows, pair_length),
-        out_shape=(
-            jax.ShapeDtypeStruct(own.shape, jnp.bfloat16),
-            jax.ShapeDtypeStruct((pairs, spectral_fields, padded), jnp.bfloat16),
-        ),
-        in_specs=[pl.BlockSpec(memory_space=pltpu.SMEM)] + [vm] * 7,
-        out_specs=(vm, vm),
-        scratch_shapes=[
-            pltpu.SMEM((30 * pairs,), jnp.int32),
-            pltpu.VMEM((2 * near, fields, EW), jnp.bfloat16),
-            pltpu.VMEM((pairs * ROWS, 8, padded), jnp.float32),
-            pltpu.VMEM((pairs, fields, padded), jnp.bfloat16),
-        ],
-        name="interp",
-    )(first, before, own, after, dep_row, dep_lon, lon_frac, lat_frac)
+        functools.partial(far_kernel, half_rows, pair_length),
+        out_shape=(full, head),
+        in_specs=[scalars, scalars] + [anywhere] * 9,
+        out_specs=(anywhere, anywhere),
+        scratch_shapes=local + [pltpu.VMEM(full.shape, b16), pltpu.VMEM(head.shape, b16), pltpu.SemaphoreType.DMA],
+        input_output_aliases={9: 0, 10: 1},
+        name="far",
+    )(far, first, before, grid, after, dep_row, dep_lon, lon_frac, lat_frac, out, first_fields)
 
 
 COS = (1, -19.7392087, 64.9393842, -85.4565372, 60.2407014, -26.3960673, 7.77462739, -1.42354417)
@@ -475,21 +588,16 @@
 
 def on_device(grid, dep_row, dep_lon, lon_frac, lat_frac, wave_slot, legendre):
     half_rows = wave_slot.shape[0]
-    fields, levels, pairs, pair_length = grid.shape
+    _, levels, pairs, pair_length = grid.shape
     slots = legendre.shape[0]
     axes = ("aa", "ba")
     sizes = (lax.axis_size("aa"), lax.axis_size("ba"))
     devices = sizes[0] * sizes[1]
-    device = lax.axis_index(axes)
-    first = (device * pairs).astype(jnp.int32).reshape(1)
+    first = (lax.axis_index(axes) * pairs).astype(jnp.int32).reshape(1)
     own = jnp.transpose(grid, (0, 2, 1, 3))
-    up = [(i, i + 1) for i in range(devices - 1)]
-    down = [(j, i) for i, j in up]
-    before = lax.ppermute(own[:, pairs - 2:], axes, up)
-    after = lax.ppermute(own[:, :2], axes, down)
     order = jnp.transpose(wave_slot.reshape(devices, slots)).reshape(1, half_rows)
-    out, head = interpolate(first, before, own, after, dep_row, jnp.transpose(dep_lon, (1, 0, 2)),
-                            jnp.transpose(lon_frac, (1, 0, 2)), lat_frac, half_rows, 2 * levels)
+    out, head = interpolate(first, own, dep_row, jnp.transpose(dep_lon, (1, 0, 2)), jnp.transpose(lon_frac, (1, 0, 2)),
+                            lat_frac, half_rows, 2 * levels, sizes)
     result = transform(head, order, wave_slot, legendre, half_rows, pair_length, sizes)
     return (jnp.transpose(out, (0, 2, 1, 3)), jnp.transpose(result, (1, 0, 2)))
 

time: 53 us -> 46.8 us (0.88)
  starting transfers between devices: 8.8 us -> 0 us
  Pallas kernels: 33.5 us -> 42 us
  waiting for transfers between devices: 4.73 us -> 0 us
  local copies, waits for them, and re-layouts: 4.98 us -> 3.99 us
    ppermute x2 -> x0, starting transfers between devices: 8.8 us -> none  [the longest x1 6.88 us: on_device(): before = lax.ppermute(own[:, pairs - 2:], axes, up)]
    pallas_call x1 -> x2, Pallas kernels: 13.8 us -> 20.9 us  [the longest x1 20.2 us: interpolate(): pl.pallas_call(functools.partial(near_kernel, sizes, half_rows, pair_leng...]
    ppermute x2 -> x0, waiting for transfers between devices: 4.73 us -> none  [the longest x1 4.73 us: on_device(): after = lax.ppermute(own[:, :2], axes, down)]
    pallas_call x1, Pallas kernels: 19.7 us -> 21.1 us  [transform(): pl.pallas_call(functools.partial(transform_kernel, sizes, pair_length), o...]
    slice x1 -> x0, local copies, waits for them, and re-layouts: 1.13 us -> none  [on_device(): after = lax.ppermute(own[:, :2], axes, down)]
    unnamed x6 -> x5, local copies, waits for them, and re-layouts: 2.91 us -> 3 us
  transfers between devices with their start and end apart: 2 -> 0, of which waited for: 1 -> 0; matrix products, arithmetic and copies ran while one was open for 3% -> 0% of each run, Pallas kernels for 0% -> 0%
where the time goes in v4:
time: 46.8 us; the launch traced here: 46.7 us
  Pallas kernels  42 us (90%)
  local copies, waits for them, and re-layouts  3.99 us (9%)
  between operations  0.68 us (1%)
    pallas_call x1, Pallas kernels, transform(): pl.pallas_call(functools.partial(transform_kernel, sizes, pair_length), o...  21.1 us
    pallas_call x1, Pallas kernels, interpolate(): pl.pallas_call(functools.partial(near_kernel, sizes, half_rows, pair_leng...  20.2 us
    unnamed x5, local copies, waits for them, and re-layouts  3 us

profile of v4, /device:TPU:1, one launch (start us, length us, event | category | flops | bytes accessed | tf_op | source)
XLA Modules:
  0.0 46.7 jit_solution(8414654736992759997)
XLA Ops:
  0.6 20.2 %near.1 = (bf16[4,5,4,2596]{3,2,1,0:T(4,128)(2,1)}, bf16[5,8,2688]{2,1,0:T(8,128)(2,1)}, s32[1]{0:T(128)}, bf16[4,2,4,2596]{3,2,1,0:T(4,128)(2,1)}, bf16[4,2,4,2596]{3,2,1,0:T(4,128)(2,1)}) custom-call(bf16[4,5,4,2596]{3,2,1,0:T(4,128)(2,1)} %bitcast.12, s32[5,2596]{1,0:T(8,128)} %row_hbm.3, s32[5,4,2596]{2,1,0:T(4,128)} %bitcast.15, ...), custom_call_target="tpu_custom_call" | custom-call | tf_op jit(solution)/shard_map/near/pallas_call | solution.py:371
  20.9 0.6 %far.1 = (bf16[4,5,4,2596]{3,2,1,0:T(4,128)(2,1)}, bf16[5,8,2688]{2,1,0:T(8,128)(2,1)}) custom-call(s32[1]{0:T(128)} %get-tuple-element.9.far_ref, s32[1]{0:T(128)} %bitcast.3.first_ref, bf16[4,2,4,2596]{3,2,1,0:T(4,128)(2,1)} %get-tuple-element.10.before_hbm, bf16[4,5,4,2596]{3,2,1,0:T(4,128)(2,1)} %bitcast.13, ...), custom_call_target="tpu_custom_call", output_to_operand_aliasing={{0}: (9, {}), {1}: (10, {})} | custom-call | tf_op jit(solution)/shard_map/far/pallas_call | solution.py:381
  21.5 0.0 copy-start
  21.5 0.9 %reshape.14 = s32[128,5]{1,0:T(8,128)S(1)} reshape(s32[640]{0:T(1024)} %waves_ref.1) | data formatting | bytes 5120 | tf_op jit(solution)/shard_map/reshape | solution.py:598
  22.5 0.1 copy.11
  22.5 0.6 %copy.14 = s32[1,1,5,128]{3,1,2,0:T(1,128)} copy(s32[1,1,5,128]{3,2,1,0:T(8,128)S(1)} %bitcast.21) | data formatting | bytes 5120
  23.1 21.1 %transform.1 = f32[5,16,640]{2,1,0:T(8,128)} custom-call(bf16[5,8,2688]{2,1,0:T(8,128)(2,1)} %get-tuple-element.15.y_ref, s32[1,640]{1,0:T(1,128)} %bitcast.22, s32[640]{0:T(1024)} %waves_ref.1, bf16[5,2,320,640]{3,2,1,0:T(8,128)(2,1)} %legendre_hbm.1), custom_call_target="tpu_custom_call" | custom-call | tf_op jit(solution)/shard_map/transform/pallas_call | solution.py:563
  44.3 0.0 copy-done
  44.3 0.8 %copy.19 = bf16[4,4,5,2596]{3,1,2,0:T(4,128)(2,1)} copy(bf16[4,4,5,2596]{3,1,2,0:T(4,128)(2,1)S(1)} %bitcast.14) | data formatting | bytes 830720
  45.0 1.6 %copy.20 = f32[16,5,640]{2,0,1:T(8,128)} copy(f32[16,5,640]{2,0,1:T(8,128)} %bitcast.19) | data formatting | bytes 409600
Async XLA Ops:
  21.5 22.7 %copy-start = (bf16[4,5,4,2596]{3,2,1,0:T(4,128)(2,1)S(1)}, bf16[4,5,4,2596]{3,2,1,0:T(4,128)(2,1)}, u32[]{:S(2)}) copy-start(bf16[4,5,4,2596]{3,2,1,0:T(4,128)(2,1)} %get-tuple-element.14) | copy-start | bytes 1246084

commit v5 on v4

--- a/solution.py
+++ b/solution.py
@@ -271,8 +271,21 @@
     ]
 
 
-def near_kernel(sizes, half_rows, pair_length, grid_hbm, row_hbm, lon_hbm, lonf_hbm, latf_hbm,
-                out_ref, head_ref, far_ref, before_hbm, after_hbm,
+def by_slot_then_device(wave, devices):
+    count = wave.shape[1]
+    slots = count // devices
+    wanted = lax.broadcasted_iota(jnp.int32, (1, count), 1)
+    wanted = slots * (wanted % devices) + wanted // devices
+    moves = (lax.broadcasted_iota(jnp.int32, (count, count), 0) == wanted).astype(jnp.float32).astype(jnp.bfloat16)
+    high, low = wave // 8, wave % 8
+    sub = lax.broadcasted_iota(jnp.int32, (16, count), 0)
+    digits = jnp.where(sub == 0, high, jnp.where(sub == 1, low, 0)).astype(jnp.float32).astype(jnp.bfloat16)
+    moved = jnp.dot(digits, moves, preferred_element_type=jnp.float32)
+    return (8.0 * moved[0:1] + moved[1:2]).astype(jnp.int32)
+
+
+def near_kernel(sizes, half_rows, pair_length, grid_hbm, row_hbm, lon_hbm, lonf_hbm, latf_hbm, wave_ref,
+                out_ref, head_ref, far_ref, before_hbm, after_hbm, order_ref,
                 before_s, own_s, after_s, row_s, lon_s, lonf_s, latf_s, place_t, ext_s, plan_s, y_s,
                 in_sem, send_sem, recv_sem, keep_sem):
     along, across = sizes
@@ -311,6 +324,7 @@
         steps.fill(j)
     for j in range(2, 2 + pairs):
         steps.close(j)
+    order_ref[...] = by_slot_then_device(wave_ref[...].reshape(1, half_rows), devices)
     for send in sends:
         send.wait()
     keeps = [pltpu.make_async_copy(before_s, before_hbm, keep_sem.at[0]), pltpu.make_async_copy(after_s, after_hbm, keep_sem.at[1])]
@@ -355,7 +369,7 @@
             copy.wait()
 
 
-def interpolate(first, grid, dep_row, dep_lon, lon_frac, lat_frac, half_rows, spectral_fields, sizes):
+def interpolate(first, grid, dep_row, dep_lon, lon_frac, lat_frac, wave_slot, half_rows, spectral_fields, sizes):
     groups, pairs, levels, pair_length = grid.shape
     fields = groups * levels
     padded = pl.cdiv(pair_length, LANES) * LANES
@@ -368,17 +382,17 @@
         pltpu.VMEM(halo.shape, b16), pltpu.VMEM(grid.shape, b16), pltpu.VMEM(halo.shape, b16),
         pltpu.VMEM(dep_row.shape, i32), pltpu.VMEM(dep_lon.shape, i32), pltpu.VMEM(lon_frac.shape, f32), pltpu.VMEM(lat_frac.shape, f32),
     ] + stencil_scratch(pairs, fields, pair_length)
-    out, first_fields, far, before, after = pl.pallas_call(
+    out, first_fields, far, before, after, order = pl.pallas_call(
         functools.partial(near_kernel, sizes, half_rows, pair_length),
-        out_shape=(full, head, jax.ShapeDtypeStruct((1,), i32), halo, halo),
-        in_specs=[anywhere] * 5,
-        out_specs=(vm, vm, scalars, anywhere, anywhere),
+        out_shape=(full, head, jax.ShapeDtypeStruct((1,), i32), halo, halo, jax.ShapeDtypeStruct((1, half_rows), i32)),
+        in_specs=[anywhere] * 5 + [vm],
+        out_specs=(vm, vm, scalars, anywhere, anywhere, vm),
         scratch_shapes=local + [pltpu.SemaphoreType.DMA((5,)), pltpu.SemaphoreType.DMA((2,)), pltpu.SemaphoreType.DMA((2,)),
                                 pltpu.SemaphoreType.DMA((2,))],
         compiler_params=pltpu.CompilerParams(collective_id=1, has_side_effects=True),
         name="near",
-    )(grid, dep_row, dep_lon, lon_frac, lat_frac)
-    return pl.pallas_call(
+    )(grid, dep_row, dep_lon, lon_frac, lat_frac, wave_slot)
+    out, first_fields = pl.pallas_call(
         functools.partial(far_kernel, half_rows, pair_length),
         out_shape=(full, head),
         in_specs=[scalars, scalars] + [anywhere] * 9,
@@ -387,7 +401,9 @@
         input_output_aliases={9: 0, 10: 1},
         name="far",
     )(far, first, before, grid, after, dep_row, dep_lon, lon_frac, lat_frac, out, first_fields)
-
+    return out, first_fields, order
+
+WIDE = 256
 
 COS = (1, -19.7392087, 64.9393842, -85.4565372, 60.2407014, -26.3960673, 7.77462739, -1.42354417)
 SIN = (6.28318531, -41.3417022, 81.6052456, -76.7057546, 42.0572162, -15.0833301, 3.7717259, -0.609657301)
@@ -407,7 +423,7 @@
 
 
 def transform_kernel(sizes, pair_length, y_ref, order_ref, waves_ref, legendre_hbm, out_ref,
-                     table_s, sums_s, four_s, mix_s, stage_s, send_s, got_s, plain_s, anti_s, kept_s, keptanti_s, turn_s, legendre_s,
+                     table_s, sums_s, back_s, turn_c, turn_n, four_s, mix_s, stage_s, send_s, got_s, plain_s, anti_s, kept_s, keptanti_s, turn_s, legendre_s,
                      legendre_sem, own_sem, send_sem, recv_sem):
     along, across = sizes
     devices = along * across
@@ -422,6 +438,7 @@
     first = me * pairs
     north = me < devices // 2
     parts = 8
+    wides = pl.cdiv(tiles * LANES, WIDE)
 
     weights_in = pltpu.make_async_copy(legendre_hbm, legendre_s, legendre_sem)
     weights_in.start()
@@ -457,36 +474,60 @@
         def line(n):
             return lax.broadcasted_iota(jnp.int32, (n, LANES), 0)
 
-        def waves(n, w):
-            return lax.broadcasted_iota(jnp.int32, (n, LANES), 1) + w * LANES
-
-        for w in range(slots):
-            fine_c, fine_s = cos_sin_turns((waves(16, w) * line(16)).astype(jnp.float32), length, inverse)
-            step_c, step_s = cos_sin_turns((waves(8, w) * (16 * line(8))).astype(jnp.float32), length, inverse)
-            for a in range(8):
-                ca, sa = step_c[a:a + 1], step_s[a:a + 1]
-                table_s[pl.ds(16 * a, 16), pl.ds(w * LANES, LANES)] = (ca * fine_c - sa * fine_s).astype(jnp.bfloat16)
-                table_s[pl.ds(16 * a, 16), pl.ds(half_rows + w * LANES, LANES)] = (sa * fine_c + ca * fine_s).astype(jnp.bfloat16)
+        wave = lax.broadcasted_iota(jnp.int32, (16, LANES), 1)
+        fine_c, fine_s = cos_sin_turns((wave * line(16)).astype(jnp.float32), length, inverse)
+        step_c, step_s = cos_sin_turns((wave * (16 * line(16))).astype(jnp.float32), length, inverse)
+        for a in range(WIDE // 16):
+            ca, sa = step_c[a:a + 1], step_s[a:a + 1]
+            cosine = ca * fine_c - sa * fine_s
+            sine = sa * fine_c + ca * fine_s
+            top, bottom = pl.ds(16 * a, 16), pl.ds(WIDE + 16 * a, 16)
+            left, right = pl.ds(0, LANES), pl.ds(LANES, LANES)
+            table_s[top, left] = cosine.astype(jnp.bfloat16)
+            table_s[top, right] = sine.astype(jnp.bfloat16)
+            table_s[bottom, left] = (-sine).astype(jnp.bfloat16)
+            table_s[bottom, right] = cosine.astype(jnp.bfloat16)
+        tile_c, tile_s = cos_sin_turns((wave * (WIDE * line(16) - start)).astype(jnp.float32), length, inverse)
+        back_s[0], back_s[1] = tile_c, tile_s
         lane = lax.broadcasted_iota(jnp.int32, (parts, LANES), 1)
-        blocks = []
-        for t in range(tiles):
-            col = lane + t * LANES
-            mine = (col >= start) & (col < start + whole)
-            blocks.append(jnp.where(mine, y_ref[q, :, pl.ds(t * LANES, LANES)].astype(jnp.float32)[:parts], 0.0))
-        stacked = jnp.concatenate(blocks, axis=0).astype(jnp.bfloat16)
+        part_c, part_s = cos_sin_turns((LANES * line(8) * (WIDE * lane - start)).astype(jnp.float32), length, inverse)
+        shifts = [cos_sin_turns((LANES * line(8) * (lane + i * LANES)).astype(jnp.float32), length, inverse) for i in range(2)]
+        for t in range(wides):
+            pc, ps = part_c[:, t:t + 1], part_s[:, t:t + 1]
+            for i in range(2):
+                sc, ss = shifts[i]
+                at = pl.ds(t * WIDE + i * LANES, LANES)
+                turn_c[:, at] = pc * sc - ps * ss
+                turn_n[:, at] = ps * sc + pc * ss
+        blocks = [[None] * (2 * 2) for _ in range(wides * slots)]
+        for t in range(wides):
+            for i in range(2):
+                at = t * WIDE + i * LANES
+                if at < tiles * LANES:
+                    col = lane + at
+                    mine = (col >= start) & (col < start + whole)
+                    v = jnp.where(mine, y_ref[q, :, pl.ds(at, LANES)].astype(jnp.float32)[:parts], 0.0)
+                for w in range(slots):
+                    row = blocks[w * wides + t]
+                    if at < tiles * LANES:
+                        row[i] = v * turn_c[pl.ds(w, 1), pl.ds(at, LANES)]
+                        row[2 + i] = v * turn_n[pl.ds(w, 1), pl.ds(at, LANES)]
+                    else:
+                        row[i] = row[2 + i] = jnp.zeros((parts, LANES), jnp.float32)
+        stacked = jnp.concatenate([jnp.concatenate(row, axis=1) for row in blocks], axis=0).astype(jnp.bfloat16)
         sums_s[...] = jnp.dot(stacked, table_s[...], preferred_element_type=jnp.float32)
         place = 2 * jnp.where(north, q, pairs - 1 - q) + half
         for w in range(slots):
-            tile_c, tile_s = cos_sin_turns((waves(24, w) * (LANES * line(24) - start)).astype(jnp.float32), length, inverse)
             real = jnp.zeros((parts, LANES), jnp.float32)
             imag = jnp.zeros((parts, LANES), jnp.float32)
-            for t in range(tiles):
-                c = sums_s[pl.ds(parts * t, parts), pl.ds(w * LANES, LANES)]
-                s = sums_s[pl.ds(parts * t, parts), pl.ds(half_rows + w * LANES, LANES)]
-                tc, ts = tile_c[t:t + 1], tile_s[t:t + 1]
+            for t in range(wides):
+                at = pl.ds(parts * (w * wides + t), parts)
+                c, s = sums_s[at, pl.ds(0, LANES)], sums_s[at, pl.ds(LANES, LANES)]
+                tc, ts = back_s[0, pl.ds(t, 1), :], back_s[1, pl.ds(t, 1), :]
                 real = real + (tc * c - ts * s)
                 imag = imag - (ts * c + tc * s)
-            keep = jnp.where(2 * waves(1, w) < whole, inverse, 0.0)
+            waves = lax.broadcasted_iota(jnp.int32, (1, LANES), 1) + w * LANES
+            keep = jnp.where(2 * waves < whole, inverse, 0.0)
             four_s[pl.ds(pl.multiple_of(place * 16, 16), 16), pl.ds(w * LANES, LANES)] = jnp.concatenate(
                 [real * keep, imag * keep], axis=0).astype(jnp.bfloat16)
         return 0
@@ -558,6 +599,7 @@
     pairs = y.shape[0]
     slots = legendre.shape[0]
     tiles = pl.cdiv(pair_length, LANES)
+    wides = pl.cdiv(tiles * LANES, WIDE)
     vm = pl.BlockSpec(memory_space=pltpu.VMEM)
     f32, b16 = jnp.float32, jnp.bfloat16
     return pl.pallas_call(
@@ -566,8 +608,11 @@
         in_specs=[vm, vm, pl.BlockSpec(memory_space=pltpu.SMEM), pl.BlockSpec(memory_space=pl.ANY)],
         out_specs=vm,
         scratch_shapes=[
-            pltpu.VMEM((LANES, 2 * half_rows), b16),
-            pltpu.VMEM((8 * tiles, 2 * half_rows), f32),
+            pltpu.VMEM((2 * WIDE, 2 * LANES), b16),
+            pltpu.VMEM((8 * wides * slots, 2 * LANES), f32),
+            pltpu.VMEM((2, 16, LANES), f32),
+            pltpu.VMEM((8, WIDE * wides), f32),
+            pltpu.VMEM((8, WIDE * wides), f32),
             pltpu.VMEM((32 * pairs, half_rows), b16),
             pltpu.VMEM((8, LANES, LANES), f32),
             pltpu.VMEM((8 * LANES, LANES), f32),
@@ -595,9 +640,8 @@
     devices = sizes[0] * sizes[1]
     first = (lax.axis_index(axes) * pairs).astype(jnp.int32).reshape(1)
     own = jnp.transpose(grid, (0, 2, 1, 3))
-    order = jnp.transpose(wave_slot.reshape(devices, slots)).reshape(1, half_rows)
-    out, head = interpolate(first, own, dep_row, jnp.transpose(dep_lon, (1, 0, 2)), jnp.transpose(lon_frac, (1, 0, 2)),
-                            lat_frac, half_rows, 2 * levels, sizes)
+    out, head, order = interpolate(first, own, dep_row, jnp.transpose(dep_lon, (1, 0, 2)), jnp.transpose(lon_frac, (1, 0, 2)),
+                                   lat_frac, wave_slot, half_rows, 2 * levels, sizes)
     result = transform(head, order, wave_slot, legendre, half_rows, pair_length, sizes)
     return (jnp.transpose(out, (0, 2, 1, 3)), jnp.transpose(result, (1, 0, 2)))
 

time: 46.8 us -> 44.8 us (0.957)
  local copies, waits for them, and re-layouts: 3.99 us -> 2.39 us
  Pallas kernels: 42 us -> 41.5 us
    pallas_call x1, Pallas kernels: 21.1 us -> 20 us  [transform(): pl.pallas_call(functools.partial(transform_kernel, sizes, pair_length), o...]
    reshape x1 -> x0, local copies, waits for them, and re-layouts: 0.93 us -> none  [on_device(): wave_slot.reshape(devices, slots)]
    pallas_call x1, Pallas kernels: 20.2 us -> 20.9 us  [interpolate(): pl.pallas_call(functools.partial(near_kernel, sizes, half_rows, pair_leng...]
    unnamed x5 -> x4, local copies, waits for them, and re-layouts: 3 us -> 2.39 us
where the time goes in v5:
time: 44.8 us; the launch traced here: 44.6 us
  Pallas kernels  41.5 us (93%)
  local copies, waits for them, and re-layouts  2.39 us (5%)
  between operations  0.68 us (2%)
    pallas_call x1, Pallas kernels, interpolate(): pl.pallas_call(functools.partial(near_kernel, sizes, half_rows, pair_leng...  20.9 us
    pallas_call x1, Pallas kernels, transform(): pl.pallas_call(functools.partial(transform_kernel, sizes, pair_length), o...  20 us
    unnamed x4, local copies, waits for them, and re-layouts  2.39 us

profile of v5, /device:TPU:1, one launch (start us, length us, event | category | flops | bytes accessed | tf_op | source)
XLA Modules:
  0.0 44.6 jit_solution(10582209677891992983)
XLA Ops:
  0.6 20.9 %near.1 = (bf16[4,5,4,2596]{3,2,1,0:T(4,128)(2,1)}, bf16[5,8,2688]{2,1,0:T(8,128)(2,1)}, s32[1]{0:T(128)}, bf16[4,2,4,2596]{3,2,1,0:T(4,128)(2,1)}, bf16[4,2,4,2596]{3,2,1,0:T(4,128)(2,1)}, /*index=5*/s32[1,640]{1,0:T(1,128)}) custom-call(bf16[4,5,4,2596]{3,2,1,0:T(4,128)(2,1)} %bitcast.6, s32[5,2596]{1,0:T(8,128)} %row_hbm.3, s32[5,4,2596]{2,1,0:T(4,128)} %bitcast.9, ...), custom_call_target="tpu_custom_call" | custom-call | tf_op jit(solution)/shard_map/near/pallas_call | solution.py:385
  21.5 0.6 %far.1 = (bf16[4,5,4,2596]{3,2,1,0:T(4,128)(2,1)}, bf16[5,8,2688]{2,1,0:T(8,128)(2,1)}) custom-call(s32[1]{0:T(128)} %get-tuple-element.10.far_ref, s32[1]{0:T(128)} %bitcast.3.first_ref, bf16[4,2,4,2596]{3,2,1,0:T(4,128)(2,1)} %get-tuple-element.11.before_hbm, bf16[4,5,4,2596]{3,2,1,0:T(4,128)(2,1)} %bitcast.7, ...), custom_call_target="tpu_custom_call", output_to_operand_aliasing={{0}: (9, {}), {1}: (10, {})} | custom-call | tf_op jit(solution)/shard_map/far/pallas_call | solution.py:395
  22.2 0.0 copy-start
  22.2 20.0 %transform.1 = f32[5,16,640]{2,1,0:T(8,128)} custom-call(bf16[5,8,2688]{2,1,0:T(8,128)(2,1)} %get-tuple-element.16.y_ref, s32[1,640]{1,0:T(1,128)} %get-tuple-element.17.order_ref, s32[640]{0:T(1024)} %waves_ref.1, bf16[5,2,320,640]{3,2,1,0:T(8,128)(2,1)} %legendre_hbm.1), custom_call_target="tpu_custom_call" | custom-call | tf_op jit(solution)/shard_map/transform/pallas_call | solution.py:605
  42.2 0.0 copy-done
  42.2 0.8 %copy.15 = bf16[4,4,5,2596]{3,1,2,0:T(4,128)(2,1)} copy(bf16[4,4,5,2596]{3,1,2,0:T(4,128)(2,1)S(1)} %bitcast.8) | data formatting | bytes 830720
  43.0 1.6 %copy.16 = f32[16,5,640]{2,0,1:T(8,128)} copy(f32[16,5,640]{2,0,1:T(8,128)} %bitcast.13) | data formatting | bytes 409600
Async XLA Ops:
  22.2 20.0 %copy-start = (bf16[4,5,4,2596]{3,2,1,0:T(4,128)(2,1)S(1)}, bf16[4,5,4,2596]{3,2,1,0:T(4,128)(2,1)}, u32[]{:S(2)}) copy-start(bf16[4,5,4,2596]{3,2,1,0:T(4,128)(2,1)} %get-tuple-element.15) | copy-start | bytes 1246084

commit v6 on v5

--- a/solution.py
+++ b/solution.py
@@ -204,7 +204,7 @@
         head_s[q, :, at] = total[:head_s.shape[1]].astype(jnp.bfloat16)
         return total
 
-    def near_units():
+    def near_units(chosen):
         def unit(q, u, carry):
             len0, straddle, half, tile, base, k0 = unit_scalars(q, u)
             at = pl.ds(pl.multiple_of(tile * LANES, LANES), LANES)
@@ -223,8 +223,8 @@
                             preferred_element_type=jnp.float32)
             return finish(q, u, straddle, tile, total, carry)
 
-        lax.fori_loop(0, tiles + 1, lambda u, carry: tuple(unit(q, u, carry[q]) for q in range(pairs)),
-                      (jnp.zeros((fields, LANES), jnp.float32),) * pairs)
+        lax.fori_loop(0, tiles + 1, lambda u, carry: tuple(unit(q, u, c) for q, c in zip(chosen, carry)),
+                      (jnp.zeros((fields, LANES), jnp.float32),) * len(chosen))
 
     def any_units():
         def unit(q, u, carry):
@@ -284,10 +284,10 @@
     return (8.0 * moved[0:1] + moved[1:2]).astype(jnp.int32)
 
 
-def near_kernel(sizes, half_rows, pair_length, grid_hbm, row_hbm, lon_hbm, lonf_hbm, latf_hbm, wave_ref,
-                out_ref, head_ref, far_ref, before_hbm, after_hbm, order_ref,
-                before_s, own_s, after_s, row_s, lon_s, lonf_s, latf_s, place_t, ext_s, plan_s, y_s,
-                in_sem, send_sem, recv_sem, keep_sem):
+def whole_kernel(sizes, half_rows, pair_length, grid_hbm, row_hbm, lon_hbm, lonf_hbm, latf_hbm, wave_ref, waves_ref, legendre_hbm,
+                 out_ref, result_ref, far_ref, before_hbm, after_hbm, order_ref,
+                 before_s, own_s, after_s, row_s, lon_s, lonf_s, latf_s, place_t, ext_s, plan_s, y_s, head_s,
+                 in_sem, halo_send_sem, halo_recv_sem, keep_sem, *refs):
     along, across = sizes
     devices = along * across
     pairs = own_s.shape[1]
@@ -298,33 +298,37 @@
     def where(device):
         return (device // across, lax.rem(device, across))
 
+    after_steps = transform_steps(sizes, pair_length, head_s, waves_ref, legendre_hbm, result_ref, refs[:16], refs[16:])
     barrier = pltpu.get_barrier_semaphore()
-    for device in (up, down):
-        pl.semaphore_signal(barrier, inc=1, device_id=where(device), device_id_type=pl.DeviceIdType.MESH)
     loads = [pltpu.make_async_copy(src, dst, in_sem.at[i]) for i, (src, dst) in enumerate((
         (row_hbm, row_s), (lon_hbm, lon_s), (lonf_hbm, lonf_s), (latf_hbm, latf_s), (grid_hbm, own_s)))]
     for load in loads:
         load.start()
-    pl.semaphore_wait(barrier, 2)
-    sends = []
-    for i, (begin, dst, device) in enumerate(((pairs - 2, before_s, up), (0, after_s, down))):
-        sends.append(pltpu.make_async_remote_copy(
-            src_ref=grid_hbm.at[:, pl.ds(begin, 2)], dst_ref=dst, send_sem=send_sem.at[i], recv_sem=recv_sem.at[i],
-            device_id=where(device), device_id_type=pl.DeviceIdType.MESH))
-        sends[-1].start()
+    after_steps.greet(barrier)
 
     steps = stencil_steps(half_rows, pair_length, me * pairs, (before_s, own_s, after_s), row_s, lon_s, lonf_s, latf_s,
-                          place_t, ext_s, plan_s, y_s, head_ref)
+                          place_t, ext_s, plan_s, y_s, head_s)
     steps.locate()
     steps.clear()
     for load in loads:
         load.wait()
-    far_ref[0] = jnp.max(steps.weigh_all())
+    flag = jnp.max(steps.weigh_all())
+
+    pl.semaphore_wait(barrier, devices - 1)
+    sends = []
+    for i, (begin, dst, device) in enumerate(((pairs - 2, before_s, up), (0, after_s, down))):
+        sends.append(pltpu.make_async_remote_copy(
+            src_ref=grid_hbm.at[:, pl.ds(begin, 2)], dst_ref=dst, send_sem=halo_send_sem.at[i], recv_sem=halo_recv_sem.at[i],
+            device_id=where(device), device_id_type=pl.DeviceIdType.MESH))
+        sends[-1].start()
     for j in range(2, 2 + pairs):
         steps.fill(j)
     for j in range(2, 2 + pairs):
         steps.close(j)
-    order_ref[...] = by_slot_then_device(wave_ref[...].reshape(1, half_rows), devices)
+    order = by_slot_then_device(wave_ref[...].reshape(1, half_rows), devices)
+    order_ref[...] = order
+    inner = tuple(range(2, pairs - 2))
+    steps.near_units(inner)
     for send in sends:
         send.wait()
     keeps = [pltpu.make_async_copy(before_s, before_hbm, keep_sem.at[0]), pltpu.make_async_copy(after_s, after_hbm, keep_sem.at[1])]
@@ -334,74 +338,70 @@
         steps.fill(j)
     for j in (0, 1, 2 + pairs, 3 + pairs):
         steps.close(j)
-    steps.near_units()
+    steps.near_units(tuple(q for q in range(pairs) if q not in inner))
+    after_steps.sums()
+    after_steps.lay_out(order_ref[...], flag)
+    own = after_steps.trade()
     steps.deliver(out_ref)
+    far_ref[0] = (after_steps.finish(own) > 0.0).astype(jnp.int32)
     for keep in keeps:
         keep.wait()
 
 
-def far_kernel(half_rows, pair_length, far_ref, first_ref, before_hbm, grid_hbm, after_hbm, row_hbm, lon_hbm, lonf_hbm, latf_hbm,
-               out_in, head_in, out_hbm, head_hbm,
-               before_s, own_s, after_s, row_s, lon_s, lonf_s, latf_s, place_t, ext_s, plan_s, y_s, out_s, head_s, sem):
-    del out_in, head_in
-
-    @pl.when(far_ref[0] > 0)
-    def _():
-        for src, dst in ((before_hbm, before_s), (grid_hbm, own_s), (after_hbm, after_s), (row_hbm, row_s), (lon_hbm, lon_s),
-                         (lonf_hbm, lonf_s), (latf_hbm, latf_s)):
-            copy = pltpu.make_async_copy(src, dst, sem)
-            copy.start()
-            copy.wait()
-        steps = stencil_steps(half_rows, pair_length, first_ref[0], (before_s, own_s, after_s), row_s, lon_s, lonf_s, latf_s,
-                              place_t, ext_s, plan_s, y_s, head_s)
-        steps.locate()
-        steps.clear()
-        steps.weigh_all()
-        for j in range(steps.near):
-            steps.fill(j)
-        for j in range(steps.near):
-            steps.close(j)
-        steps.any_units()
-        steps.deliver(out_s)
-        for src, dst in ((out_s, out_hbm), (head_s, head_hbm)):
-            copy = pltpu.make_async_copy(src, dst, sem)
-            copy.start()
-            copy.wait()
-
-
-def interpolate(first, grid, dep_row, dep_lon, lon_frac, lat_frac, wave_slot, half_rows, spectral_fields, sizes):
+def far_kernel(half_rows, pair_length, first_ref, before_ref, own_ref, after_ref, row_ref, lon_ref, lonf_ref, latf_ref,
+               out_ref, head_ref, place_t, ext_s, plan_s, y_s):
+    steps = stencil_steps(half_rows, pair_length, first_ref[0], (before_ref, own_ref, after_ref), row_ref, lon_ref, lonf_ref, latf_ref,
+                          place_t, ext_s, plan_s, y_s, head_ref)
+    steps.locate()
+    steps.clear()
+    steps.weigh_all()
+    for j in range(steps.near):
+        steps.fill(j)
+    for j in range(steps.near):
+        steps.close(j)
+    steps.any_units()
+    steps.deliver(out_ref)
+
+
+def both(first, grid, dep_row, dep_lon, lon_frac, lat_frac, wave_slot, legendre, half_rows, spectral_fields, sizes):
     groups, pairs, levels, pair_length = grid.shape
     fields = groups * levels
+    slots = legendre.shape[0]
     padded = pl.cdiv(pair_length, LANES) * LANES
     b16, f32, i32 = jnp.bfloat16, jnp.float32, jnp.int32
     vm, anywhere, scalars = (pl.BlockSpec(memory_space=m) for m in (pltpu.VMEM, pl.ANY, pltpu.SMEM))
     halo = jax.ShapeDtypeStruct((groups, 2, levels, pair_length), b16)
     head = jax.ShapeDtypeStruct((pairs, spectral_fields, padded), b16)
     full = jax.ShapeDtypeStruct(grid.shape, b16)
+    stencil = stencil_scratch(pairs, fields, pair_length)
     local = [
         pltpu.VMEM(halo.shape, b16), pltpu.VMEM(grid.shape, b16), pltpu.VMEM(halo.shape, b16),
         pltpu.VMEM(dep_row.shape, i32), pltpu.VMEM(dep_lon.shape, i32), pltpu.VMEM(lon_frac.shape, f32), pltpu.VMEM(lat_frac.shape, f32),
-    ] + stencil_scratch(pairs, fields, pair_length)
-    out, first_fields, far, before, after, order = pl.pallas_call(
-        functools.partial(near_kernel, sizes, half_rows, pair_length),
-        out_shape=(full, head, jax.ShapeDtypeStruct((1,), i32), halo, halo, jax.ShapeDtypeStruct((1, half_rows), i32)),
-        in_specs=[anywhere] * 5 + [vm],
+    ] + stencil + [pltpu.VMEM(head.shape, b16)]
+    out, result, far, before, after, order = pl.pallas_call(
+        functools.partial(whole_kernel, sizes, half_rows, pair_length),
+        out_shape=(full, jax.ShapeDtypeStruct((slots, 16, half_rows), f32), jax.ShapeDtypeStruct((1,), i32), halo, halo,
+                   jax.ShapeDtypeStruct((1, half_rows), i32)),
+        in_specs=[anywhere] * 5 + [vm, scalars, anywhere],
         out_specs=(vm, vm, scalars, anywhere, anywhere, vm),
         scratch_shapes=local + [pltpu.SemaphoreType.DMA((5,)), pltpu.SemaphoreType.DMA((2,)), pltpu.SemaphoreType.DMA((2,)),
-                                pltpu.SemaphoreType.DMA((2,))],
+                                pltpu.SemaphoreType.DMA((2,))] + transform_scratch(pairs, slots, half_rows, pair_length, legendre),
         compiler_params=pltpu.CompilerParams(collective_id=1, has_side_effects=True),
-        name="near",
-    )(grid, dep_row, dep_lon, lon_frac, lat_frac, wave_slot)
-    out, first_fields = pl.pallas_call(
-        functools.partial(far_kernel, half_rows, pair_length),
-        out_shape=(full, head),
-        in_specs=[scalars, scalars] + [anywhere] * 9,
-        out_specs=(anywhere, anywhere),
-        scratch_shapes=local + [pltpu.VMEM(full.shape, b16), pltpu.VMEM(head.shape, b16), pltpu.SemaphoreType.DMA],
-        input_output_aliases={9: 0, 10: 1},
-        name="far",
-    )(far, first, before, grid, after, dep_row, dep_lon, lon_frac, lat_frac, out, first_fields)
-    return out, first_fields, order
+        name="whole",
+    )(grid, dep_row, dep_lon, lon_frac, lat_frac, wave_slot, wave_slot, legendre)
+
+    def again():
+        redone, first_fields = pl.pallas_call(
+            functools.partial(far_kernel, half_rows, pair_length),
+            out_shape=(full, head),
+            in_specs=[scalars] + [vm] * 7,
+            out_specs=(vm, vm),
+            scratch_shapes=stencil,
+            name="far",
+        )(first, before, grid, after, dep_row, dep_lon, lon_frac, lat_frac)
+        return redone, transform(first_fields, order, wave_slot, legendre, half_rows, pair_length, sizes)
+
+    return lax.cond(far[0] > 0, again, lambda: (out, result))
 
 WIDE = 256
 
@@ -422,9 +422,9 @@
     return c, s * t
 
 
-def transform_kernel(sizes, pair_length, y_ref, order_ref, waves_ref, legendre_hbm, out_ref,
-                     table_s, sums_s, back_s, turn_c, turn_n, four_s, mix_s, stage_s, send_s, got_s, plain_s, anti_s, kept_s, keptanti_s, turn_s, legendre_s,
-                     legendre_sem, own_sem, send_sem, recv_sem):
+def transform_steps(sizes, pair_length, y_ref, waves_ref, legendre_hbm, result_ref, scratch, sems):
+    (table_s, sums_s, back_s, turn_c, turn_n, four_s, mix_s, stage_s, send_s, got_s, plain_s, anti_s, kept_s, keptanti_s, turn_s, legendre_s) = scratch
+    legendre_sem, own_sem, send_sem, recv_sem = sems
     along, across = sizes
     devices = along * across
     pairs = y_ref.shape[0]
@@ -440,8 +440,9 @@
     parts = 8
     wides = pl.cdiv(tiles * LANES, WIDE)
 
+    steps = Stencil()
+
     weights_in = pltpu.make_async_copy(legendre_hbm, legendre_s, legendre_sem)
-    weights_in.start()
 
     columns = [lax.rem(my_b + i, across) for i in range(across)]
 
@@ -457,8 +458,9 @@
 
         lax.fori_loop(1, along, others, 0)
 
-    barrier = pltpu.get_barrier_semaphore()
-    partners(lambda a, b: pl.semaphore_signal(barrier, inc=1, device_id=(a, b), device_id_type=pl.DeviceIdType.MESH))
+    def greet(barrier):
+        weights_in.start()
+        partners(lambda a, b: pl.semaphore_signal(barrier, inc=1, device_id=(a, b), device_id_type=pl.DeviceIdType.MESH))
 
     def one(i, _):
         q = i // 2
@@ -532,100 +534,127 @@
                 [real * keep, imag * keep], axis=0).astype(jnp.bfloat16)
         return 0
 
-    lax.fori_loop(0, rows, one, 0)
-
-    hot = (lax.broadcasted_iota(jnp.int32, (half_rows, half_rows), 0) == order_ref[...]).astype(jnp.float32).astype(jnp.bfloat16)
-    moved = jnp.dot(four_s[...], hot, preferred_element_type=jnp.float32)
-    mix_s[...] = jnp.zeros_like(mix_s)
-    for r in range(8):
-        for s in range(slots):
-            mix_s[r, pl.ds(16 * s, 16), :] = moved[16 * r:16 * r + 16, s * LANES:(s + 1) * LANES]
-        if r < slots:
-            for e in range(rows - 8):
-                mix_s[r, pl.ds(16 * (slots + e), 16), :] = moved[16 * (8 + e):16 * (8 + e) + 16, r * LANES:(r + 1) * LANES]
-        stage_s[pl.ds(r, LANES, stride=8), :] = mix_s[r].T
-    send_s[...] = stage_s[...].astype(jnp.bfloat16).reshape(send_s.shape)
-
-    pl.semaphore_wait(barrier, devices - 1)
+    def sums():
+        lax.fori_loop(0, rows, one, 0)
+
+    def lay_out(order, flag):
+        hot = (lax.broadcasted_iota(jnp.int32, (half_rows, half_rows), 0) == order).astype(jnp.float32).astype(jnp.bfloat16)
+        moved = jnp.dot(four_s[...], hot, preferred_element_type=jnp.float32)
+        mix_s[...] = jnp.zeros_like(mix_s)
+        raised = jnp.full((16, LANES), flag, jnp.int32).astype(jnp.float32)
+        for r in range(8):
+            for s in range(slots):
+                mix_s[r, pl.ds(16 * s, 16), :] = moved[16 * r:16 * r + 16, s * LANES:(s + 1) * LANES]
+            mix_s[r, pl.ds(LANES - 16, 16), :] = raised
+            if r < slots:
+                for e in range(rows - 8):
+                    mix_s[r, pl.ds(16 * (slots + e), 16), :] = moved[16 * (8 + e):16 * (8 + e) + 16, r * LANES:(r + 1) * LANES]
+            stage_s[pl.ds(r, LANES, stride=8), :] = mix_s[r].T
+        send_s[...] = stage_s[...].astype(jnp.bfloat16).reshape(send_s.shape)
 
     def post(a, b):
         pltpu.make_async_remote_copy(
             src_ref=send_s.at[a * across + b], dst_ref=got_s.at[me], send_sem=send_sem, recv_sem=recv_sem,
             device_id=(a, b), device_id_type=pl.DeviceIdType.MESH).start()
 
-    partners(post)
-    own = pltpu.make_async_copy(send_s.at[me], got_s.at[me], own_sem)
-    own.start()
-
-    src = lax.broadcasted_iota(jnp.int32, (slots * LANES, 2 * LANES), 0)
-    dst = lax.broadcasted_iota(jnp.int32, (slots * LANES, 2 * LANES), 1)
-    unfold = (((dst & 127) >> 4) == (src >> 7)) & ((src & 127) == 16 * (slots + (dst >> 7)) + (dst & 15))
-    unfold = unfold.astype(jnp.float32).astype(jnp.bfloat16)
-    slot_of = (lax.broadcasted_iota(jnp.int32, (half_rows, LANES), 1) >> 4).astype(jnp.float32).astype(jnp.bfloat16)
-    rest = pl.ds(0, devices - 1)
-    every = pltpu.make_async_remote_copy(
-        src_ref=send_s.at[rest], dst_ref=got_s.at[rest], send_sem=send_sem, recv_sem=recv_sem,
-        device_id=(my_a, columns[1]), device_id_type=pl.DeviceIdType.MESH)
-    every.wait_send()
-    every.wait_recv()
-    own.wait()
-
-    for d in range(devices // 2):
-        n = got_s[d].astype(jnp.float32)
-        o = got_s[devices - 1 - d].astype(jnp.float32)
-        plain_s[pl.ds(rows * d, 8), :] = n + o
-        anti_s[pl.ds(rows * d, 8), :] = n - o
-        kept_s[pl.ds(8 * d, 8), :] = n + o
-        keptanti_s[pl.ds(8 * d, 8), :] = n - o
-    weights_in.wait()
-    for par, wide, kept in ((0, plain_s, kept_s), (1, anti_s, keptanti_s)):
-        folded = jnp.concatenate([kept[pl.ds(s, devices // 2, stride=8), :] for s in range(slots)], axis=1).astype(jnp.bfloat16)
-        extra = jnp.dot(folded, unfold, preferred_element_type=jnp.float32)
-        for e in range(rows - 8):
-            wide[pl.ds(8 + e, devices // 2, stride=rows), :] = extra[:, e * LANES:(e + 1) * LANES]
-        values = wide[...].astype(jnp.bfloat16)
-        zero = jnp.zeros_like(values)
-        picked = jnp.concatenate([jnp.where(slot_of == jnp.bfloat16(s), values, zero) for s in range(slots)], axis=0)
-        table = jnp.concatenate([legendre_s[s, par] for s in range(slots)], axis=1)
-        turn_s[pl.ds(par, half_rows // 2, stride=2), :] = jnp.dot(table, picked, preferred_element_type=jnp.float32)
-    z = turn_s[...].T
-    degree = lax.broadcasted_iota(jnp.int32, (16, half_rows), 1)
-    for s in range(slots):
-        limit = half_rows - waves_ref[me * slots + s]
-        out_ref[s] = jnp.where(degree < limit, z[16 * s:16 * s + 16], 0.0)
+    def trade():
+        partners(post)
+        own = pltpu.make_async_copy(send_s.at[me], got_s.at[me], own_sem)
+        own.start()
+        return own
+
+    def finish(own):
+        src = lax.broadcasted_iota(jnp.int32, (slots * LANES, 2 * LANES), 0)
+        dst = lax.broadcasted_iota(jnp.int32, (slots * LANES, 2 * LANES), 1)
+        unfold = (((dst & 127) >> 4) == (src >> 7)) & ((src & 127) == 16 * (slots + (dst >> 7)) + (dst & 15))
+        unfold = unfold.astype(jnp.float32).astype(jnp.bfloat16)
+        slot_of = (lax.broadcasted_iota(jnp.int32, (half_rows, LANES), 1) >> 4).astype(jnp.float32).astype(jnp.bfloat16)
+        rest = pl.ds(0, devices - 1)
+        every = pltpu.make_async_remote_copy(
+            src_ref=send_s.at[rest], dst_ref=got_s.at[rest], send_sem=send_sem, recv_sem=recv_sem,
+            device_id=(my_a, columns[1]), device_id_type=pl.DeviceIdType.MESH)
+        every.wait_send()
+        every.wait_recv()
+        own.wait()
+
+        highest = jnp.zeros((8, LANES), jnp.float32)
+        for d in range(devices // 2):
+            n = got_s[d].astype(jnp.float32)
+            o = got_s[devices - 1 - d].astype(jnp.float32)
+            highest = jnp.maximum(highest, jnp.maximum(n, o))
+            plain_s[pl.ds(rows * d, 8), :] = n + o
+            anti_s[pl.ds(rows * d, 8), :] = n - o
+            kept_s[pl.ds(8 * d, 8), :] = n + o
+            keptanti_s[pl.ds(8 * d, 8), :] = n - o
+        weights_in.wait()
+        for par, wide, kept in ((0, plain_s, kept_s), (1, anti_s, keptanti_s)):
+            folded = jnp.concatenate([kept[pl.ds(s, devices // 2, stride=8), :] for s in range(slots)], axis=1).astype(jnp.bfloat16)
+            extra = jnp.dot(folded, unfold, preferred_element_type=jnp.float32)
+            for e in range(rows - 8):
+                wide[pl.ds(8 + e, devices // 2, stride=rows), :] = extra[:, e * LANES:(e + 1) * LANES]
+            values = wide[...].astype(jnp.bfloat16)
+            zero = jnp.zeros_like(values)
+            picked = jnp.concatenate([jnp.where(slot_of == jnp.bfloat16(s), values, zero) for s in range(slots)], axis=0)
+            table = jnp.concatenate([legendre_s[s, par] for s in range(slots)], axis=1)
+            turn_s[pl.ds(par, half_rows // 2, stride=2), :] = jnp.dot(table, picked, preferred_element_type=jnp.float32)
+        z = turn_s[...].T
+        degree = lax.broadcasted_iota(jnp.int32, (16, half_rows), 1)
+        for s in range(slots):
+            limit = half_rows - waves_ref[me * slots + s]
+            result_ref[s] = jnp.where(degree < limit, z[16 * s:16 * s + 16], 0.0)
+        lanes = lax.broadcasted_iota(jnp.int32, (8, LANES), 1)
+        return jnp.max(jnp.where(lanes >= LANES - 16, highest, 0.0))
+
+    steps.greet, steps.sums, steps.lay_out, steps.trade, steps.finish, steps.others = greet, sums, lay_out, trade, finish, devices - 1
+    return steps
+
+
+def transform_kernel(sizes, pair_length, y_ref, order_ref, waves_ref, legendre_hbm, out_ref, *refs):
+    steps = transform_steps(sizes, pair_length, y_ref, waves_ref, legendre_hbm, out_ref, refs[:16], refs[16:])
+    barrier = pltpu.get_barrier_semaphore()
+    steps.greet(barrier)
+    steps.sums()
+    steps.lay_out(order_ref[...], 0)
+    pl.semaphore_wait(barrier, steps.others)
+    steps.finish(steps.trade())
+
+
+def transform_scratch(pairs, slots, half_rows, pair_length, legendre):
+    tiles = pl.cdiv(pair_length, LANES)
+    wides = pl.cdiv(tiles * LANES, WIDE)
+    f32, b16 = jnp.float32, jnp.bfloat16
+    return [
+        pltpu.VMEM((2 * WIDE, 2 * LANES), b16),
+        pltpu.VMEM((8 * wides * slots, 2 * LANES), f32),
+        pltpu.VMEM((2, 16, LANES), f32),
+        pltpu.VMEM((8, WIDE * wides), f32),
+        pltpu.VMEM((8, WIDE * wides), f32),
+        pltpu.VMEM((32 * pairs, half_rows), b16),
+        pltpu.VMEM((8, LANES, LANES), f32),
+        pltpu.VMEM((8 * LANES, LANES), f32),
+        pltpu.VMEM((LANES, 8, LANES), b16),
+        pltpu.VMEM((LANES, 8, LANES), b16),
+        pltpu.VMEM((half_rows, LANES), f32),
+        pltpu.VMEM((half_rows, LANES), f32),
+        pltpu.VMEM((8 * LANES // 2, LANES), f32),
+        pltpu.VMEM((8 * LANES // 2, LANES), f32),
+        pltpu.VMEM((half_rows, LANES), f32),
+        pltpu.VMEM(legendre.shape, b16),
+        pltpu.SemaphoreType.DMA, pltpu.SemaphoreType.DMA, pltpu.SemaphoreType.DMA, pltpu.SemaphoreType.DMA,
+    ]
 
 
 def transform(y, order, waves, legendre, half_rows, pair_length, sizes):
     pairs = y.shape[0]
     slots = legendre.shape[0]
-    tiles = pl.cdiv(pair_length, LANES)
-    wides = pl.cdiv(tiles * LANES, WIDE)
     vm = pl.BlockSpec(memory_space=pltpu.VMEM)
-    f32, b16 = jnp.float32, jnp.bfloat16
+    f32 = jnp.float32
     return pl.pallas_call(
         functools.partial(transform_kernel, sizes, pair_length),
         out_shape=jax.ShapeDtypeStruct((slots, 16, half_rows), f32),
         in_specs=[vm, vm, pl.BlockSpec(memory_space=pltpu.SMEM), pl.BlockSpec(memory_space=pl.ANY)],
         out_specs=vm,
-        scratch_shapes=[
-            pltpu.VMEM((2 * WIDE, 2 * LANES), b16),
-            pltpu.VMEM((8 * wides * slots, 2 * LANES), f32),
-            pltpu.VMEM((2, 16, LANES), f32),
-            pltpu.VMEM((8, WIDE * wides), f32),
-            pltpu.VMEM((8, WIDE * wides), f32),
-            pltpu.VMEM((32 * pairs, half_rows), b16),
-            pltpu.VMEM((8, LANES, LANES), f32),
-            pltpu.VMEM((8 * LANES, LANES), f32),
-            pltpu.VMEM((LANES, 8, LANES), b16),
-            pltpu.VMEM((LANES, 8, LANES), b16),
-            pltpu.VMEM((half_rows, LANES), f32),
-            pltpu.VMEM((half_rows, LANES), f32),
-            pltpu.VMEM((8 * LANES // 2, LANES), f32),
-            pltpu.VMEM((8 * LANES // 2, LANES), f32),
-            pltpu.VMEM((half_rows, LANES), f32),
-            pltpu.VMEM(legendre.shape, b16),
-            pltpu.SemaphoreType.DMA, pltpu.SemaphoreType.DMA, pltpu.SemaphoreType.DMA, pltpu.SemaphoreType.DMA,
-        ],
+        scratch_shapes=transform_scratch(pairs, slots, half_rows, pair_length, legendre),
         compiler_params=pltpu.CompilerParams(collective_id=0, has_side_effects=True),
         name="transform",
     )(y, order, waves, legendre)
@@ -634,15 +663,13 @@
 def on_device(grid, dep_row, dep_lon, lon_frac, lat_frac, wave_slot, legendre):
     half_rows = wave_slot.shape[0]
     _, levels, pairs, pair_length = grid.shape
-    slots = legendre.shape[0]
     axes = ("aa", "ba")
     sizes = (lax.axis_size("aa"), lax.axis_size("ba"))
     devices = sizes[0] * sizes[1]
     first = (lax.axis_index(axes) * pairs).astype(jnp.int32).reshape(1)
     own = jnp.transpose(grid, (0, 2, 1, 3))
-    out, head, order = interpolate(first, own, dep_row, jnp.transpose(dep_lon, (1, 0, 2)), jnp.transpose(lon_frac, (1, 0, 2)),
-                                   lat_frac, wave_slot, half_rows, 2 * levels, sizes)
-    result = transform(head, order, wave_slot, legendre, half_rows, pair_length, sizes)
+    out, result = both(first, own, dep_row, jnp.transpose(dep_lon, (1, 0, 2)), jnp.transpose(lon_frac, (1, 0, 2)),
+                       lat_frac, wave_slot, legendre, half_rows, 2 * levels, sizes)
     return (jnp.transpose(out, (0, 2, 1, 3)), jnp.transpose(result, (1, 0, 2)))
 
 

time: 44.8 us -> 42.1 us (0.940)
  Pallas kernels: 41.5 us -> 39.1 us
  local copies, waits for them, and re-layouts: 2.39 us -> 1.47 us
  between operations: 0.68 us -> 1.38 us
    pallas_call x3 -> x1, Pallas kernels: 41.5 us -> 39.1 us  [both(): pl.pallas_call(functools.partial(whole_kernel, sizes, half_rows, pair_len...]
    unnamed x4 -> x14, local copies, waits for them, and re-layouts: 2.39 us -> 1.47 us
where the time goes in v6:
time: 42.1 us; the launch traced here: 42 us
  Pallas kernels  39.1 us (93%)
  local copies, waits for them, and re-layouts  1.47 us (3%)
  between operations  1.38 us (3%)
    pallas_call x1, Pallas kernels, both(): pl.pallas_call(functools.partial(whole_kernel, sizes, half_rows, pair_len...  39.1 us
    unnamed x14, local copies, waits for them, and re-layouts  1.47 us

profile of v6, /device:TPU:1, one launch (start us, length us, event | category | flops | bytes accessed | tf_op | source)
XLA Modules:
  0.0 42.0 jit_solution(8325635013494734641)
XLA Ops:
  0.6 0.0 copy-start.5
  0.6 0.0 copy-start.4
  0.7 0.0 copy-start.3
  0.7 0.0 copy-start.2
  0.7 0.0 copy-start.1
  0.7 0.0 copy-start
  0.7 39.1 %whole.1 = (bf16[4,5,4,2596]{3,2,1,0:T(4,128)(2,1)S(1)}, f32[5,16,640]{2,1,0:T(8,128)S(1)}, s32[1]{0:T(128)}, bf16[4,2,4,2596]{3,2,1,0:T(4,128)(2,1)S(1)}, bf16[...) custom-call(bf16[4,5,4,2596]{3,2,1,0:T(4,128)(2,1)} %bitcast.7, s32[5,2596]{1,0:T(8,128)} %row_hbm.1, ...), custom_call_target="tpu_custom_call" | custom-call | tf_op jit(solution)/shard_map/whole/pallas_call | solution.py:381
  40.5 0.0 copy-done.5
  40.5 0.0 copy-done.4
  40.5 0.0 copy-done.3
  40.5 0.0 copy-done.2
  40.5 0.0 copy-done.1
  40.5 0.0 copy-done
  40.5 0.8 %copy.15 = bf16[4,4,5,2596]{3,1,2,0:T(4,128)(2,1)} copy(bf16[4,4,5,2596]{3,1,2,0:T(4,128)(2,1)S(1)} %bitcast.13) | data formatting | bytes 830720
  41.3 0.7 %copy.16 = f32[16,5,640]{2,0,1:T(8,128)} copy(f32[16,5,640]{2,0,1:T(8,128)S(1)} %bitcast.14) | data formatting | bytes 409600
  (1 shorter events, 0.0 us)
Async XLA Ops:
  0.6 39.8 %copy-start.5 = (s32[640]{0:T(1024)S(1)}, s32[640]{0:T(1024)}, u32[]{:S(2)}) copy-start(s32[640]{0:T(1024)} %waves_ref.1) | copy-start | bytes 7684
  0.6 39.8 %copy-start.4 = (f32[5,2596]{1,0:T(8,128)S(1)}, f32[5,2596]{1,0:T(8,128)}, u32[]{:S(2)}) copy-start(f32[5,2596]{1,0:T(8,128)} %latf_hbm.1) | copy-start | bytes 155764
  0.7 39.8 %copy-start.3 = (s32[5,2596]{1,0:T(8,128)S(1)}, s32[5,2596]{1,0:T(8,128)}, u32[]{:S(2)}) copy-start(s32[5,2596]{1,0:T(8,128)} %row_hbm.1) | copy-start | bytes 155764
  0.7 39.8 %copy-start.2 = (f32[4,5,2596]{2,0,1:T(4,128)S(1)}, f32[4,5,2596]{2,0,1:T(4,128)}, u32[]{:S(2)}) copy-start(f32[4,5,2596]{2,0,1:T(4,128)} %param.12) | copy-start | bytes 623044
  0.7 39.8 %copy-start.1 = (s32[4,5,2596]{2,0,1:T(4,128)S(1)}, s32[4,5,2596]{2,0,1:T(4,128)}, u32[]{:S(2)}) copy-start(s32[4,5,2596]{2,0,1:T(4,128)} %param.11) | copy-start | bytes 623044
  0.7 39.8 %copy-start = (bf16[4,4,5,2596]{3,1,2,0:T(4,128)(2,1)S(1)}, bf16[4,4,5,2596]{3,1,2,0:T(4,128)(2,1)}, u32[]{:S(2)}) copy-start(bf16[4,4,5,2596]{3,1,2,0:T(4,128)(2,1)} %param.9) | copy-start | bytes 1246084

commit v7 on v6

--- a/solution.py
+++ b/solution.py
@@ -285,9 +285,9 @@
 
 
 def whole_kernel(sizes, half_rows, pair_length, grid_hbm, row_hbm, lon_hbm, lonf_hbm, latf_hbm, wave_ref, waves_ref, legendre_hbm,
-                 out_ref, result_ref, far_ref, before_hbm, after_hbm, order_ref,
-                 before_s, own_s, after_s, row_s, lon_s, lonf_s, latf_s, place_t, ext_s, plan_s, y_s, head_s,
-                 in_sem, halo_send_sem, halo_recv_sem, keep_sem, *refs):
+                 out_ref, result_ref, far_ref, before_s, after_s, order_ref,
+                 own_s, row_s, lon_s, lonf_s, latf_s, place_t, ext_s, plan_s, y_s, head_s,
+                 in_sem, halo_send_sem, halo_recv_sem, *refs):
     along, across = sizes
     devices = along * across
     pairs = own_s.shape[1]
@@ -298,7 +298,7 @@
     def where(device):
         return (device // across, lax.rem(device, across))
 
-    after_steps = transform_steps(sizes, pair_length, head_s, waves_ref, legendre_hbm, result_ref, refs[:16], refs[16:])
+    after_steps = transform_steps(sizes, pair_length, head_s, waves_ref, legendre_hbm, result_ref, refs[:14], refs[14:])
     barrier = pltpu.get_barrier_semaphore()
     loads = [pltpu.make_async_copy(src, dst, in_sem.at[i]) for i, (src, dst) in enumerate((
         (row_hbm, row_s), (lon_hbm, lon_s), (lonf_hbm, lonf_s), (latf_hbm, latf_s), (grid_hbm, own_s)))]
@@ -308,7 +308,6 @@
 
     steps = stencil_steps(half_rows, pair_length, me * pairs, (before_s, own_s, after_s), row_s, lon_s, lonf_s, latf_s,
                           place_t, ext_s, plan_s, y_s, head_s)
-    steps.locate()
     steps.clear()
     for load in loads:
         load.wait()
@@ -327,13 +326,11 @@
         steps.close(j)
     order = by_slot_then_device(wave_ref[...].reshape(1, half_rows), devices)
     order_ref[...] = order
+    steps.locate()
     inner = tuple(range(2, pairs - 2))
     steps.near_units(inner)
     for send in sends:
         send.wait()
-    keeps = [pltpu.make_async_copy(before_s, before_hbm, keep_sem.at[0]), pltpu.make_async_copy(after_s, after_hbm, keep_sem.at[1])]
-    for keep in keeps:
-        keep.start()
     for j in (0, 1, 2 + pairs, 3 + pairs):
         steps.fill(j)
     for j in (0, 1, 2 + pairs, 3 + pairs):
@@ -344,8 +341,6 @@
     own = after_steps.trade()
     steps.deliver(out_ref)
     far_ref[0] = (after_steps.finish(own) > 0.0).astype(jnp.int32)
-    for keep in keeps:
-        keep.wait()
 
 
 def far_kernel(half_rows, pair_length, first_ref, before_ref, own_ref, after_ref, row_ref, lon_ref, lonf_ref, latf_ref,
@@ -375,17 +370,15 @@
     full = jax.ShapeDtypeStruct(grid.shape, b16)
     stencil = stencil_scratch(pairs, fields, pair_length)
     local = [
-        pltpu.VMEM(halo.shape, b16), pltpu.VMEM(grid.shape, b16), pltpu.VMEM(halo.shape, b16),
-        pltpu.VMEM(dep_row.shape, i32), pltpu.VMEM(dep_lon.shape, i32), pltpu.VMEM(lon_frac.shape, f32), pltpu.VMEM(lat_frac.shape, f32),
+        pltpu.VMEM(grid.shape, b16), pltpu.VMEM(dep_row.shape, i32), pltpu.VMEM(dep_lon.shape, i32), pltpu.VMEM(lon_frac.shape, f32), pltpu.VMEM(lat_frac.shape, f32),
     ] + stencil + [pltpu.VMEM(head.shape, b16)]
     out, result, far, before, after, order = pl.pallas_call(
         functools.partial(whole_kernel, sizes, half_rows, pair_length),
         out_shape=(full, jax.ShapeDtypeStruct((slots, 16, half_rows), f32), jax.ShapeDtypeStruct((1,), i32), halo, halo,
                    jax.ShapeDtypeStruct((1, half_rows), i32)),
         in_specs=[anywhere] * 5 + [vm, scalars, anywhere],
-        out_specs=(vm, vm, scalars, anywhere, anywhere, vm),
-        scratch_shapes=local + [pltpu.SemaphoreType.DMA((5,)), pltpu.SemaphoreType.DMA((2,)), pltpu.SemaphoreType.DMA((2,)),
-                                pltpu.SemaphoreType.DMA((2,))] + transform_scratch(pairs, slots, half_rows, pair_length, legendre),
+        out_specs=(vm, vm, scalars, vm, vm, vm),
+        scratch_shapes=local + [pltpu.SemaphoreType.DMA((5,)), pltpu.SemaphoreType.DMA((2,)), pltpu.SemaphoreType.DMA((2,))] + transform_scratch(pairs, slots, half_rows, pair_length, legendre),
         compiler_params=pltpu.CompilerParams(collective_id=1, has_side_effects=True),
         name="whole",
     )(grid, dep_row, dep_lon, lon_frac, lat_frac, wave_slot, wave_slot, legendre)
@@ -423,7 +416,7 @@
 
 
 def transform_steps(sizes, pair_length, y_ref, waves_ref, legendre_hbm, result_ref, scratch, sems):
-    (table_s, sums_s, back_s, turn_c, turn_n, four_s, mix_s, stage_s, send_s, got_s, plain_s, anti_s, kept_s, keptanti_s, turn_s, legendre_s) = scratch
+    (table_s, sums_s, back_s, turn_c, turn_n, four_s, mix_s, stage_s, send_s, got_s, plain_s, anti_s, turn_s, legendre_s) = scratch
     legendre_sem, own_sem, send_sem, recv_sem = sems
     along, across = sizes
     devices = along * across
@@ -447,29 +440,27 @@
     columns = [lax.rem(my_b + i, across) for i in range(across)]
 
     def partners(act):
-        for b in range(1, across):
-            act(my_a, columns[b])
-
         def others(i, _):
-            a = lax.rem(my_a + i, along)
+            a = lax.rem(my_a + along // 2 + (1 - 2 * lax.rem(i, 2)) * ((i + 1) // 2), along)
             for b in range(across):
                 act(a, columns[b])
             return 0
 
-        lax.fori_loop(1, along, others, 0)
+        lax.fori_loop(0, along - 1, others, 0)
+        for b in range(1, across):
+            act(my_a, columns[b])
 
     def greet(barrier):
         weights_in.start()
         partners(lambda a, b: pl.semaphore_signal(barrier, inc=1, device_id=(a, b), device_id_type=pl.DeviceIdType.MESH))
 
-    def one(i, _):
-        q = i // 2
-        half = i - 2 * q
+    def one(q, half):
+        table, sums_of, back, turns_c, turns_n = (x.at[half] for x in (table_s, sums_s, back_s, turn_c, turn_n))
         pair = first + q
         inner = jnp.where(north, pair, half_rows - 1 - pair)
         len0 = 16 + 4 * (half_rows // 2 - inner)
-        start = jnp.where(half == 1, len0, 0)
-        whole = jnp.where(half == 1, 16 + 4 * (half_rows // 2 + 1 + inner), len0)
+        start = len0 if half else 0
+        whole = 16 + 4 * (half_rows // 2 + 1 + inner) if half else len0
         length = jnp.full((1, LANES), whole, jnp.int32).astype(jnp.float32)
         inverse = 1.0 / length
 
@@ -485,12 +476,12 @@
             sine = sa * fine_c + ca * fine_s
             top, bottom = pl.ds(16 * a, 16), pl.ds(WIDE + 16 * a, 16)
             left, right = pl.ds(0, LANES), pl.ds(LANES, LANES)
-            table_s[top, left] = cosine.astype(jnp.bfloat16)
-            table_s[top, right] = sine.astype(jnp.bfloat16)
-            table_s[bottom, left] = (-sine).astype(jnp.bfloat16)
-            table_s[bottom, right] = cosine.astype(jnp.bfloat16)
+            table[top, left] = cosine.astype(jnp.bfloat16)
+            table[top, right] = sine.astype(jnp.bfloat16)
+            table[bottom, left] = (-sine).astype(jnp.bfloat16)
+            table[bottom, right] = cosine.astype(jnp.bfloat16)
         tile_c, tile_s = cos_sin_turns((wave * (WIDE * line(16) - start)).astype(jnp.float32), length, inverse)
-        back_s[0], back_s[1] = tile_c, tile_s
+        back[0], back[1] = tile_c, tile_s
         lane = lax.broadcasted_iota(jnp.int32, (parts, LANES), 1)
         part_c, part_s = cos_sin_turns((LANES * line(8) * (WIDE * lane - start)).astype(jnp.float32), length, inverse)
         shifts = [cos_sin_turns((LANES * line(8) * (lane + i * LANES)).astype(jnp.float32), length, inverse) for i in range(2)]
@@ -499,8 +490,8 @@
             for i in range(2):
                 sc, ss = shifts[i]
                 at = pl.ds(t * WIDE + i * LANES, LANES)
-                turn_c[:, at] = pc * sc - ps * ss
-                turn_n[:, at] = ps * sc + pc * ss
+                turns_c[:, at] = pc * sc - ps * ss
+                turns_n[:, at] = ps * sc + pc * ss
         blocks = [[None] * (2 * 2) for _ in range(wides * slots)]
         for t in range(wides):
             for i in range(2):
@@ -512,30 +503,34 @@
                 for w in range(slots):
                     row = blocks[w * wides + t]
                     if at < tiles * LANES:
-                        row[i] = v * turn_c[pl.ds(w, 1), pl.ds(at, LANES)]
-                        row[2 + i] = v * turn_n[pl.ds(w, 1), pl.ds(at, LANES)]
+                        row[i] = v * turns_c[pl.ds(w, 1), pl.ds(at, LANES)]
+                        row[2 + i] = v * turns_n[pl.ds(w, 1), pl.ds(at, LANES)]
                     else:
                         row[i] = row[2 + i] = jnp.zeros((parts, LANES), jnp.float32)
         stacked = jnp.concatenate([jnp.concatenate(row, axis=1) for row in blocks], axis=0).astype(jnp.bfloat16)
-        sums_s[...] = jnp.dot(stacked, table_s[...], preferred_element_type=jnp.float32)
+        sums_of[...] = jnp.dot(stacked, table[...], preferred_element_type=jnp.float32)
         place = 2 * jnp.where(north, q, pairs - 1 - q) + half
         for w in range(slots):
             real = jnp.zeros((parts, LANES), jnp.float32)
             imag = jnp.zeros((parts, LANES), jnp.float32)
             for t in range(wides):
                 at = pl.ds(parts * (w * wides + t), parts)
-                c, s = sums_s[at, pl.ds(0, LANES)], sums_s[at, pl.ds(LANES, LANES)]
-                tc, ts = back_s[0, pl.ds(t, 1), :], back_s[1, pl.ds(t, 1), :]
+                c, s = sums_of[at, pl.ds(0, LANES)], sums_of[at, pl.ds(LANES, LANES)]
+                tc, ts = back[0, pl.ds(t, 1), :], back[1, pl.ds(t, 1), :]
                 real = real + (tc * c - ts * s)
                 imag = imag - (ts * c + tc * s)
             waves = lax.broadcasted_iota(jnp.int32, (1, LANES), 1) + w * LANES
             keep = jnp.where(2 * waves < whole, inverse, 0.0)
             four_s[pl.ds(pl.multiple_of(place * 16, 16), 16), pl.ds(w * LANES, LANES)] = jnp.concatenate(
                 [real * keep, imag * keep], axis=0).astype(jnp.bfloat16)
-        return 0
 
     def sums():
-        lax.fori_loop(0, rows, one, 0)
+        def step(q, _):
+            for half in range(2):
+                one(q, half)
+            return 0
+
+        lax.fori_loop(0, pairs, step, 0)
 
     def lay_out(order, flag):
         hot = (lax.broadcasted_iota(jnp.int32, (half_rows, half_rows), 0) == order).astype(jnp.float32).astype(jnp.bfloat16)
@@ -584,11 +579,9 @@
             highest = jnp.maximum(highest, jnp.maximum(n, o))
             plain_s[pl.ds(rows * d, 8), :] = n + o
             anti_s[pl.ds(rows * d, 8), :] = n - o
-            kept_s[pl.ds(8 * d, 8), :] = n + o
-            keptanti_s[pl.ds(8 * d, 8), :] = n - o
         weights_in.wait()
-        for par, wide, kept in ((0, plain_s, kept_s), (1, anti_s, keptanti_s)):
-            folded = jnp.concatenate([kept[pl.ds(s, devices // 2, stride=8), :] for s in range(slots)], axis=1).astype(jnp.bfloat16)
+        for par, wide in ((0, plain_s), (1, anti_s)):
+            folded = jnp.concatenate([wide[pl.ds(s, devices // 2, stride=rows), :] for s in range(slots)], axis=1).astype(jnp.bfloat16)
             extra = jnp.dot(folded, unfold, preferred_element_type=jnp.float32)
             for e in range(rows - 8):
                 wide[pl.ds(8 + e, devices // 2, stride=rows), :] = extra[:, e * LANES:(e + 1) * LANES]
@@ -610,7 +603,7 @@
 
 
 def transform_kernel(sizes, pair_length, y_ref, order_ref, waves_ref, legendre_hbm, out_ref, *refs):
-    steps = transform_steps(sizes, pair_length, y_ref, waves_ref, legendre_hbm, out_ref, refs[:16], refs[16:])
+    steps = transform_steps(sizes, pair_length, y_ref, waves_ref, legendre_hbm, out_ref, refs[:14], refs[14:])
     barrier = pltpu.get_barrier_semaphore()
     steps.greet(barrier)
     steps.sums()
@@ -624,11 +617,11 @@
     wides = pl.cdiv(tiles * LANES, WIDE)
     f32, b16 = jnp.float32, jnp.bfloat16
     return [
-        pltpu.VMEM((2 * WIDE, 2 * LANES), b16),
-        pltpu.VMEM((8 * wides * slots, 2 * LANES), f32),
-        pltpu.VMEM((2, 16, LANES), f32),
-        pltpu.VMEM((8, WIDE * wides), f32),
-        pltpu.VMEM((8, WIDE * wides), f32),
+        pltpu.VMEM((2, 2 * WIDE, 2 * LANES), b16),
+        pltpu.VMEM((2, 8 * wides * slots, 2 * LANES), f32),
+        pltpu.VMEM((2, 2, 16, LANES), f32),
+        pltpu.VMEM((2, 8, WIDE * wides), f32),
+        pltpu.VMEM((2, 8, WIDE * wides), f32),
         pltpu.VMEM((32 * pairs, half_rows), b16),
         pltpu.VMEM((8, LANES, LANES), f32),
         pltpu.VMEM((8 * LANES, LANES), f32),
@@ -636,8 +629,6 @@
         pltpu.VMEM((LANES, 8, LANES), b16),
         pltpu.VMEM((half_rows, LANES), f32),
         pltpu.VMEM((half_rows, LANES), f32),
-        pltpu.VMEM((8 * LANES // 2, LANES), f32),
-        pltpu.VMEM((8 * LANES // 2, LANES), f32),
         pltpu.VMEM((half_rows, LANES), f32),
         pltpu.VMEM(legendre.shape, b16),
         pltpu.SemaphoreType.DMA, pltpu.SemaphoreType.DMA, pltpu.SemaphoreType.DMA, pltpu.SemaphoreType.DMA,

time: 42.1 us -> 40.5 us (0.962)
  Pallas kernels: 39.1 us -> 37.5 us
    pallas_call x1, Pallas kernels: 39.1 us -> 37.5 us  [both(): pl.pallas_call(functools.partial(whole_kernel, sizes, half_rows, pair_len...]
where the time goes in v7:
time: 40.5 us; the launch traced here: 40.4 us
  Pallas kernels  37.5 us (93%)
  local copies, waits for them, and re-layouts  1.47 us (4%)
  between operations  1.38 us (3%)
    pallas_call x1, Pallas kernels, both(): pl.pallas_call(functools.partial(whole_kernel, sizes, half_rows, pair_len...  37.5 us
    unnamed x14, local copies, waits for them, and re-layouts  1.47 us

profile of v7, /device:TPU:1, one launch (start us, length us, event | category | flops | bytes accessed | tf_op | source)
XLA Modules:
  0.0 40.4 jit_solution(15932464612465041300)
XLA Ops:
  0.6 0.0 copy-start.5
  0.6 0.0 copy-start.4
  0.7 0.0 copy-start.3
  0.7 0.0 copy-start.2
  0.7 0.0 copy-start.1
  0.7 0.0 copy-start
  0.7 37.5 %whole.1 = (bf16[4,5,4,2596]{3,2,1,0:T(4,128)(2,1)S(1)}, f32[5,16,640]{2,1,0:T(8,128)S(1)}, s32[1]{0:T(128)}, bf16[4,2,4,2596]{3,2,1,0:T(4,128)(2,1)S(1)}, bf16[...) custom-call(bf16[4,5,4,2596]{3,2,1,0:T(4,128)(2,1)} %bitcast.7, s32[5,2596]{1,0:T(8,128)} %row_hbm.1, ...), custom_call_target="tpu_custom_call" | custom-call | tf_op jit(solution)/shard_map/whole/pallas_call | solution.py:375
  38.9 0.0 copy-done.5
  38.9 0.0 copy-done.4
  38.9 0.0 copy-done.3
  38.9 0.0 copy-done.2
  38.9 0.0 copy-done.1
  38.9 0.0 copy-done
  38.9 0.8 %copy.15 = bf16[4,4,5,2596]{3,1,2,0:T(4,128)(2,1)} copy(bf16[4,4,5,2596]{3,1,2,0:T(4,128)(2,1)S(1)} %bitcast.13) | data formatting | bytes 830720
  39.7 0.7 %copy.16 = f32[16,5,640]{2,0,1:T(8,128)} copy(f32[16,5,640]{2,0,1:T(8,128)S(1)} %bitcast.14) | data formatting | bytes 409600
  (1 shorter events, 0.0 us)
Async XLA Ops:
  0.6 38.2 %copy-start.5 = (s32[640]{0:T(1024)S(1)}, s32[640]{0:T(1024)}, u32[]{:S(2)}) copy-start(s32[640]{0:T(1024)} %waves_ref.1) | copy-start | bytes 7684
  0.6 38.2 %copy-start.4 = (f32[5,2596]{1,0:T(8,128)S(1)}, f32[5,2596]{1,0:T(8,128)}, u32[]{:S(2)}) copy-start(f32[5,2596]{1,0:T(8,128)} %latf_hbm.1) | copy-start | bytes 155764
  0.7 38.2 %copy-start.3 = (s32[5,2596]{1,0:T(8,128)S(1)}, s32[5,2596]{1,0:T(8,128)}, u32[]{:S(2)}) copy-start(s32[5,2596]{1,0:T(8,128)} %row_hbm.1) | copy-start | bytes 155764
  0.7 38.2 %copy-start.2 = (f32[4,5,2596]{2,0,1:T(4,128)S(1)}, f32[4,5,2596]{2,0,1:T(4,128)}, u32[]{:S(2)}) copy-start(f32[4,5,2596]{2,0,1:T(4,128)} %param.12) | copy-start | bytes 623044
  0.7 38.2 %copy-start.1 = (s32[4,5,2596]{2,0,1:T(4,128)S(1)}, s32[4,5,2596]{2,0,1:T(4,128)}, u32[]{:S(2)}) copy-start(s32[4,5,2596]{2,0,1:T(4,128)} %param.11) | copy-start | bytes 623044
  0.7 38.2 %copy-start = (bf16[4,4,5,2596]{3,1,2,0:T(4,128)(2,1)S(1)}, bf16[4,4,5,2596]{3,1,2,0:T(4,128)(2,1)}, u32[]{:S(2)}) copy-start(bf16[4,4,5,2596]{3,1,2,0:T(4,128)(2,1)} %param.9) | copy-start | bytes 1246084

commit v8 on v7

--- a/solution.py
+++ b/solution.py
@@ -315,10 +315,11 @@
 
     pl.semaphore_wait(barrier, devices - 1)
     sends = []
-    for i, (begin, dst, device) in enumerate(((pairs - 2, before_s, up), (0, after_s, down))):
+    for i, (row, dst, slot, device) in enumerate((
+            (pairs - 1, before_s, 1, up), (0, after_s, 0, down), (pairs - 2, before_s, 0, up), (1, after_s, 1, down))):
         sends.append(pltpu.make_async_remote_copy(
-            src_ref=grid_hbm.at[:, pl.ds(begin, 2)], dst_ref=dst, send_sem=halo_send_sem.at[i], recv_sem=halo_recv_sem.at[i],
-            device_id=where(device), device_id_type=pl.DeviceIdType.MESH))
+            src_ref=grid_hbm.at[:, pl.ds(row, 1)], dst_ref=dst.at[:, pl.ds(slot, 1)], send_sem=halo_send_sem.at[i],
+            recv_sem=halo_recv_sem.at[i], device_id=where(device), device_id_type=pl.DeviceIdType.MESH))
         sends[-1].start()
     for j in range(2, 2 + pairs):
         steps.fill(j)
@@ -329,13 +330,14 @@
     steps.locate()
     inner = tuple(range(2, pairs - 2))
     steps.near_units(inner)
-    for send in sends:
-        send.wait()
-    for j in (0, 1, 2 + pairs, 3 + pairs):
-        steps.fill(j)
-    for j in (0, 1, 2 + pairs, 3 + pairs):
-        steps.close(j)
-    steps.near_units(tuple(q for q in range(pairs) if q not in inner))
+    for arriving, rows, units in ((sends[:2], (1, 2 + pairs), (1, pairs - 2)), (sends[2:], (0, 3 + pairs), (0, pairs - 1))):
+        for send in arriving:
+            send.wait()
+        for j in rows:
+            steps.fill(j)
+        for j in rows:
+            steps.close(j)
+        steps.near_units(units)
     after_steps.sums()
     after_steps.lay_out(order_ref[...], flag)
     own = after_steps.trade()
@@ -378,7 +380,7 @@
                    jax.ShapeDtypeStruct((1, half_rows), i32)),
         in_specs=[anywhere] * 5 + [vm, scalars, anywhere],
         out_specs=(vm, vm, scalars, vm, vm, vm),
-        scratch_shapes=local + [pltpu.SemaphoreType.DMA((5,)), pltpu.SemaphoreType.DMA((2,)), pltpu.SemaphoreType.DMA((2,))] + transform_scratch(pairs, slots, half_rows, pair_length, legendre),
+        scratch_shapes=local + [pltpu.SemaphoreType.DMA((5,)), pltpu.SemaphoreType.DMA((4,)), pltpu.SemaphoreType.DMA((4,))] + transform_scratch(pairs, slots, half_rows, pair_length, legendre),
         compiler_params=pltpu.CompilerParams(collective_id=1, has_side_effects=True),
         name="whole",
     )(grid, dep_row, dep_lon, lon_frac, lat_frac, wave_slot, wave_slot, legendre)

time: 40.5 us -> 42.7 us (1.054)
  Pallas kernels: 37.5 us -> 39.7 us
    pallas_call x1, Pallas kernels: 37.5 us -> 39.7 us  [both(): pl.pallas_call(functools.partial(whole_kernel, sizes, half_rows, pair_len...]
where the time goes in v8:
time: 42.7 us; the launch traced here: 42.6 us
  Pallas kernels  39.7 us (93%)
  local copies, waits for them, and re-layouts  1.47 us (3%)
  between operations  1.38 us (3%)
    pallas_call x1, Pallas kernels, both(): pl.pallas_call(functools.partial(whole_kernel, sizes, half_rows, pair_len...  39.7 us
    unnamed x14, local copies, waits for them, and re-layouts  1.47 us

profile of v8, /device:TPU:1, one launch (start us, length us, event | category | flops | bytes accessed | tf_op | source)
XLA Modules:
  0.0 42.6 jit_solution(9459422801162162930)
XLA Ops:
  0.6 0.0 copy-start.5
  0.6 0.0 copy-start.4
  0.7 0.0 copy-start.3
  0.7 0.0 copy-start.2
  0.7 0.0 copy-start.1
  0.7 0.0 copy-start
  0.7 39.7 %whole.1 = (bf16[4,5,4,2596]{3,2,1,0:T(4,128)(2,1)S(1)}, f32[5,16,640]{2,1,0:T(8,128)S(1)}, s32[1]{0:T(128)}, bf16[4,2,4,2596]{3,2,1,0:T(4,128)(2,1)S(1)}, bf16[...) custom-call(bf16[4,5,4,2596]{3,2,1,0:T(4,128)(2,1)} %bitcast.7, s32[5,2596]{1,0:T(8,128)} %row_hbm.1, ...), custom_call_target="tpu_custom_call" | custom-call | tf_op jit(solution)/shard_map/whole/pallas_call | solution.py:377
  41.1 0.0 copy-done.5
  41.1 0.0 copy-done.4
  41.1 0.0 copy-done.3
  41.1 0.0 copy-done.2
  41.1 0.0 copy-done.1
  41.1 0.0 copy-done
  41.2 0.8 %copy.15 = bf16[4,4,5,2596]{3,1,2,0:T(4,128)(2,1)} copy(bf16[4,4,5,2596]{3,1,2,0:T(4,128)(2,1)S(1)} %bitcast.13) | data formatting | bytes 830720
  41.9 0.7 %copy.16 = f32[16,5,640]{2,0,1:T(8,128)} copy(f32[16,5,640]{2,0,1:T(8,128)S(1)} %bitcast.14) | data formatting | bytes 409600
  (1 shorter events, 0.0 us)
Async XLA Ops:
  0.6 40.5 %copy-start.5 = (s32[640]{0:T(1024)S(1)}, s32[640]{0:T(1024)}, u32[]{:S(2)}) copy-start(s32[640]{0:T(1024)} %waves_ref.1) | copy-start | bytes 7684
  0.6 40.5 %copy-start.4 = (f32[5,2596]{1,0:T(8,128)S(1)}, f32[5,2596]{1,0:T(8,128)}, u32[]{:S(2)}) copy-start(f32[5,2596]{1,0:T(8,128)} %latf_hbm.1) | copy-start | bytes 155764
  0.7 40.5 %copy-start.3 = (s32[5,2596]{1,0:T(8,128)S(1)}, s32[5,2596]{1,0:T(8,128)}, u32[]{:S(2)}) copy-start(s32[5,2596]{1,0:T(8,128)} %row_hbm.1) | copy-start | bytes 155764
  0.7 40.5 %copy-start.2 = (f32[4,5,2596]{2,0,1:T(4,128)S(1)}, f32[4,5,2596]{2,0,1:T(4,128)}, u32[]{:S(2)}) copy-start(f32[4,5,2596]{2,0,1:T(4,128)} %param.12) | copy-start | bytes 623044
  0.7 40.5 %copy-start.1 = (s32[4,5,2596]{2,0,1:T(4,128)S(1)}, s32[4,5,2596]{2,0,1:T(4,128)}, u32[]{:S(2)}) copy-start(s32[4,5,2596]{2,0,1:T(4,128)} %param.11) | copy-start | bytes 623044
  0.7 40.5 %copy-start = (bf16[4,4,5,2596]{3,1,2,0:T(4,128)(2,1)S(1)}, bf16[4,4,5,2596]{3,1,2,0:T(4,128)(2,1)}, u32[]{:S(2)}) copy-start(bf16[4,4,5,2596]{3,1,2,0:T(4,128)(2,1)} %param.9) | copy-start | bytes 1246084
